TPU v7x, 32 devices: a whole 2x2x4 slice. The times are simulated.
32 devices in a mesh: dp: 2 (over x), expert: 16 (over z, y, core).
Axes of the slice: x: 2, y: 2, z: 4, core: 2. Of those that a mesh axis runs over, the one named last changes fastest.
Arguments:
- tokens: bfloat16 [4096, 2048], P(('dp', 'expert')), may hold values from -6 to 6
- segments: int32 [4096], P('dp'), may hold values from 0 to 15, never falling along the last dimension, each value on 1 to 2048 neighbouring positions
- routes: int32 [4096, 8], P(('dp', 'expert')), may hold values from 0 to 15, all different within a row; in each aligned block of 128 rows (0 to 127, 128 to 255, ...) at most 96 rows name the same one
- route_gates: float32 [4096, 8], P(('dp', 'expert')), may hold values from 0.0625 to 0.1875
- attn_gain: float32 [2048], replicated, may hold values from 0.5 to 1.5
- query_gain: float32 [2048], replicated, may hold values from 0.5 to 1.5
- key_gain: float32 [2048], replicated, may hold values from 0.5 to 1.5
- ffn_gain: float32 [2048], replicated, may hold values from 0.5 to 1.5
- w_query: bfloat16 [2048, 2048], P('expert'), may hold values from -0.125 to 0.125
- w_key: bfloat16 [2048, 2048], P('expert'), may hold values from -0.125 to 0.125
- w_value: bfloat16 [2048, 2048], P('expert'), may hold values from -0.125 to 0.125
- w_out: bfloat16 [2048, 2048], P('expert'), may hold values from -0.375 to 0.375
- w_gate: bfloat16 [16, 2048, 1024], P('expert'), may hold values from -0.125 to 0.125
- w_up: bfloat16 [16, 2048, 1024], P('expert'), may hold values from -0.125 to 0.125
- w_down: bfloat16 [16, 1024, 2048], P('expert'), may hold values from -0.75 to 0.75
- cotangent: bfloat16 [4096, 2048], P(('dp', 'expert')), may hold values from -6 to 6
Outputs:
- activations: bfloat16 [4096, 2048], P(('dp', 'expert'))
- input_grad: bfloat16 [4096, 2048], P(('dp', 'expert'))
- grad_attn_gain: float32 [2048], replicated
- grad_query_gain: float32 [2048], replicated
- grad_key_gain: float32 [2048], replicated
- grad_ffn_gain: float32 [2048], replicated
- grad_w_query: float32 [2048, 2048], P('expert')
- grad_w_key: float32 [2048, 2048], P('expert')
- grad_w_value: float32 [2048, 2048], P('expert')
- grad_w_out: float32 [2048, 2048], P('expert')
- grad_w_gate: float32 [16, 2048, 1024], P('expert')
- grad_w_up: float32 [16, 2048, 1024], P('expert')
- grad_w_down: float32 [16, 1024, 2048], P('expert')
Inputs may be any that keep to these rules, and one draw needn't show every extreme that they name: `segments`: segment numbers never fall along the tokens; a document holds 1 to 2048 tokens, and one holds exactly 2048. `routes`: each token names 8 different experts. In the rows of one device no expert is named more than 96 times, and in some device's rows one expert is named exactly 96 times.
All inputs are finite; a program needn't handle non-finite values.
Results may differ from a plain program's by a relative error of at most 0.023.
Values may be sent and summed in bfloat16 or wider, within the bound.
No kernel may reach another device: no remote copies, remote signals or barrier semaphores. Data moves between devices by JAX's collectives and lax.ppermute only.
A program may use at most 384 MiB of HBM per device.

v0:
```python
import jax
import jax.numpy as jnp
from jax import lax
from jax.sharding import PartitionSpec as P

HEADS = 16
HEAD_DIM = 128


eps = 1e-05
rope_base = 50000.0
negative = -1e30
block_rows = 512


def norm_rows(values, norm_gain):
    inverse = lax.rsqrt(jnp.mean(values * values, axis=-1, keepdims=True) + eps)
    normal = values * inverse
    return (normal * norm_gain, normal, inverse)


def norm_back(upstream, normal, inverse, norm_gain):
    weighted = upstream * norm_gain
    inner_mean = jnp.mean(weighted * normal, axis=-1, keepdims=True)
    return (inverse * (weighted - normal * inner_mean), jnp.sum(upstream * normal, axis=0))


def rope_tables(positions):
    half_dim = HEAD_DIM // 2
    frequency = rope_base ** (-(jnp.arange(half_dim, dtype=jnp.float32) * 2.0 / HEAD_DIM))
    theta = positions.astype(jnp.float32)[:, None] * frequency[None, :]
    return (jnp.cos(theta)[:, None, :], jnp.sin(theta)[:, None, :])


def rotate(tensor, cosine, rope_sine):
    half_dim = tensor.shape[-1] // 2
    first_half = tensor[..., :half_dim]
    second_half = tensor[..., half_dim:]
    return jnp.concatenate(
        [
            first_half * cosine - second_half * rope_sine,
            second_half * cosine + first_half * rope_sine,
        ],
        axis=-1,
    )


def contract_rows(left, right):
    return lax.dot_general(
        left, right, (((0,), (0,)), ((), ())), preferred_element_type=jnp.float32
    )


def contract_cols(left, right):
    return lax.dot_general(
        left, right, (((1,), (1,)), ((), ())), preferred_element_type=jnp.float32
    )


def over_blocks(block_step, state_now, pieces, first_row):
    piece_rows = pieces[0].shape[0]
    block_count = piece_rows // block_rows
    stacked = tuple(
        (member.reshape((block_count, block_rows) + member.shape[1:]) for member in pieces)
    )

    def inner_step(state_in, packed):
        block_index, block_parts = packed
        return (block_step(state_in, block_parts, first_row + block_index * block_rows), None)

    state_out, _ = lax.scan(
        inner_step, state_now, (jnp.arange(block_count, dtype=jnp.int32), stacked)
    )
    return state_out


def local(
    tokens,
    segments,
    routes,
    route_gates,
    attn_gain,
    query_gain,
    key_gain,
    ffn_gain,
    w_query,
    w_key,
    w_value,
    w_out,
    w_gate,
    w_up,
    w_down,
    cotangent,
):
    row_count, width = tokens.shape
    top_count = routes.shape[1]
    devices = lax.axis_size("expert")
    seq_length = row_count * devices
    first_own = lax.axis_index("expert") * row_count
    own_positions = first_own + jnp.arange(row_count, dtype=jnp.int32)
    own_segs = lax.dynamic_slice_in_dim(segments, first_own, row_count)
    own_seqs = own_positions // seq_length
    score_scale = HEAD_DIM ** (-0.5)

    def piece_labels(first_row, piece_rows):
        positions = first_row + jnp.arange(piece_rows, dtype=jnp.int32)
        return (lax.dynamic_slice_in_dim(segments, first_row, piece_rows), positions // seq_length)

    def live_mask(query_segs, query_seqs, key_segs, key_seqs):
        return (query_segs[:, None] == key_segs[None, :]) & (
            query_seqs[:, None] == key_seqs[None, :]
        )

    query_full, key_full, value_full, out_full = (
        lax.all_gather(w_query, "expert", axis=0, tiled=True),
        lax.all_gather(w_key, "expert", axis=0, tiled=True),
        lax.all_gather(w_value, "expert", axis=0, tiled=True),
        lax.all_gather(w_out, "expert", axis=0, tiled=True),
    )
    resid_in = tokens.astype(jnp.float32)
    pre_in, normal_in, inverse_in = norm_rows(resid_in, attn_gain)
    normed_in = pre_in.astype(jnp.bfloat16)
    query_raw = jnp.dot(normed_in, query_full, preferred_element_type=jnp.float32)
    key_raw = jnp.dot(normed_in, key_full, preferred_element_type=jnp.float32)
    value_rows = (
        jnp.dot(normed_in, value_full, preferred_element_type=jnp.float32)
        .astype(jnp.bfloat16)
        .reshape(row_count, HEADS, HEAD_DIM)
    )
    query_pre, normal_query, inverse_query = norm_rows(query_raw, query_gain)
    key_pre, normal_key, inverse_key = norm_rows(key_raw, key_gain)
    cosine, rope_sine = rope_tables(own_positions % seq_length)
    query_rot = rotate(query_pre.reshape(row_count, HEADS, HEAD_DIM), cosine, rope_sine).astype(
        jnp.bfloat16
    )
    key_rot = rotate(key_pre.reshape(row_count, HEADS, HEAD_DIM), cosine, rope_sine).astype(
        jnp.bfloat16
    )

    def forward_step(state_now, pieces, first_row):
        key_piece, value_piece = pieces
        key_segs, key_seqs = piece_labels(first_row, key_piece.shape[0])
        is_live = live_mask(own_segs, own_seqs, key_segs, key_seqs)[None]
        run_peak, run_total, run_acc = state_now
        scores = (
            jnp.einsum("qhd,khd->hqk", query_rot, key_piece, preferred_element_type=jnp.float32)
            * score_scale
        )
        scores = jnp.where(is_live, scores, negative)
        new_peak = jnp.maximum(run_peak, jnp.max(scores, axis=-1))
        attn_probs = jnp.where(is_live, jnp.exp(scores - new_peak[:, :, None]), 0.0)
        factor = jnp.exp(run_peak - new_peak)
        run_total = run_total * factor + jnp.sum(attn_probs, axis=-1)
        update = jnp.einsum(
            "hqk,khd->qhd",
            attn_probs.astype(jnp.bfloat16),
            value_piece,
            preferred_element_type=jnp.float32,
        )
        run_acc = run_acc * factor.T[:, :, None] + update
        return (new_peak, run_total, run_acc)

    start_state = (
        jnp.full((HEADS, row_count), negative, jnp.float32),
        jnp.zeros((HEADS, row_count), jnp.float32),
        jnp.zeros((row_count, HEADS, HEAD_DIM), jnp.float32),
    )
    final_state = over_blocks(
        forward_step,
        start_state,
        (
            lax.all_gather(key_rot, "expert", axis=0, tiled=True),
            lax.all_gather(value_rows, "expert", axis=0, tiled=True),
        ),
        jnp.int32(0),
    )
    run_peak, run_total, run_acc = final_state
    log_total = run_peak + jnp.log(run_total)
    attended = run_acc / run_total.T[:, :, None]
    attended_low = attended.reshape(row_count, width).astype(jnp.bfloat16)
    middle = resid_in + jnp.dot(attended_low, out_full, preferred_element_type=jnp.float32)
    pre_mid, normal_mid, inverse_mid = norm_rows(middle, ffn_gain)
    normed_mid = pre_mid.astype(jnp.bfloat16)
    experts_all = devices * w_gate.shape[0]
    slots = min(row_count, row_count * top_count * 3 // (2 * experts_all))
    flat_route = routes.reshape(-1)
    route_hits = (flat_route[:, None] == jnp.arange(experts_all, dtype=jnp.int32)[None, :]).astype(
        jnp.int32
    )
    slot_rank = jnp.sum((jnp.cumsum(route_hits, axis=0) - route_hits) * route_hits, axis=1)
    slot_index = flat_route * slots + slot_rank
    pair_token = jnp.arange(row_count * top_count, dtype=jnp.int32) // top_count
    owner_row = (
        jnp.full((experts_all * slots,), row_count, jnp.int32).at[slot_index].set(pair_token)
    )
    padded_mid = jnp.concatenate([normed_mid, jnp.zeros((1, width), jnp.bfloat16)], axis=0)
    send_rows = padded_mid[owner_row].reshape(experts_all, slots, width)
    received = lax.all_to_all(send_rows, "expert", split_axis=0, concat_axis=0, tiled=True).reshape(
        experts_all * slots, width
    )
    gate_fwd = jnp.dot(received, w_gate[0], preferred_element_type=jnp.float32)
    up_fwd = jnp.dot(received, w_up[0], preferred_element_type=jnp.float32)
    hidden_fwd = (gate_fwd * jax.nn.sigmoid(gate_fwd) * up_fwd).astype(jnp.bfloat16)
    expert_out = jnp.dot(hidden_fwd, w_down[0], preferred_element_type=jnp.float32).astype(
        jnp.bfloat16
    )
    returned = lax.all_to_all(
        expert_out.reshape(experts_all, slots, width),
        "expert",
        split_axis=0,
        concat_axis=0,
        tiled=True,
    ).reshape(experts_all * slots, width)
    picked = returned[slot_index].reshape(row_count, top_count, width)
    mixed = jnp.sum(picked.astype(jnp.float32) * route_gates[:, :, None], axis=1)
    activations = (middle + mixed).astype(jnp.bfloat16)
    grad_out = cotangent.astype(jnp.float32)
    slot_grad = (
        (grad_out[:, None, :] * route_gates[:, :, None])
        .astype(jnp.bfloat16)
        .reshape(row_count * top_count, width)
    )
    grad_send = (
        jnp.zeros((experts_all * slots, width), jnp.bfloat16)
        .at[slot_index]
        .set(slot_grad)
        .reshape(experts_all, slots, width)
    )
    rows_back, grad_back = (
        lax.all_to_all(send_rows, "expert", split_axis=0, concat_axis=0, tiled=True),
        lax.all_to_all(grad_send, "expert", split_axis=0, concat_axis=0, tiled=True),
    )
    rows_in = rows_back.reshape(experts_all * slots, width)
    grad_recv = grad_back.reshape(experts_all * slots, width)
    gate_in = jnp.dot(rows_in, w_gate[0], preferred_element_type=jnp.float32)
    up_in = jnp.dot(rows_in, w_up[0], preferred_element_type=jnp.float32)
    sigmoid_in = jax.nn.sigmoid(gate_in)
    silu_in = gate_in * sigmoid_in
    hidden_in = (silu_in * up_in).astype(jnp.bfloat16)
    grad_hidden = contract_cols(grad_recv, w_down[0])
    grad_up_pre = (grad_hidden * silu_in).astype(jnp.bfloat16)
    grad_gate_pre = (
        grad_hidden * up_in * sigmoid_in * (1.0 + gate_in * (1.0 - sigmoid_in))
    ).astype(jnp.bfloat16)
    local_down = contract_rows(hidden_in, grad_recv)
    local_gate = contract_rows(rows_in, grad_gate_pre)
    local_up = contract_rows(rows_in, grad_up_pre)
    grad_rows = (
        contract_cols(grad_gate_pre, w_gate[0]) + contract_cols(grad_up_pre, w_up[0])
    ).astype(jnp.bfloat16)
    back_rows = lax.all_to_all(
        grad_rows.reshape(experts_all, slots, width),
        "expert",
        split_axis=0,
        concat_axis=0,
        tiled=True,
    ).reshape(experts_all * slots, width)
    grad_normed_mid = jnp.sum(
        back_rows[slot_index].reshape(row_count, top_count, width).astype(jnp.float32), axis=1
    )
    mid_back, grad_ffn_gain = norm_back(grad_normed_mid, normal_mid, inverse_mid, ffn_gain)
    grad_middle = grad_out + mid_back
    grad_branch = grad_middle.astype(jnp.bfloat16)
    grad_attended = (
        contract_cols(grad_branch, out_full)
        .astype(jnp.bfloat16)
        .reshape(row_count, HEADS, HEAD_DIM)
    )
    delta = jnp.sum(grad_attended.astype(jnp.float32) * attended, axis=-1).T

    def query_step(state_now, pieces, first_row):
        key_piece, value_piece = pieces
        key_segs, key_seqs = piece_labels(first_row, key_piece.shape[0])
        is_live = live_mask(own_segs, own_seqs, key_segs, key_seqs)[None]
        scores = (
            jnp.einsum("qhd,khd->hqk", query_rot, key_piece, preferred_element_type=jnp.float32)
            * score_scale
        )
        attn_probs = jnp.where(is_live, jnp.exp(scores - log_total[:, :, None]), 0.0)
        grad_probs = jnp.einsum(
            "qhd,khd->hqk", grad_attended, value_piece, preferred_element_type=jnp.float32
        )
        grad_scores = (attn_probs * (grad_probs - delta[:, :, None])).astype(jnp.bfloat16)
        return state_now + jnp.einsum(
            "hqk,khd->qhd", grad_scores, key_piece, preferred_element_type=jnp.float32
        )

    zero_heads = jnp.zeros((row_count, HEADS, HEAD_DIM), jnp.float32)
    key_all, value_all = (
        lax.all_gather(key_rot, "expert", axis=0, tiled=True),
        lax.all_gather(value_rows, "expert", axis=0, tiled=True),
    )
    grad_query_rot = over_blocks(query_step, zero_heads, (key_all, value_all), 0) * score_scale
    stat_total, stat_delta = (
        lax.all_gather(log_total.T, "expert", axis=0, tiled=True),
        lax.all_gather(delta.T, "expert", axis=0, tiled=True),
    )

    def key_step(state_now, pieces, first_row):
        query_piece, grad_piece = pieces
        piece_rows = query_piece.shape[0]
        query_segs, query_seqs = piece_labels(first_row, piece_rows)
        is_live = live_mask(query_segs, query_seqs, own_segs, own_seqs)[None]
        piece_total = lax.dynamic_slice_in_dim(stat_total, first_row, piece_rows).T
        piece_delta = lax.dynamic_slice_in_dim(stat_delta, first_row, piece_rows).T
        scores = (
            jnp.einsum("qhd,khd->hqk", query_piece, key_rot, preferred_element_type=jnp.float32)
            * score_scale
        )
        attn_probs = jnp.where(is_live, jnp.exp(scores - piece_total[:, :, None]), 0.0)
        value_acc, key_acc = state_now
        value_acc = value_acc + jnp.einsum(
            "hqk,qhd->khd",
            attn_probs.astype(jnp.bfloat16),
            grad_piece,
            preferred_element_type=jnp.float32,
        )
        grad_probs = jnp.einsum(
            "qhd,khd->hqk", grad_piece, value_rows, preferred_element_type=jnp.float32
        )
        grad_scores = (attn_probs * (grad_probs - piece_delta[:, :, None])).astype(jnp.bfloat16)
        key_acc = key_acc + jnp.einsum(
            "hqk,qhd->khd", grad_scores, query_piece, preferred_element_type=jnp.float32
        )
        return (value_acc, key_acc)

    grad_value_acc, grad_key_acc = over_blocks(
        key_step,
        (zero_heads, zero_heads),
        (
            lax.all_gather(query_rot, "expert", axis=0, tiled=True),
            lax.all_gather(grad_attended, "expert", axis=0, tiled=True),
        ),
        jnp.int32(0),
    )
    grad_key_rot = grad_key_acc * score_scale
    grad_value = grad_value_acc.reshape(row_count, width).astype(jnp.bfloat16)
    grad_query_pre = rotate(grad_query_rot, cosine, -rope_sine).reshape(row_count, width)
    grad_key_pre = rotate(grad_key_rot, cosine, -rope_sine).reshape(row_count, width)
    grad_query_raw, grad_query_gain = norm_back(
        grad_query_pre, normal_query, inverse_query, query_gain
    )
    grad_key_raw, grad_key_gain = norm_back(grad_key_pre, normal_key, inverse_key, key_gain)
    grad_query = grad_query_raw.astype(jnp.bfloat16)
    grad_key = grad_key_raw.astype(jnp.bfloat16)
    grad_normed_in = (
        contract_cols(grad_query, query_full)
        + contract_cols(grad_key, key_full)
        + contract_cols(grad_value, value_full)
    )
    in_back, grad_attn_gain = norm_back(grad_normed_in, normal_in, inverse_in, attn_gain)
    input_grad = (grad_middle + in_back).astype(jnp.bfloat16)
    dense_rows = lax.psum_scatter(
        jnp.concatenate(
            [
                contract_rows(normed_in, grad_query),
                contract_rows(normed_in, grad_key),
                contract_rows(normed_in, grad_value),
                contract_rows(attended_low, grad_branch),
            ],
            axis=1,
        ).astype(jnp.bfloat16),
        "expert",
        scatter_dimension=0,
        tiled=True,
    )
    dense_total, gate_total, up_total, down_total = (
        lax.psum(dense_rows, "dp").astype(jnp.float32),
        lax.psum(local_gate[None].astype(jnp.bfloat16), "dp").astype(jnp.float32),
        lax.psum(local_up[None].astype(jnp.bfloat16), "dp").astype(jnp.float32),
        lax.psum(local_down[None].astype(jnp.bfloat16), "dp").astype(jnp.float32),
    )
    gain_total = lax.psum(
        jnp.stack([grad_attn_gain, grad_query_gain, grad_key_gain, grad_ffn_gain]), ("dp", "expert")
    )
    return (
        activations,
        input_grad,
        gain_total[0],
        gain_total[1],
        gain_total[2],
        gain_total[3],
        dense_total[:, :width],
        dense_total[:, width : 2 * width],
        dense_total[:, 2 * width : 3 * width],
        dense_total[:, 3 * width :],
        gate_total,
        up_total,
        down_total,
    )


def solution(mesh):
    in_specs = (
        P(("dp", "expert"), None),
        P("dp"),
        P(("dp", "expert"), None),
        P(("dp", "expert"), None),
        P(),
        P(),
        P(),
        P(),
        P("expert", None),
        P("expert", None),
        P("expert", None),
        P("expert", None),
        P("expert", None, None),
        P("expert", None, None),
        P("expert", None, None),
        P(("dp", "expert"), None),
    )
    out_specs = (
        P(("dp", "expert"), None),
        P(("dp", "expert"), None),
        P(),
        P(),
        P(),
        P(),
        P("expert", None),
        P("expert", None),
        P("expert", None),
        P("expert", None),
        P("expert", None, None),
        P("expert", None, None),
        P("expert", None, None),
    )
    return jax.shard_map(local, mesh=mesh, in_specs=in_specs, out_specs=out_specs, check_vma=False)
```

profile of v0, /device:TPU:0, one launch (start us, length us, event | category | flops | bytes accessed | tf_op | source)
XLA Modules:
  0.0 2219.4 jit_solution(8471534130006966108)
XLA Ops:
  11.5 76.3 %all-gather.13.cloned.1.call-done = bf16[2048,2048]{1,0:T(8,128)(2,1)} async-done(((bf16[128,2048]{1,0:T(8,128)(2,1)}), bf16[2048,2048]{1,0:T(8,128)(2,1)}) %all-gather.13.cloned.1.call-update) | async-done | bytes 8388624 | tf_op jit(solution)/shard_map/all_gather | solution.py:115
  94.3 68.9 %all-gather.9.cloned.1.call-done = bf16[2048,2048]{1,0:T(8,128)(2,1)} async-done(((bf16[128,2048]{1,0:T(8,128)(2,1)}), bf16[2048,2048]{1,0:T(8,128)(2,1)}) %all-gather.9.cloned.1.call-update) | async-done | bytes 8388624 | tf_op jit(solution)/shard_map/all_gather | solution.py:116
  172.9 65.6 %all-gather.15.cloned.1.call-done = bf16[2048,2048]{1,0:T(8,128)(2,1)} async-done(((bf16[128,2048]{1,0:T(8,128)(2,1)}), bf16[2048,2048]{1,0:T(8,128)(2,1)}) %all-gather.15.cloned.1.call-update) | async-done | bytes 8388624 | tf_op jit(solution)/shard_map/all_gather | solution.py:117
  256.7 60.7 %all-gather.11.cloned.1.call-done = bf16[2048,16,128]{0,2,1:T(8,128)(2,1)} async-done(((bf16[128,16,128]{0,2,1:T(8,128)(2,1)}), bf16[2048,16,128]{0,2,1:T(8,128)(2,1)}) %all-gather.11.cloned.1.call-update) | async-done | bytes 8388624 | tf_op jit(solution)/shard_map/all_gather | solution.py:172
  346.5 46.6 %all-gather.17.cloned.1.call-done = bf16[2048,16,128]{2,1,0:T(8,128)(2,1)} async-done(((bf16[128,16,128]{2,1,0:T(8,128)(2,1)}), bf16[2048,16,128]{2,1,0:T(8,128)(2,1)}) %all-gather.17.cloned.1.call-update) | async-done | bytes 8388624 | tf_op jit(solution)/shard_map/all_gather | solution.py:173
  393.1 80.0 %while.45 = (s32[]{:T(128)}, f32[16,128]{1,0:T(8,128)S(1)}, f32[16,128]{1,0:T(8,128)S(1)}, f32[128,16,128]{0,2,1:T(8,128)}, s32[128]{0:T(128)S(1)}, /*index=5*/s...) while((s32[]{:T(128)}, f32[16,128]{1,0:T(8,128)S(1)}, ...), condition=%wide.region_6.7_spmd.clone, body=%wide.region_3.6_spmd.clone.sunk | while | flops 551507968 | bytes 28192492 | solution.py:71
  504.6 103.2 %all-to-all-done = bf16[16,96,2048]{2,1,0:T(8,128)(2,1)} async-done(((bf16[16,96,2048]{2,1,0:T(8,128)(2,1)}), bf16[16,96,2048]{2,1,0:T(8,128)(2,1)}, u32[]{:S(2)}, u32[]{:S(2)}) %all-to-all-start) | async-done | bytes 6291488 | tf_op jit(solution)/shard_map/all_to_all | solution.py:198
  607.8 28.6 %all-to-all-start.2 = ((bf16[16,96,2048]{2,1,0:T(8,128)(2,1)}), bf16[16,96,2048]{2,1,0:T(8,128)(2,1)}, u32[]{:S(2)}, u32[]{:S(2)}) async-start(bf16[16,96,2048]{2,1,0:T(8,128)(2,1)} %bitcast.295), calls=%async_computation.2 | async-start | bytes 12582912 | tf_op jit(solution)/shard_map/all_to_all | solution.py:231
  658.5 92.0 %all-to-all-done.2 = bf16[16,96,2048]{2,1,0:T(8,128)(2,1)} async-done(((bf16[16,96,2048]{2,1,0:T(8,128)(2,1)}), bf16[16,96,2048]{2,1,0:T(8,128)(2,1)}, u32[]{:S(2)}, u32[]{:S(2)}) %all-to-all-start.2) | async-done | bytes 6291488 | tf_op jit(solution)/shard_map/all_to_all | solution.py:231
  750.5 17.7 multiply_convert_fusion.1
  790.3 28.1 %all-to-all-start.3 = ((bf16[16,96,2048]{2,1,0:T(8,128)(2,1)}), bf16[16,96,2048]{2,1,0:T(8,128)(2,1)}, u32[]{:S(2)}, u32[]{:S(2)}) async-start(bf16[16,96,2048]{2,1,0:T(8,128)(2,1)} %bitcast.302), calls=%async_computation.3 | async-start | bytes 12582912 | tf_op jit(solution)/shard_map/all_to_all | solution.py:251
  830.3 148.4 %all-to-all-done.3 = bf16[16,96,2048]{2,1,0:T(8,128)(2,1)} async-done(((bf16[16,96,2048]{2,1,0:T(8,128)(2,1)}), bf16[16,96,2048]{2,1,0:T(8,128)(2,1)}, u32[]{:S(2)}, u32[]{:S(2)}) %all-to-all-start.3) | async-done | bytes 6291488 | tf_op jit(solution)/shard_map/all_to_all | solution.py:251
  978.7 32.6 %all-to-all-start.1 = ((bf16[16,96,2048]{2,1,0:T(8,128)(2,1)}), bf16[16,96,2048]{2,1,0:T(8,128)(2,1)}, u32[]{:S(2)}, u32[]{:S(2)}) async-start(bf16[16,96,2048]{2,1,0:T(8,128)(2,1)} %bitcast.303), calls=%async_computation.1 | async-start | bytes 12582912 | tf_op jit(solution)/shard_map/all_to_all | solution.py:207
  1023.9 101.5 %all-to-all-done.1 = bf16[16,96,2048]{2,1,0:T(8,128)(2,1)} async-done(((bf16[16,96,2048]{2,1,0:T(8,128)(2,1)}), bf16[16,96,2048]{2,1,0:T(8,128)(2,1)}, u32[]{:S(2)}, u32[]{:S(2)}) %all-to-all-start.1) | async-done | bytes 6291488 | tf_op jit(solution)/shard_map/all_to_all | solution.py:207
  1172.0 14.6 copy.110
  1187.3 45.1 %all_gather.40 = f32[2048,16]{0,1:T(8,128)S(1)} all-gather(f32[128,16]{0,1:T(8,128)S(1)} %bitcast.320), channel_id=1, replica_groups=mesh['dp'=2,'expert'=16] {'expert'}, dimensions={0}, use_global_device_ids=true | all-gather | bytes 139264 | tf_op jit(solution)/shard_map/all_gather | solution.py:295
  1233.1 25.4 %all_gather.41 = f32[2048,16]{1,0:T(8,128)S(1)} all-gather(f32[128,16]{1,0:T(8,128)S(1)} %multiply_reduce_fusion.5), channel_id=1, replica_groups=mesh['dp'=2,'expert'=16] {'expert'}, dimensions={0}, use_global_device_ids=true | all-gather | bytes 139264 | tf_op jit(solution)/shard_map/all_gather | solution.py:296
  1260.4 57.6 %while.46 = (s32[]{:T(128)}, f32[128,16,128]{0,2,1:T(8,128)}, bf16[4,512,16,128]{3,1,2,0:T(8,128)(2,1)}, s32[128]{0:T(128)S(1)}, s32[4]{0:T(128)S(1)}, /*index=5...) while((s32[]{:T(128)}, f32[128,16,128]{0,2,1:T(8,128)}, ...), condition=%wide.region_18.19_spmd.clone, body=%wide.region_17.18_spmd.clone.sunk | while | flops 812328960 | bytes 22245168 | solution.py:71
  1327.4 92.9 %while.47 = (s32[]{:T(128)}, f32[128,16,128]{0,2,1:T(8,128)}, f32[128,16,128]{0,2,1:T(8,128)}, bf16[4,512,16,128]{3,2,1,0:T(8,128)(2,1)}, s32[4]{0:T(128)S(1)}, ...) while((s32[]{:T(128)}, f32[128,16,128]{0,2,1:T(8,128)}, ...), condition=%wide.region_21.22_spmd.clone, body=%wide.region_20.21_spmd.clone.sunk | while | flops 1085483008 | bytes 43429664 | solution.py:71
  1451.5 23.8 %pad_maximum_fusion = bf16[2048,8192]{0,1:T(8,128)(2,1)} fusion(bf16[2048,2048]{0,1:T(8,128)(2,1)} %convolution_convert_fusion.2, bf16[2048,2048]{0,1:T(8,128)(2,1)} %convolution_convert_fusion.1, bf16[2048,2048]{0,1:T(8,128)(2,1)} %convolution_convert_fusion.3, bf16[2048,2048]{0,1:T(8,128)(2,1)} %convolution_convert_fusion.4), kind=kLoop, calls=%fused_computation.124 | loop fusion | flops 134217728 | bytes 67108864 | tf_op jit(solution)/shard_map/concatenate | solution.py:354
  1475.3 39.9 %copy.126 = bf16[2048,8192]{1,0:T(8,128)(2,1)} copy(bf16[2048,8192]{0,1:T(8,128)(2,1)} %pad_maximum_fusion) | data formatting | bytes 67108864
  1551.5 295.5 %reduce-scatter.4.cloned.1.call-done = bf16[128,8192]{1,0:T(8,128)(2,1)} async-done(((bf16[2048,8192]{1,0:T(8,128)(2,1)}), bf16[128,8192]{1,0:T(8,128)(2,1)}) %reduce-scatter.4.cloned.1.call-update) | async-done | bytes 2097168
  1867.4 40.0 %psum.35 = f32[4,2048]{1,0:T(4,128)S(1)} all-reduce(f32[4,2048]{1,0:T(4,128)S(1)} %pad_maximum_fusion.5), channel_id=1, replica_groups=mesh['dp'=2,'expert'=16] {'dp','expert'}, use_global_device_ids=true, to_apply=%region_28.29 | all-reduce | flops 8192 | bytes 65536 | tf_op jit(solution)/shard_map/psum | solution.py:373
  1909.2 278.0 %all-reduce.4.cloned.1.call-done = (bf16[128,8192]{0,1:T(8,128)(2,1)}, bf16[1,2048,1024]{2,1,0:T(8,128)(2,1)}, bf16[1,2048,1024]{2,1,0:T(8,128)(2,1)}, bf16[1,1024,2048]{2,1,0:T(8,128)(2,1)}) async-done(((bf16[128,8192]{0,1:T(8,128)(2,1)}, bf16[1,2048,1024]{2,1,0:T(8,128)(2,1)}, bf16[1,2048,1024]{2,1,0:T(8,128)(2,1)}, bf16[1,1024,2048]{2,1,0:T(8,128)(2,1)}), (bf16[128,8192]{0,1:T(8,128)(2,1)}, ...) | async-done | bytes 14680080 | tf_op jit(solution)/shard_map/psum | solution.py:368
  (419 shorter events, 562.6 us)
Async XLA Ops:
  7.2 80.6 %all-gather.13.cloned.1.call-start = ((), (), s32[]{:S(2)}) async-start(), calls=%async_computation.7 | async-start | bytes 8912896 | tf_op jit(solution)/shard_map/all_gather | solution.py:115
  7.9 155.2 %all-gather.9.cloned.1.call-start = ((), (), s32[]{:S(2)}) async-start(), calls=%async_computation.5 | async-start | bytes 8912896 | tf_op jit(solution)/shard_map/all_gather | solution.py:116
  8.7 229.8 %all-gather.15.cloned.1.call-start = ((), (), s32[]{:S(2)}) async-start(), calls=%async_computation.8 | async-start | bytes 8912896 | tf_op jit(solution)/shard_map/all_gather | solution.py:117
  9.4 308.1 %all-gather.11.cloned.1.call-start = ((), (), s32[]{:S(2)}) async-start(), calls=%async_computation.6 | async-start | bytes 8912896 | tf_op jit(solution)/shard_map/all_gather | solution.py:172
  10.7 227.8 %copy-start.38 = (f32[128]{0:T(128)}, f32[128]{0:T(128)S(1)}, u32[]{:S(2)}) copy-start(f32[128]{0:T(128)S(1)} %add_rsqrt_fusion.3) | copy-start | bytes 1540
  11.5 160.2 %copy-start.32 = (f32[128,64]{0,1:T(8,128)}, f32[128,64]{0,1:T(8,128)S(1)}, u32[]{:S(2)}) copy-start(f32[128,64]{0,1:T(8,128)S(1)} %get-tuple-element.862) | copy-start | bytes 98308
  11.5 82.2 %copy-start.41 = (f32[2048]{0:T(1024)S(1)}, f32[2048]{0:T(1024)}, u32[]{:S(2)}) copy-start(f32[2048]{0:T(1024)} %param.27) | copy-start | bytes 24580
  92.8 75.1 %copy-start.52 = (f32[128]{0:T(128)}, f32[128]{0:T(128)S(1)}, u32[]{:S(2)}) copy-start(f32[128]{0:T(128)S(1)} %add_rsqrt_fusion.1) | copy-start | bytes 1540
  94.2 74.7 %copy-start.43 = (f32[2048]{0:T(1024)S(1)}, f32[2048]{0:T(1024)}, u32[]{:S(2)}) copy-start(f32[2048]{0:T(1024)} %param.28) | copy-start | bytes 24580
  172.9 220.3 %all-gather.17.cloned.1.call-start = ((), (), s32[]{:S(2)}) async-start(), calls=%async_computation.9 | async-start | bytes 8912896 | tf_op jit(solution)/shard_map/all_gather | solution.py:173
  244.9 231.4 %all-gather.19.cloned.1.call-start = ((), (), s32[]{:S(2)}) async-start(), calls=%async_computation.10 | async-start | bytes 8912896 | tf_op jit(solution)/shard_map/all_gather | solution.py:118
  256.4 75.6 %copy-start.16 = (bf16[128,16,128]{0,2,1:T(8,128)(2,1)}, bf16[128,16,128]{0,2,1:T(8,128)(2,1)S(1)}, u32[]{:S(2)}) copy-start(bf16[128,16,128]{0,2,1:T(8,128)(2,1)S(1)} %pad_maximum_fusion.4) | copy-start | bytes 1572868
  488.6 119.2 %all-to-all-start = ((bf16[16,96,2048]{2,1,0:T(8,128)(2,1)}), bf16[16,96,2048]{2,1,0:T(8,128)(2,1)}, u32[]{:S(2)}, u32[]{:S(2)}) async-start(bf16[16,96,2048]{2,1,0:T(8,128)(2,1)} %bitcast.296), calls=%async_computation | async-start | bytes 12582912 | tf_op jit(solution)/shard_map/all_to_all | solution.py:198
  607.8 142.7 %all-to-all-start.2 = ((bf16[16,96,2048]{2,1,0:T(8,128)(2,1)}), bf16[16,96,2048]{2,1,0:T(8,128)(2,1)}, u32[]{:S(2)}, u32[]{:S(2)}) async-start(bf16[16,96,2048]{2,1,0:T(8,128)(2,1)} %bitcast.295), calls=%async_computation.2 | async-start | bytes 12582912 | tf_op jit(solution)/shard_map/all_to_all | solution.py:231
  790.3 188.4 %all-to-all-start.3 = ((bf16[16,96,2048]{2,1,0:T(8,128)(2,1)}), bf16[16,96,2048]{2,1,0:T(8,128)(2,1)}, u32[]{:S(2)}, u32[]{:S(2)}) async-start(bf16[16,96,2048]{2,1,0:T(8,128)(2,1)} %bitcast.302), calls=%async_computation.3 | async-start | bytes 12582912 | tf_op jit(solution)/shard_map/all_to_all | solution.py:251
  818.4 339.1 %all-gather.23.cloned.1.call-start = ((), (), s32[]{:S(2)}) async-start(), calls=%async_computation.12 | async-start | bytes 8912896 | tf_op jit(solution)/shard_map/all_gather | solution.py:331
  978.7 146.8 %all-to-all-start.1 = ((bf16[16,96,2048]{2,1,0:T(8,128)(2,1)}), bf16[16,96,2048]{2,1,0:T(8,128)(2,1)}, u32[]{:S(2)}, u32[]{:S(2)}) async-start(bf16[16,96,2048]{2,1,0:T(8,128)(2,1)} %bitcast.303), calls=%async_computation.1 | async-start | bytes 12582912 | tf_op jit(solution)/shard_map/all_to_all | solution.py:207
  1011.2 316.2 %all-gather.21.cloned.1.call-start = ((), (), s32[]{:S(2)}) async-start(), calls=%async_computation.11 | async-start | bytes 8912896 | tf_op jit(solution)/shard_map/all_gather | solution.py:332
  1156.2 690.9 %reduce-scatter.4.cloned.1.call-start = ((), (), s32[]{:S(2)}) async-start(), calls=%async_computation.13 | async-start | bytes 35651584
  1186.6 73.7 %copy-start.36 = (s32[128]{0:T(128)S(1)}, s32[128]{0:T(128)}, u32[]{:S(2)}) copy-start(s32[128]{0:T(128)} %copy-done.35) | copy-start | bytes 1540
  1186.6 73.7 %copy-start.37 = (s32[2048]{0:T(1024)S(1)}, s32[2048]{0:T(1024)}, u32[]{:S(2)}) copy-start(s32[2048]{0:T(1024)} %get-tuple-element.1314) | copy-start | bytes 24580
  1327.4 94.2 %copy-start.33 = (f32[128,64]{0,1:T(8,128)S(1)}, f32[128,64]{0,1:T(8,128)}, u32[]{:S(2)}) copy-start(f32[128,64]{0,1:T(8,128)} %copy-done.32) | copy-start | bytes 98308
  1327.4 94.2 %copy-start.34 = (f32[128,64]{0,1:T(8,128)S(1)}, f32[128,64]{0,1:T(8,128)}, u32[]{:S(2)}) copy-start(f32[128,64]{0,1:T(8,128)} %get-tuple-element.860) | copy-start | bytes 98308
  1515.2 672.0 %all-reduce.4.cloned.1.call-start = ((), (), s32[]{:S(2)}) async-start(), calls=%async_computation.14 | async-start | bytes 29360128 | tf_op jit(solution)/shard_map/psum | solution.py:368
  (62 other events, 873.7 us)
Sparse Core Ops, SparseCore 0:
  10.2 77.5 all-gather.12
  90.0 73.1 all-gather.8
  165.3 73.1 all-gather.14
  241.1 76.3 all-gather.10
  320.0 73.0 all-gather.16
  395.1 73.1 all-gather.18
  821.4 175.8 all-gather.22
  1156.3 104.9 all-gather.20
  1515.4 331.6 reduce-scatter.3
  1851.5 335.6 all-reduce.3
where the time goes:
time: 2230 us; the launch traced here: 2220 us
  waiting for transfers between devices  1340 us (60%)
  matrix products  325 us (15%)
  local copies, waits for them, and re-layouts  223 us (10%)
  blocking collectives  110 us (5%)
  other arithmetic  101 us (5%)
  starting transfers between devices  94.7 us (4%)
    unnamed x11, waiting for transfers between devices  299 us
    psum x1, waiting for transfers between devices, local(): lax.psum(dense_rows, 'dp').astype(jnp.float32)  278 us
    all_to_all x1, waiting for transfers between devices, local(): lax.all_to_all(grad_rows.reshape(experts_all, slots, width), 'expert', sp...  148 us
    all_to_all x1, waiting for transfers between devices, local(): lax.all_to_all(send_rows, 'expert', split_axis=0, concat_axis=0, tiled=True)  103 us
    all_to_all x1, waiting for transfers between devices, local(): lax.all_to_all(expert_out.reshape(experts_all, slots, width), 'expert', s...  102 us
    all_to_all x1, waiting for transfers between devices, local(): lax.all_to_all(grad_send, 'expert', split_axis=0, concat_axis=0, tiled=True)  92 us
    unnamed x138, local copies, waits for them, and re-layouts  89.3 us
    all_gather x1, waiting for transfers between devices, local(): lax.all_gather(w_query, 'expert', axis=0, tiled=True)  76.3 us
  transfers between devices with their start and end apart: 14, of which 11 were waited for; matrix products, arithmetic and copies ran while one was open for 17% of the time, Pallas kernels for 0%

commit v1 on v0

v1 whole, which is shorter than its diff:
```python
import functools

import jax
import jax.numpy as jnp
from jax import lax
from jax.experimental import pallas as pl
from jax.experimental.pallas import tpu as pltpu
from jax.sharding import PartitionSpec as P

HEADS = 16
HEAD_DIM = 128


eps = 1e-05
rope_base = 50000.0
negative = -1e30
score_scale = HEAD_DIM ** (-0.5)
query_block = 256


def norm_rows(values, norm_gain):
    inverse = lax.rsqrt(jnp.mean(values * values, axis=-1, keepdims=True) + eps)
    normal = values * inverse
    return (normal * norm_gain, normal, inverse)


def norm_back(upstream, normal, inverse, norm_gain):
    weighted = upstream * norm_gain
    inner_mean = jnp.mean(weighted * normal, axis=-1, keepdims=True)
    return (inverse * (weighted - normal * inner_mean), jnp.sum(upstream * normal, axis=0))


def rope_tables(positions):
    half_dim = HEAD_DIM // 2
    frequency = rope_base ** (-(jnp.arange(half_dim, dtype=jnp.float32) * 2.0 / HEAD_DIM))
    theta = positions.astype(jnp.float32)[:, None] * frequency[None, :]
    return (jnp.cos(theta), jnp.sin(theta))


def rotate(tensor, cosine, rope_sine):
    half_dim = tensor.shape[-1] // 2
    first_half = tensor[..., :half_dim]
    second_half = tensor[..., half_dim:]
    return jnp.concatenate(
        [
            first_half * cosine - second_half * rope_sine,
            second_half * cosine + first_half * rope_sine,
        ],
        axis=-1,
    )


def mm(left, right):
    return jnp.dot(left, right, preferred_element_type=jnp.float32)


def contract_rows(left, right):
    return lax.dot_general(
        left, right, (((0,), (0,)), ((), ())), preferred_element_type=jnp.float32
    )


def contract_cols(left, right):
    return lax.dot_general(
        left, right, (((1,), (1,)), ((), ())), preferred_element_type=jnp.float32
    )


def swap(values, axis, step):
    count = lax.axis_size(axis)
    return lax.ppermute(values, axis, [(i, i ^ step) for i in range(count)])


def butterfly(values, axis):
    step = 1
    while step < lax.axis_size(axis):
        values = values + swap(values, axis, step)
        step *= 2
    return values


def dp_total(values):
    step = 1
    total = values.astype(jnp.float32)
    while step < lax.axis_size("dp"):
        held = total.astype(jnp.bfloat16)
        total = held.astype(jnp.float32) + swap(held, "dp", step).astype(jnp.float32)
        step *= 2
    return total


def attend_kernel(key_seg, query_seg, query, key, value_t, out_t, log_total):
    scores = contract_cols(key[...], query[...]) * score_scale
    scores = jnp.where(key_seg[:, :1] == query_seg[...], scores, negative)
    peak = jnp.max(scores, axis=0, keepdims=True)
    weights = jnp.exp(scores - peak)
    total = jnp.sum(weights, axis=0, keepdims=True)
    out_t[...] = (mm(value_t[...], weights.astype(jnp.bfloat16)) / total).T.astype(out_t.dtype)
    log_total[...] = peak + jnp.log(total)


def attend(key_seg, query_seg, query, key, value_t):
    count = query.shape[0]
    whole = lambda i: (0, 0)
    return pl.pallas_call(
        attend_kernel,
        grid=(count // query_block,),
        in_specs=[
            pl.BlockSpec((count, HEAD_DIM), whole),
            pl.BlockSpec((1, query_block), lambda i: (0, i)),
            pl.BlockSpec((query_block, HEAD_DIM), lambda i: (i, 0)),
            pl.BlockSpec((count, HEAD_DIM), whole),
            pl.BlockSpec((HEAD_DIM, count), whole),
        ],
        out_specs=[
            pl.BlockSpec((query_block, HEAD_DIM), lambda i: (i, 0)),
            pl.BlockSpec((1, query_block), lambda i: (0, i)),
        ],
        out_shape=[
            jax.ShapeDtypeStruct((count, HEAD_DIM), jnp.bfloat16),
            jax.ShapeDtypeStruct((1, count), jnp.float32),
        ],
        cost_estimate=pl.CostEstimate(
            flops=4 * count * count * HEAD_DIM,
            bytes_accessed=count * HEAD_DIM * 10,
            transcendentals=count * count,
        ),
        name="attend",
    )(key_seg, query_seg, query, key, value_t)


def attend_back_kernel(
    key_seg, query_seg, log_total, query, upstream, key, key_t, value, dquery, dkey, dvalue
):
    @pl.when(pl.program_id(0) == 0)
    def _():
        dkey[...] = jnp.zeros_like(dkey)
        dvalue[...] = jnp.zeros_like(dvalue)

    scores = contract_cols(key[...], query[...]) * score_scale
    probs = jnp.where(
        key_seg[:, :1] == query_seg[...], jnp.exp(scores - log_total[...]), 0.0
    )
    dvalue[...] += mm(probs.astype(jnp.bfloat16), upstream[...])
    dprobs = contract_cols(value[...], upstream[...])
    delta = jnp.sum(probs * dprobs, axis=0, keepdims=True)
    dscores = (probs * (dprobs - delta)).astype(jnp.bfloat16)
    dkey[...] += mm(dscores, query[...]) * score_scale
    dquery[...] = (mm(key_t[...], dscores) * score_scale).T


def attend_back(key_seg, query_seg, log_total, query, upstream, key, key_t, value):
    count = query.shape[0]
    whole = lambda i: (0, 0)
    return pl.pallas_call(
        attend_back_kernel,
        grid=(count // query_block,),
        in_specs=[
            pl.BlockSpec((count, HEAD_DIM), whole),
            pl.BlockSpec((1, query_block), lambda i: (0, i)),
            pl.BlockSpec((1, query_block), lambda i: (0, i)),
            pl.BlockSpec((query_block, HEAD_DIM), lambda i: (i, 0)),
            pl.BlockSpec((query_block, HEAD_DIM), lambda i: (i, 0)),
            pl.BlockSpec((count, HEAD_DIM), whole),
            pl.BlockSpec((HEAD_DIM, count), whole),
            pl.BlockSpec((count, HEAD_DIM), whole),
        ],
        out_specs=[
            pl.BlockSpec((query_block, HEAD_DIM), lambda i: (i, 0)),
            pl.BlockSpec((count, HEAD_DIM), whole),
            pl.BlockSpec((count, HEAD_DIM), whole),
        ],
        out_shape=[jax.ShapeDtypeStruct((count, HEAD_DIM), jnp.float32)] * 3,
        cost_estimate=pl.CostEstimate(
            flops=10 * count * count * HEAD_DIM,
            bytes_accessed=count * HEAD_DIM * 20,
            transcendentals=count * count,
        ),
        name="attend_back",
    )(key_seg, query_seg, log_total, query, upstream, key, key_t, value)


def local(
    tokens,
    segments,
    routes,
    route_gates,
    attn_gain,
    query_gain,
    key_gain,
    ffn_gain,
    w_query,
    w_key,
    w_value,
    w_out,
    w_gate,
    w_up,
    w_down,
    cotangent,
):
    row_count, width = tokens.shape
    top_count = routes.shape[1]
    devices = lax.axis_size("expert")
    me = lax.axis_index("expert")
    seq_length = row_count * devices
    part = width // devices
    sharing = HEAD_DIM // part
    head = me // sharing
    sub = me % sharing
    w_rows = w_query.shape[0]

    def gather(values):
        return lax.all_gather(values, "expert", axis=0, tiled=True)

    def exchange(values):
        return lax.all_to_all(values, "expert", split_axis=0, concat_axis=0, tiled=True)

    def to_heads(rows):
        blocks = rows.reshape(rows.shape[0], HEADS, HEAD_DIM).transpose(1, 0, 2)
        return jnp.repeat(blocks, sharing, axis=0)

    def my_part(columns):
        return lax.dynamic_slice_in_dim(columns, sub * part, part, axis=columns.ndim - 1)

    resid_in = tokens.astype(jnp.float32)
    pre_in, normal_in, inverse_in = norm_rows(resid_in, attn_gain)
    normed_in = pre_in.astype(jnp.bfloat16)
    normed_all = gather(normed_in)

    head_w = exchange(
        jnp.concatenate([to_heads(w_query), to_heads(w_key), to_heads(w_value)], axis=2)
    ).reshape(width, 3 * HEAD_DIM)

    out_full = gather(w_out)
    cot_all = gather(cotangent)

    experts_all = devices * w_gate.shape[0]
    slots = min(row_count, row_count * top_count * 3 // (2 * experts_all))
    hits = routes[:, :, None] == jnp.arange(experts_all, dtype=jnp.int32)[None, None, :]
    gate_table = jnp.sum(jnp.where(hits, route_gates[:, :, None], 0.0), axis=1)
    gate_mine = exchange(gate_table.T.reshape(devices, 1, row_count)).reshape(devices, row_count)
    chosen = gate_mine > 0.0
    before = jnp.arange(row_count)[:, None] < jnp.arange(row_count)[None, :]
    rank = mm(chosen.astype(jnp.bfloat16), before.astype(jnp.bfloat16)).astype(jnp.int32)
    rank = jnp.where(chosen, rank, -1)
    picks = rank[:, None, :] == jnp.arange(slots, dtype=jnp.int32)[None, :, None]
    slot_gate = jnp.sum(jnp.where(picks, gate_mine[:, None, :], 0.0), axis=2).reshape(-1, 1)
    picks = picks.astype(jnp.bfloat16)

    def pick(rows):
        return jnp.einsum(
            "bst,btd->bsd",
            picks,
            rows.reshape(devices, row_count, width),
            preferred_element_type=jnp.bfloat16,
        ).reshape(devices * slots, width)

    def unpick(rows):
        return jnp.einsum(
            "bst,bsd->btd",
            picks,
            rows.reshape(devices, slots, width),
            preferred_element_type=jnp.bfloat16,
        ).reshape(seq_length, width)

    raw = mm(normed_all, head_w)
    query_raw, key_raw = raw[:, :HEAD_DIM], raw[:, HEAD_DIM : 2 * HEAD_DIM]
    value = raw[:, 2 * HEAD_DIM :].astype(jnp.bfloat16)
    squares = jnp.stack(
        [jnp.sum(jnp.square(my_part(query_raw)), axis=1), jnp.sum(jnp.square(my_part(key_raw)), axis=1)]
    )
    squares = butterfly(squares, "expert")
    inverse = lax.rsqrt(squares / width + eps)
    inverse_query, inverse_key = inverse[0][:, None], inverse[1][:, None]
    my_query_gain = lax.dynamic_slice_in_dim(query_gain, head * HEAD_DIM, HEAD_DIM)
    my_key_gain = lax.dynamic_slice_in_dim(key_gain, head * HEAD_DIM, HEAD_DIM)
    normal_query = query_raw * inverse_query
    normal_key = key_raw * inverse_key
    cosine, rope_sine = rope_tables(jnp.arange(seq_length, dtype=jnp.int32))
    query_rot = rotate(normal_query * my_query_gain, cosine, rope_sine).astype(jnp.bfloat16)
    key_rot = rotate(normal_key * my_key_gain, cosine, rope_sine).astype(jnp.bfloat16)

    key_seg = jnp.broadcast_to(segments[:, None], (seq_length, HEAD_DIM))
    query_seg = segments[None, :]
    attended, log_total = attend(key_seg, query_seg, query_rot, key_rot, value.T)

    attended_low = (
        exchange(my_part(attended).reshape(devices, row_count, part))
        .transpose(1, 0, 2)
        .reshape(row_count, width)
    )
    middle = resid_in + mm(attended_low, out_full)
    pre_mid, normal_mid, inverse_mid = norm_rows(middle, ffn_gain)
    normed_mid = pre_mid.astype(jnp.bfloat16)

    rows_in = pick(gather(normed_mid))
    grad_eo = (pick(cot_all).astype(jnp.float32) * slot_gate).astype(jnp.bfloat16)
    gate_in = mm(rows_in, w_gate[0])
    up_in = mm(rows_in, w_up[0])
    sigmoid_in = jax.nn.sigmoid(gate_in)
    silu_in = gate_in * sigmoid_in
    hidden = (silu_in * up_in).astype(jnp.bfloat16)
    grad_hidden = contract_cols(grad_eo, w_down[0])
    grad_up_pre = (grad_hidden * silu_in).astype(jnp.bfloat16)
    grad_gate_pre = (
        grad_hidden * up_in * sigmoid_in * (1.0 + gate_in * (1.0 - sigmoid_in))
    ).astype(jnp.bfloat16)
    grad_rows = (
        contract_cols(grad_gate_pre, w_gate[0]) + contract_cols(grad_up_pre, w_up[0])
    ).astype(jnp.bfloat16)

    def scatter(rows):
        return lax.psum_scatter(rows, "expert", scatter_dimension=0, tiled=True)

    grad_normed_mid = scatter(unpick(grad_rows)).astype(jnp.float32)
    down_total = dp_total(contract_rows(hidden, grad_eo).astype(jnp.bfloat16))[None]
    gate_total = dp_total(contract_rows(rows_in, grad_gate_pre).astype(jnp.bfloat16))[None]
    up_total = dp_total(contract_rows(rows_in, grad_up_pre).astype(jnp.bfloat16))[None]
    expert_out = (mm(hidden, w_down[0]) * slot_gate).astype(jnp.bfloat16)
    mixed = scatter(unpick(expert_out)).astype(jnp.float32)
    activations = (middle + mixed).astype(jnp.bfloat16)

    grad_out = cotangent.astype(jnp.float32)
    mid_back, grad_ffn_gain = norm_back(grad_normed_mid, normal_mid, inverse_mid, ffn_gain)
    grad_middle = grad_out + mid_back
    grad_branch = grad_middle.astype(jnp.bfloat16)
    grad_attended = exchange(
        to_heads(contract_cols(grad_branch, out_full).astype(jnp.bfloat16))
    ).reshape(seq_length, HEAD_DIM)
    branch_all = gather(grad_branch)
    out_part = contract_rows(my_part(attended), branch_all)

    grad_query_rot, grad_key_rot, grad_value = attend_back(
        key_seg, query_seg, log_total, query_rot, grad_attended, key_rot, key_rot.T, value
    )
    grad_value = grad_value.astype(jnp.bfloat16)
    grad_query_pre = rotate(grad_query_rot, cosine, -rope_sine)
    grad_key_pre = rotate(grad_key_rot, cosine, -rope_sine)
    weighted_query = grad_query_pre * my_query_gain
    weighted_key = grad_key_pre * my_key_gain
    inner = jnp.stack(
        [
            jnp.sum(my_part(weighted_query * normal_query), axis=1),
            jnp.sum(my_part(weighted_key * normal_key), axis=1),
        ]
    )
    inner = butterfly(inner, "expert") / width
    grad_query = (inverse_query * (weighted_query - normal_query * inner[0][:, None])).astype(
        jnp.bfloat16
    )
    grad_key = (inverse_key * (weighted_key - normal_key * inner[1][:, None])).astype(jnp.bfloat16)
    grad_query_gain = my_part(jnp.sum(grad_query_pre * normal_query, axis=0))
    grad_key_gain = my_part(jnp.sum(grad_key_pre * normal_key, axis=0))

    grad_raw = jnp.concatenate(
        [my_part(grad_query), my_part(grad_key), my_part(grad_value)], axis=1
    )
    part_w = jnp.concatenate(
        [my_part(head_w[:, i * HEAD_DIM : (i + 1) * HEAD_DIM]) for i in range(3)], axis=1
    )
    grad_normed_in = scatter(contract_cols(grad_raw, part_w).astype(jnp.bfloat16)).astype(
        jnp.float32
    )
    in_back, _ = norm_back(grad_normed_in, normal_in, inverse_in, attn_gain)
    input_grad = (grad_middle + in_back).astype(jnp.bfloat16)

    grad_w = contract_rows(normed_all, grad_raw)
    grad_attn_gain = jnp.sum(grad_w * part_w.astype(jnp.float32), axis=1) / attn_gain
    w_columns = exchange(grad_w.astype(jnp.bfloat16).reshape(devices, w_rows, 3 * part))
    dense = (
        w_columns.reshape(devices, w_rows, 3, part)
        .transpose(1, 2, 0, 3)
        .reshape(w_rows, 3 * width)
    )
    dense_total = dp_total(jnp.concatenate([dense, out_part.astype(jnp.bfloat16)], axis=1))

    def placed(values):
        return lax.dynamic_update_slice_in_dim(
            jnp.zeros((width,), jnp.float32), values, me * part, 0
        )

    gain_total = butterfly(
        butterfly(
            jnp.stack(
                [grad_attn_gain, placed(grad_query_gain), placed(grad_key_gain), grad_ffn_gain]
            ),
            "expert",
        ),
        "dp",
    )
    return (
        activations,
        input_grad,
        gain_total[0],
        gain_total[1],
        gain_total[2],
        gain_total[3],
        dense_total[:, :width],
        dense_total[:, width : 2 * width],
        dense_total[:, 2 * width : 3 * width],
        dense_total[:, 3 * width :],
        gate_total,
        up_total,
        down_total,
    )


def solution(mesh):
    in_specs = (
        P(("dp", "expert"), None),
        P("dp"),
        P(("dp", "expert"), None),
        P(("dp", "expert"), None),
        P(),
        P(),
        P(),
        P(),
        P("expert", None),
        P("expert", None),
        P("expert", None),
        P("expert", None),
        P("expert", None, None),
        P("expert", None, None),
        P("expert", None, None),
        P(("dp", "expert"), None),
    )
    out_specs = (
        P(("dp", "expert"), None),
        P(("dp", "expert"), None),
        P(),
        P(),
        P(),
        P(),
        P("expert", None),
        P("expert", None),
        P("expert", None),
        P("expert", None),
        P("expert", None, None),
        P("expert", None, None),
        P("expert", None, None),
    )
    return jax.shard_map(local, mesh=mesh, in_specs=in_specs, out_specs=out_specs, check_vma=False)
```

time: 2230 us -> 995 us (0.45)
  waiting for transfers between devices: 1340 us -> 546 us
  local copies, waits for them, and re-layouts: 223 us -> 37.6 us
  matrix products: 325 us -> 161 us
  starting transfers between devices: 94.7 us -> 32.7 us
  other arithmetic: 101 us -> 64.9 us
  Pallas kernels: 0 us -> 32.4 us
    all_to_all x4 -> x2, waiting for transfers between devices: 445 us -> 0.01 us  [exchange(): lax.all_to_all(values, 'expert', split_axis=0, concat_axis=0, tiled=True)]
    unnamed x11 -> x8, waiting for transfers between devices: 299 us -> 1.46 us
    psum x1 -> x0, waiting for transfers between devices: 278 us -> none  [local(): lax.psum(dense_rows, 'dp').astype(jnp.float32)]
    ppermute x0 -> x17, waiting for transfers between devices: none -> 243 us  [swap(): return lax.ppermute(values, axis, [(i, i ^ step) for i in range(count)])]
    dot_general x35 -> x10, matrix products: 202 us -> 66.4 us  [the longest x6 37.6 us: mm(): return jnp.dot(left, right, preferred_element_type=jnp.float32)]
    all_gather x8 -> x5, waiting for transfers between devices: 318 us -> 199 us  [gather(): return lax.all_gather(values, 'expert', axis=0, tiled=True)]
    reduce_scatter x0 -> x3, waiting for transfers between devices: none -> 103 us  [scatter(): return lax.psum_scatter(rows, 'expert', scatter_dimension=0, tiled=True)]
    all_to_all x0 -> x3, blocking collectives: none -> 97.5 us  [exchange(): lax.all_to_all(values, 'expert', split_axis=0, concat_axis=0, tiled=True)]
  transfers between devices with their start and end apart: 14 -> 27, of which waited for: 11 -> 18; matrix products, arithmetic and copies ran while one was open for 17% -> 18% of each run, Pallas kernels for 0% -> 3%
where the time goes in v1:
time: 995 us; the launch traced here: 987 us
  waiting for transfers between devices  546 us (55%)
  matrix products  161 us (16%)
  blocking collectives  97.5 us (10%)
  other arithmetic  64.9 us (7%)
  local copies, waits for them, and re-layouts  37.6 us (4%)
  starting transfers between devices  32.7 us (3%)
  Pallas kernels  32.4 us (3%)
  between operations  15.3 us (2%)
    ppermute x17, waiting for transfers between devices, swap(): return lax.ppermute(values, axis, [(i, i ^ step) for i in range(count)])  243 us
    all_gather x5, waiting for transfers between devices, gather(): return lax.all_gather(values, 'expert', axis=0, tiled=True)  199 us
    reduce_scatter x3, waiting for transfers between devices, scatter(): return lax.psum_scatter(rows, 'expert', scatter_dimension=0, tiled=True)  103 us
    all_to_all x3, blocking collectives, exchange(): lax.all_to_all(values, 'expert', split_axis=0, concat_axis=0, tiled=True)  97.5 us
    dot_general x5, matrix products, contract_cols(): lax.dot_general(left, right, (((1,), (1,)), ((), ())), preferred_element_...  52.1 us
    dot_general x5, matrix products, contract_rows(): lax.dot_general(left, right, (((0,), (0,)), ((), ())), preferred_element_...  42.1 us
    dot_general x6, matrix products, mm(): return jnp.dot(left, right, preferred_element_type=jnp.float32)  37.6 us
    ppermute x17, starting transfers between devices, swap(): return lax.ppermute(values, axis, [(i, i ^ step) for i in range(count)])  22.9 us
  transfers between devices with their start and end apart: 27, of which 18 were waited for; matrix products, arithmetic and copies ran while one was open for 18% of the time, Pallas kernels for 3%

profile of v1, /device:TPU:0, one launch (start us, length us, event | category | flops | bytes accessed | tf_op | source)
XLA Modules:
  0.0 987.3 jit_solution(17618562435692863333)
XLA Ops:
  13.8 60.1 %all_to_all.25 = bf16[16,128,384]{2,1,0:T(8,128)(2,1)S(1)} all-to-all(bf16[16,128,384]{2,1,0:T(8,128)(2,1)S(1)} %pad_maximum_fusion.1), channel_id=1, replica_groups=mesh['dp'=2,'expert'=16] {'expert'}, dimensions={0} | all-to-all | bytes 3145728 | tf_op jit(solution)/shard_map/all_to_all | solution.py:216
  74.0 40.0 %all-gather.6.cloned.1.call-done = bf16[2048,2048]{1,0:T(8,128)(2,1)} async-done(((bf16[128,2048]{1,0:T(8,128)(2,1)}), bf16[2048,2048]{1,0:T(8,128)(2,1)}) %all-gather.6.cloned.1.call-update) | async-done | bytes 8388624 | tf_op jit(solution)/shard_map/all_gather | solution.py:213
  145.4 12.7 %attend.1 = (bf16[2048,128]{1,0:T(8,128)(2,1)}, f32[1,2048]{1,0:T(1,128)}) custom-call(s32[2048,128]{1,0:T(8,128)} %broadcast_in_dim.38.key_seg, s32[1,2048]{1,0:T(1,128)} %bitcast.185, bf16[2048,128]{1,0:T(8,128)(2,1)} %copy.120.query, bf16[2048,128]{1,0:T(8,128)(2,1)} %copy.121.key, bf16[128,2048]{1,0:T(8,128)(2,1)} %copy.122.value_t), custom_call_target="tpu_custom_call" | custom-call | flops 2147483648 | bytes 2621440 | tf_op jit(solution)/shard_map/attend/pallas_call | solution.py:105
  163.8 35.3 %all-gather.8.cloned.1.call-done = bf16[2048,2048]{1,0:T(8,128)(2,1)} async-done(((bf16[128,2048]{1,0:T(8,128)(2,1)}), bf16[2048,2048]{1,0:T(8,128)(2,1)}) %all-gather.8.cloned.1.call-update) | async-done | bytes 8388624 | tf_op jit(solution)/shard_map/all_gather | solution.py:213
  205.0 10.0 %all_to_all.26 = f32[16,1,128]{2,1,0:T(1,128)S(1)} all-to-all(f32[16,1,128]{2,1,0:T(1,128)S(1)} %bitcast.184), channel_id=1, replica_groups=mesh['dp'=2,'expert'=16] {'expert'}, dimensions={0} | all-to-all | bytes 16384 | tf_op jit(solution)/shard_map/all_to_all | solution.py:216
  215.5 59.9 %all-gather.12.cloned.1.call-done = bf16[2048,2048]{1,0:T(8,128)(2,1)} async-done(((bf16[128,2048]{1,0:T(8,128)(2,1)}), bf16[2048,2048]{1,0:T(8,128)(2,1)}) %all-gather.12.cloned.1.call-update) | async-done | bytes 8388624 | tf_op jit(solution)/shard_map/all_gather | solution.py:213
  275.4 12.0 %multiply_convert_fusion = (bf16[16,96,2048]{2,1,0:T(8,128)(2,1)}, f32[16,96,2048]{2,1,0:T(8,128)}) fusion(f32[16,96]{1,0:T(8,128)S(1)} %select_reduce_fusion, bf16[16,128,2048]{2,1,0:T(8,128)(2,1)} %bitcast.132, s32[16,128]{1,0:T(8,128)S(1)} %fusion.18), kind=kOutput, calls=%fused_computation.3 | convolution fusion | flops 814940160 | bytes 27277312 | tf_op jit(solution)/shard_map/bst,btd->bsd/dot_general | solution.py:251
  287.4 63.7 %all-gather.10.cloned.1.call-done = bf16[2048,2048]{1,0:T(8,128)(2,1)} async-done(((bf16[128,2048]{1,0:T(8,128)(2,1)}), bf16[2048,2048]{1,0:T(8,128)(2,1)}) %all-gather.10.cloned.1.call-update) | async-done | bytes 8388624 | tf_op jit(solution)/shard_map/all_gather | solution.py:213
  373.6 15.6 %multiply_convert_fusion.2 = (bf16[1536,1024]{1,0:T(8,128)(2,1)}, bf16[1536,1024]{1,0:T(8,128)(2,1)}, bf16[1536,1024]{1,0:T(8,128)(2,1)}) fusion(f32[1536,1024]{1,0:T(8,128)} %fusion.10, f32[1536,1024]{1,0:T(8,128)} %fusion.6, bf16[1536,2048]{1,0:T(8,128)(2,1)S(1)} %bitcast.136, bf16[1,1024,2048]{2,1,0:T(8,128)(2,1)} %param.30), kind=kOutput, calls=%fused_computation.9 | convolution fusion | flops 6466043904 | bytes 32505856 | tf_op jit(solution)/shard_map/dot_general | solution.py:64
  389.3 12.4 %fusion.8 = f32[1536,2048]{1,0:T(8,128)} fusion(bf16[1536,1024]{1,0:T(8,128)(2,1)} %get-tuple-element.73, bf16[1,2048,1024]{2,1,0:T(8,128)(2,1)} %param.28), kind=kOutput, calls=%fused_computation.21 | convolution fusion | flops 6442450944 | bytes 19922944 | tf_op jit(solution)/shard_map/dot_general | solution.py:64
  401.7 10.7 %add_convert_fusion = bf16[1536,2048]{1,0:T(8,128)(2,1)S(1)} fusion(f32[1536,2048]{1,0:T(8,128)} %fusion.8, bf16[1536,1024]{1,0:T(8,128)(2,1)} %get-tuple-element.72, bf16[1,2048,1024]{2,1,0:T(8,128)(2,1)S(1)} %copy-done.32), kind=kOutput, calls=%fused_computation.2 | convolution fusion | flops 6448742400 | bytes 26214400 | tf_op jit(solution)/shard_map/dot_general | solution.py:64
  418.6 102.5 %reduce-scatter.6.cloned.1.call-done = bf16[128,2048]{1,0:T(8,128)(2,1)} async-done(((bf16[2048,2048]{1,0:T(8,128)(2,1)}), bf16[128,2048]{1,0:T(8,128)(2,1)}) %reduce-scatter.6.cloned.1.call-update) | async-done | bytes 524304 | tf_op jit(solution)/shard_map/reduce_scatter | solution.py:313
  531.5 27.4 %all_to_all.27 = bf16[16,128,128]{2,1,0:T(8,128)(2,1)} all-to-all(bf16[16,128,128]{2,1,0:T(8,128)(2,1)S(1)} %bitcast.151), channel_id=1, replica_groups=mesh['dp'=2,'expert'=16] {'expert'}, dimensions={0} | all-to-all | bytes 1048576 | tf_op jit(solution)/shard_map/all_to_all | solution.py:216
  558.9 19.8 %attend_back.1 = (f32[2048,128]{1,0:T(8,128)}, f32[2048,128]{1,0:T(8,128)}, f32[2048,128]{1,0:T(8,128)}) custom-call(s32[2048,128]{1,0:T(8,128)} %broadcast_in_dim.38.key_seg, s32[1,2048]{1,0:T(1,128)} %bitcast.186, f32[1,2048]{1,0:T(1,128)} %get-tuple-element.19.log_total, bf16[2048,128]{1,0:T(8,128)(2,1)} %copy.120.query, bf16[2048,128]{1,0:T(8,128)(2,1)} %bitcast.155, ...), custom_call_target="tpu_custom_call" | custom-call | flops 5368709120 | bytes 5242880 | tf_op jit(solution)/shard_map/attend_back/pallas_call | solution.py:155
  625.6 9.7 multiply_convert_fusion.1
  641.0 11.3 %convolution_convert_fusion.4 = bf16[2048,1024]{1,0:T(8,128)(2,1)} fusion(bf16[1536,2048]{1,0:T(8,128)(2,1)} %bitcast.139, bf16[1536,1024]{1,0:T(8,128)(2,1)} %get-tuple-element.73), kind=kOutput, calls=%fused_computation.28 | convolution fusion | flops 6444548096 | bytes 13631488 | tf_op jit(solution)/shard_map/dot_general | solution.py:58
  675.5 11.5 %convolution_convert_fusion.2 = bf16[1024,2048]{1,0:T(8,128)(2,1)} fusion(bf16[1536,1024]{1,0:T(8,128)(2,1)} %get-tuple-element.74, bf16[1536,2048]{1,0:T(8,128)(2,1)} %fusion), kind=kOutput, calls=%fused_computation.26 | convolution fusion | flops 6444548096 | bytes 13631488 | tf_op jit(solution)/shard_map/dot_general | solution.py:58
  696.1 50.2 %collective-permute-done.14 = bf16[2048,1024]{1,0:T(8,128)(2,1)} collective-permute-done((bf16[2048,1024]{1,0:T(8,128)(2,1)}, bf16[2048,1024]{1,0:T(8,128)(2,1)}, u32[]{:S(2)}, u32[]{:S(2)}) %collective-permute-start.14) | collective-permute-done | bytes 4194336 | tf_op jit(solution)/shard_map/ppermute | solution.py:71
  746.3 9.8 add_bitcast_fusion.2
  758.3 77.9 %collective-permute-done.15 = bf16[2048,1024]{1,0:T(8,128)(2,1)} collective-permute-done((bf16[2048,1024]{1,0:T(8,128)(2,1)}, bf16[2048,1024]{1,0:T(8,128)(2,1)}, u32[]{:S(2)}, u32[]{:S(2)}) %collective-permute-start.15) | collective-permute-done | bytes 4194336 | tf_op jit(solution)/shard_map/ppermute | solution.py:71
  836.2 8.9 add_bitcast_fusion.1
  858.9 67.1 %collective-permute-done.16 = bf16[1024,2048]{1,0:T(8,128)(2,1)} collective-permute-done((bf16[1024,2048]{1,0:T(8,128)(2,1)}, bf16[1024,2048]{1,0:T(8,128)(2,1)}, u32[]{:S(2)}, u32[]{:S(2)}) %collective-permute-start.16) | collective-permute-done | bytes 4194336 | tf_op jit(solution)/shard_map/ppermute | solution.py:71
  926.0 8.8 add_bitcast_fusion
  940.0 28.6 %collective-permute-done.13 = bf16[128,8192]{0,1:T(8,128)(2,1)} collective-permute-done((bf16[128,8192]{0,1:T(8,128)(2,1)}, bf16[128,8192]{0,1:T(8,128)(2,1)}, u32[]{:S(2)}, u32[]{:S(2)}) %collective-permute-start.13) | collective-permute-done | bytes 2097184 | tf_op jit(solution)/shard_map/ppermute | solution.py:71
  (226 shorter events, 205.9 us)
Async XLA Ops:
  7.2 106.8 %all-gather.6.cloned.1.call-start = ((), (), s32[]{:S(2)}) async-start(), calls=%async_computation.8 | async-start | bytes 8912896 | tf_op jit(solution)/shard_map/all_gather | solution.py:213
  10.6 188.5 %all-gather.8.cloned.1.call-start = ((), (), s32[]{:S(2)}) async-start(), calls=%async_computation.9 | async-start | bytes 8912896 | tf_op jit(solution)/shard_map/all_gather | solution.py:213
  11.4 264.0 %all-gather.12.cloned.1.call-start = ((), (), s32[]{:S(2)}) async-start(), calls=%async_computation.12 | async-start | bytes 8912896 | tf_op jit(solution)/shard_map/all_gather | solution.py:213
  127.0 4.5 collective-permute-start.2
  131.5 5.3 collective-permute-start.3
  160.1 39.0 %all-to-all-start.1 = ((bf16[16,128,128]{1,2,0:T(8,128)(2,1)}), bf16[16,128,128]{1,2,0:T(8,128)(2,1)S(1)}, u32[]{:S(2)}, u32[]{:S(2)}) async-start(bf16[16,128,128]{1,2,0:T(8,128)(2,1)} %copy.123), calls=%async_computation.1 | async-start | bytes 1048576 | tf_op jit(solution)/shard_map/all_to_all | solution.py:216
  163.7 187.4 %all-gather.10.cloned.1.call-start = ((), (), s32[]{:S(2)}) async-start(), calls=%async_computation.10 | async-start | bytes 8912896 | tf_op jit(solution)/shard_map/all_gather | solution.py:213
  204.9 316.3 %reduce-scatter.6.cloned.1.call-start = ((), (), s32[]{:S(2)}) async-start(), calls=%async_computation.13 | async-start | bytes 8912896 | tf_op jit(solution)/shard_map/reduce_scatter | solution.py:313
  418.2 431.1 %all-gather.14.cloned.1.call-start = ((), (), s32[]{:S(2)}) async-start(), calls=%async_computation.15 | async-start | bytes 8912896 | tf_op jit(solution)/shard_map/all_gather | solution.py:213
  524.9 410.6 %reduce-scatter.8.cloned.1.call-start = ((), (), s32[]{:S(2)}) async-start(), calls=%async_computation.14 | async-start | bytes 8912896 | tf_op jit(solution)/shard_map/reduce_scatter | solution.py:313
  590.0 4.4 collective-permute-start.5
  594.4 7.2 collective-permute-start.6
  601.6 5.5 collective-permute-start.7
  617.1 319.8 %reduce-scatter.4.cloned.1.call-start = ((), (), s32[]{:S(2)}) async-start(), calls=%async_computation.11 | async-start | bytes 8912896 | tf_op jit(solution)/shard_map/reduce_scatter | solution.py:313
  652.4 93.9 %collective-permute-start.14 = (bf16[2048,1024]{1,0:T(8,128)(2,1)}, bf16[2048,1024]{1,0:T(8,128)(2,1)}, u32[]{:S(2)}, u32[]{:S(2)}) collective-permute-start(bf16[2048,1024]{1,0:T(8,128)(2,1)} %convolution_convert_fusion.4), channel_id=1, source_target_pairs={{0,16},{16,0},{1,17},{17,1},{2,18},{18,2},{3,19},{19,3},{4,20},{20... | collective-permute-start | bytes 12582920 | tf_op jit(solution)/shard_map/ppermute | solution.py:71
  662.6 173.5 %collective-permute-start.15 = (bf16[2048,1024]{1,0:T(8,128)(2,1)}, bf16[2048,1024]{1,0:T(8,128)(2,1)}, u32[]{:S(2)}, u32[]{:S(2)}) collective-permute-start(bf16[2048,1024]{1,0:T(8,128)(2,1)} %convolution_convert_fusion.3), channel_id=1, source_target_pairs={{0,16},{16,0},{1,17},{17,1},{2,18},{18,2},{3,19},{19,3},{4,20},{20... | collective-permute-start | bytes 12582920 | tf_op jit(solution)/shard_map/ppermute | solution.py:71
  668.6 20.0 %collective-permute-start.8 = (f32[4,2048]{1,0:T(4,128)S(1)}, f32[4,2048]{1,0:T(4,128)S(1)}, u32[]{:S(2)}, u32[]{:S(2)}) collective-permute-start(f32[4,2048]{1,0:T(4,128)S(1)} %pad_maximum_fusion.9), channel_id=1, source_target_pairs={{0,1},{1,0},{2,3},{3,2},{4,5},{5,4},{6,7},{7,6},{8,9},{9,8},{10,11... | collective-permute-start | bytes 98312 | tf_op jit(solution)/shard_map/ppermute | solution.py:71
  670.3 176.4 %all-to-all-start.4 = ((bf16[16,128,384]{1,2,0:T(8,128)(2,1)}), bf16[16,128,384]{1,2,0:T(8,128)(2,1)S(1)}, u32[]{:S(2)}, u32[]{:S(2)}) async-start(bf16[16,128,384]{1,2,0:T(8,128)(2,1)} %copy.133), calls=%async_computation.7 | async-start | bytes 3145728 | tf_op jit(solution)/shard_map/all_to_all | solution.py:216
  687.0 239.1 %collective-permute-start.16 = (bf16[1024,2048]{1,0:T(8,128)(2,1)}, bf16[1024,2048]{1,0:T(8,128)(2,1)}, u32[]{:S(2)}, u32[]{:S(2)}) collective-permute-start(bf16[1024,2048]{1,0:T(8,128)(2,1)} %convolution_convert_fusion.2), channel_id=1, source_target_pairs={{0,16},{16,0},{1,17},{17,1},{2,18},{18,2},{3,19},{19,3},{4,20},{20... | collective-permute-start | bytes 12582920 | tf_op jit(solution)/shard_map/ppermute | solution.py:71
  688.6 6.1 collective-permute-start.9
  694.7 61.4 %collective-permute-start.10 = (f32[4,2048]{1,0:T(4,128)S(1)}, f32[4,2048]{1,0:T(4,128)S(1)}, u32[]{:S(2)}, u32[]{:S(2)}) collective-permute-start(f32[4,2048]{1,0:T(4,128)S(1)} %fusion.111), channel_id=1, source_target_pairs={{0,4},{1,5},{2,6},{3,7},{4,0},{5,1},{6,2},{7,3},{8,12},{9,13},{10,... | collective-permute-start | bytes 98312 | tf_op jit(solution)/shard_map/ppermute | solution.py:71
  756.1 89.0 %collective-permute-start.11 = (f32[4,2048]{1,0:T(4,128)S(1)}, f32[4,2048]{1,0:T(4,128)S(1)}, u32[]{:S(2)}, u32[]{:S(2)}) collective-permute-start(f32[4,2048]{1,0:T(4,128)S(1)} %add.161), channel_id=1, source_target_pairs={{0,8},{1,9},{2,10},{3,11},{4,12},{5,13},{6,14},{7,15},{8,0},{9,1},... | collective-permute-start | bytes 98312 | tf_op jit(solution)/shard_map/ppermute | solution.py:71
  845.1 89.7 %collective-permute-start.12 = (f32[4,2048]{1,0:T(4,128)S(1)}, f32[4,2048]{1,0:T(4,128)S(1)}, u32[]{:S(2)}, u32[]{:S(2)}) collective-permute-start(f32[4,2048]{1,0:T(4,128)S(1)} %add.162), channel_id=1, source_target_pairs={{0,16},{16,0},{1,17},{17,1},{2,18},{18,2},{3,19},{19,3},{4,20},{20... | collective-permute-start | bytes 98312 | tf_op jit(solution)/shard_map/ppermute | solution.py:71
  858.3 110.3 %collective-permute-start.13 = (bf16[128,8192]{0,1:T(8,128)(2,1)}, bf16[128,8192]{0,1:T(8,128)(2,1)}, u32[]{:S(2)}, u32[]{:S(2)}) collective-permute-start(bf16[128,8192]{0,1:T(8,128)(2,1)} %pad_maximum_fusion), channel_id=1, source_target_pairs={{0,16},{16,0},{1,17},{17,1},{2,18},{18,2},{3,19},{19,3},{4,20},{20... | collective-permute-start | bytes 6291464 | tf_op jit(solution)/shard_map/ppermute | solution.py:71
  (44 other events, 747.1 us)
Sparse Core Ops, SparseCore 0:
  10.8 103.1 all-gather.5
  116.1 82.9 all-gather.7
  201.3 74.0 all-gather.11
  278.0 73.1 all-gather.9
  418.3 102.8 reduce-scatter.5
  525.0 86.5 all-gather.13
  617.2 120.3 reduce-scatter.7
  741.7 103.4 reduce-scatter.3

commit v2 on v1

v2 whole, which is shorter than its diff:
```python
import functools

import jax
import jax.numpy as jnp
from jax import lax
from jax.experimental import pallas as pl
from jax.experimental.pallas import tpu as pltpu
from jax.sharding import PartitionSpec as P

HEADS = 16
HEAD_DIM = 128


eps = 1e-05
rope_base = 50000.0
negative = -1e30
score_scale = HEAD_DIM ** (-0.5)
query_block = 256


def norm_rows(values, norm_gain):
    inverse = lax.rsqrt(jnp.mean(values * values, axis=-1, keepdims=True) + eps)
    normal = values * inverse
    return (normal * norm_gain, normal, inverse)


def norm_back(upstream, normal, inverse, norm_gain):
    weighted = upstream * norm_gain
    inner_mean = jnp.mean(weighted * normal, axis=-1, keepdims=True)
    return (inverse * (weighted - normal * inner_mean), jnp.sum(upstream * normal, axis=0))


def rope_tables(positions):
    half_dim = HEAD_DIM // 2
    frequency = rope_base ** (-(jnp.arange(half_dim, dtype=jnp.float32) * 2.0 / HEAD_DIM))
    theta = frequency[:, None] * positions.astype(jnp.float32)[None, :]
    return (jnp.cos(theta), jnp.sin(theta))


def mm(left, right):
    return jnp.dot(left, right, preferred_element_type=jnp.float32)


def contract_rows(left, right):
    return lax.dot_general(
        left, right, (((0,), (0,)), ((), ())), preferred_element_type=jnp.float32
    )


def contract_cols(left, right):
    return lax.dot_general(
        left, right, (((1,), (1,)), ((), ())), preferred_element_type=jnp.float32
    )


def swap(values, axis, step):
    count = lax.axis_size(axis)
    return lax.ppermute(values, axis, [(i, i ^ step) for i in range(count)])


def together(*values):
    return lax.optimization_barrier(values)


def after(values, *others):
    return lax.optimization_barrier((values,) + others)[0]


def butterfly(values, axis):
    step = 1
    while step < lax.axis_size(axis):
        values = values + swap(values, axis, step)
        step *= 2
    return values


near_order = ((0, 1, 2, 3), (1, 0, 2, 3), (2, 3, 1, 0), (3, 2, 1, 0))


def moves(target):
    pairs = []
    for index in range(16):
        far = target(index // 4)
        if far is not None:
            pairs.append((index, far * 4 + index % 4))
    return pairs


swap_near = moves(lambda z: z ^ 1)
swap_middle = moves(lambda z: {1: 2, 2: 1}.get(z))
move_out = moves(lambda z: {1: 0, 2: 3}.get(z))
move_in = moves(lambda z: {0: 1, 3: 2}.get(z))
swap_row = [(i, i ^ 2) for i in range(16)]
swap_core = [(i, i ^ 1) for i in range(16)]


def send(values, pairs):
    return lax.ppermute(values, "expert", pairs)


def arrival_order(me):
    near = jnp.asarray(near_order, jnp.int32)[me // 4] * 4
    row, core = (me // 2) % 2, me % 2
    return jnp.concatenate(
        [near + (row ^ j) * 2 + (core ^ i) for i in (0, 1) for j in (0, 1)]
    ).astype(jnp.int32)


class Rounds:
    def __init__(self, steps):
        self.steps = steps
        self.result = None
        self.over = False
        self.sent = ()
        self._go(None)

    def _go(self, arrived):
        try:
            self.sent = self.steps.send(arrived)
        except StopIteration as stop:
            self.result, self.sent, self.over = stop.value, (), True

    def step(self, *others):
        values = together(*self.sent, *others) if self.sent or others else ()
        count = len(self.sent)
        if not self.over:
            self._go(values[:count])
        return values[count:]

    def finish(self):
        while not self.over:
            self.step()
        return self.result


def gather_rounds(block):
    at = lax.axis_index("expert") // 4
    outer = (at == 0) | (at == 3)
    first, second, row = yield (
        send(block, swap_near),
        send(block, swap_middle),
        send(block, swap_row),
    )
    third, second_out, row_first, core = yield (
        send(first, swap_middle),
        send(second, move_out),
        send(first, swap_row),
        send(block, swap_core),
    )
    second = jnp.where(outer, second_out, second)
    third_out, row_second, core_first, core_row = yield (
        send(third, move_out),
        send(second, swap_row),
        send(first, swap_core),
        send(row, swap_core),
    )
    third = jnp.where(outer, third_out, third)
    row_third, core_second, core_third, core_row_first, core_row_second = yield (
        send(third, swap_row),
        send(second, swap_core),
        send(third, swap_core),
        send(row_first, swap_core),
        send(row_second, swap_core),
    )
    (core_row_third,) = yield (send(row_third, swap_core),)
    return [
        block,
        first,
        second,
        third,
        row,
        row_first,
        row_second,
        row_third,
        core,
        core_first,
        core_second,
        core_third,
        core_row,
        core_row_first,
        core_row_second,
        core_row_third,
    ]


def gather_whole(block):
    yield ()
    return list(lax.all_gather(block, "expert", axis=0))


def add_low(left, right):
    return (left.astype(jnp.float32) + right.astype(jnp.float32)).astype(jnp.bfloat16)


def scatter_rounds(make, count):
    (far,) = yield (send(make(count // 2, count // 2), swap_core),)
    close = make(0, count // 2)
    rows = count // 16

    def both(j, k):
        here = slice((j * 4 + k) * rows, (j * 4 + k + 1) * rows)
        return add_low(close[here], far[here])

    (row,) = yield (send(both(1, 3), swap_row),)
    third = add_low(both(0, 3), row)
    row, third_in = yield (send(both(1, 2), swap_row), send(third, move_in))
    second = add_low(both(0, 2), row)
    third = add_low(third, third_in)
    row, second_in, third_in = yield (
        send(both(1, 1), swap_row),
        send(second, move_in),
        send(third, swap_middle),
    )
    first = add_low(add_low(both(0, 1), row), third_in)
    second = add_low(second, second_in)
    row, second_in, first_in = yield (
        send(both(1, 0), swap_row),
        send(second, swap_middle),
        send(first, swap_near),
    )
    return (
        both(0, 0).astype(jnp.float32)
        + row.astype(jnp.float32)
        + second_in.astype(jnp.float32)
        + first_in.astype(jnp.float32)
    )


def scatter_whole(make, count):
    yield ()
    return lax.psum_scatter(make(0, count), "expert", scatter_dimension=0, tiled=True).astype(
        jnp.float32
    )


def pick_kernel(picks, scale, *refs):
    *blocks, out = refs
    slots = picks.shape[1]
    for index, block in enumerate(blocks):
        here = slice(index * slots, (index + 1) * slots)
        out[here, :] = (mm(picks[index], block[...]) * scale[here, :]).astype(out.dtype)


def pick(picks, scale, blocks):
    count, slots, tokens = picks.shape
    width = blocks[0].shape[1]
    return pl.pallas_call(
        pick_kernel,
        out_shape=jax.ShapeDtypeStruct((count * slots, width), jnp.bfloat16),
        cost_estimate=pl.CostEstimate(
            flops=2 * count * tokens * slots * width,
            bytes_accessed=2 * count * (tokens + slots) * width,
            transcendentals=0,
        ),
        name="pick",
    )(picks, scale, *blocks)


def merge_kernel(*refs):
    *pairs, out = refs
    count = len(pairs) // 2
    for index in range(count):

        @pl.when(pl.program_id(0) == index)
        def _():
            out[...] = pairs[index][...].astype(jnp.float32) + pairs[count + index][...].astype(
                jnp.float32
            )


def merge(own, far):
    rows, width = own[0].shape
    return pl.pallas_call(
        merge_kernel,
        grid=(len(own),),
        in_specs=[pl.BlockSpec((rows, width), lambda i: (0, 0))] * (2 * len(own)),
        out_specs=pl.BlockSpec((rows, width), lambda i: (i, 0)),
        out_shape=jax.ShapeDtypeStruct((len(own) * rows, width), jnp.float32),
        cost_estimate=pl.CostEstimate(
            flops=len(own) * rows * width,
            bytes_accessed=8 * len(own) * rows * width,
            transcendentals=0,
        ),
        name="merge",
    )(*own, *far)


def project_kernel(order, left_t, left_next_t, right, out):
    left = jnp.concatenate([left_t[...].T, left_next_t[...].T], axis=0)
    out[...] = mm(left, right[...]).astype(out.dtype)


def project(order, left_t, right, rows, first, count):
    depth, width = right.shape
    begin = first // rows
    return pl.pallas_call(
        project_kernel,
        grid_spec=pltpu.PrefetchScalarGridSpec(
            num_scalar_prefetch=1,
            grid=(count // (2 * rows),),
            in_specs=[
                pl.BlockSpec((depth, rows), lambda i, order: (0, order[begin + 2 * i])),
                pl.BlockSpec((depth, rows), lambda i, order: (0, order[begin + 2 * i + 1])),
                pl.BlockSpec((depth, width), lambda i, order: (0, 0)),
            ],
            out_specs=pl.BlockSpec((2 * rows, width), lambda i, order: (i, 0)),
        ),
        out_shape=jax.ShapeDtypeStruct((count, width), jnp.bfloat16),
        cost_estimate=pl.CostEstimate(
            flops=2 * count * depth * width,
            bytes_accessed=2 * (count * (depth + width) + depth * width),
            transcendentals=0,
        ),
        name="project",
    )(order, left_t, left_t, right)


scalars = pl.BlockSpec(memory_space=pltpu.SMEM)
vectors = pl.BlockSpec(memory_space=pltpu.VMEM)


def lanes(order, index, rows):
    return pl.ds(pl.multiple_of(order[index] * rows, rows), rows)


def stack_kernel(rows, order, left_t, *refs):
    *blocks, out = refs
    for index in range(0, len(blocks), 4):
        four = range(index, index + 4)
        left = jnp.concatenate([left_t[:, lanes(order, i, rows)] for i in four], axis=1)
        right = jnp.concatenate([blocks[i][:rows] for i in four], axis=0)
        term = mm(left, right)
        if index == 0:
            out[...] = term
        else:
            out[...] += term


def stack_product(order, left_t, rows, blocks):
    width = blocks[0].shape[1]
    return pl.pallas_call(
        functools.partial(stack_kernel, rows),
        in_specs=[scalars, vectors] + [vectors] * len(blocks),
        out_specs=vectors,
        out_shape=jax.ShapeDtypeStruct((left_t.shape[0], width), jnp.float32),
        cost_estimate=pl.CostEstimate(
            flops=2 * left_t.size * width,
            bytes_accessed=2 * len(blocks) * rows * width,
            transcendentals=0,
        ),
        name="stack_product",
    )(order, left_t, *blocks)


def heads_kernel(rows, order, weight, *refs):
    *blocks, query_t, key_t, value, value_t, squares = refs
    for index in range(0, len(blocks), 4):
        four = range(index, index + 4)
        raw = mm(jnp.concatenate([blocks[i][:rows] for i in four], axis=0), weight[...])
        for i in four:
            own = raw[(i - index) * rows : (i - index + 1) * rows]
            here = lanes(order, i, rows)
            query = own[:, :HEAD_DIM].T
            key = own[:, HEAD_DIM : 2 * HEAD_DIM].T
            query_t[:, here] = query
            key_t[:, here] = key
            value[here, :] = own[:, 2 * HEAD_DIM :].astype(value.dtype)
            value_t[:, here] = own[:, 2 * HEAD_DIM :].T.astype(value.dtype)
            squares[0:1, here] = jnp.sum(query * query, axis=0, keepdims=True)
            squares[1:2, here] = jnp.sum(key * key, axis=0, keepdims=True)


def heads_in(order, weight, rows, blocks):
    width = blocks[0].shape[1]
    count = len(blocks) * rows
    return pl.pallas_call(
        functools.partial(heads_kernel, rows),
        in_specs=[scalars, vectors] + [vectors] * len(blocks),
        out_specs=[vectors] * 5,
        out_shape=[
            jax.ShapeDtypeStruct((HEAD_DIM, count), jnp.float32),
            jax.ShapeDtypeStruct((HEAD_DIM, count), jnp.float32),
            jax.ShapeDtypeStruct((count, HEAD_DIM), jnp.bfloat16),
            jax.ShapeDtypeStruct((HEAD_DIM, count), jnp.bfloat16),
            jax.ShapeDtypeStruct((2, count), jnp.float32),
        ],
        cost_estimate=pl.CostEstimate(
            flops=2 * count * width * 3 * HEAD_DIM,
            bytes_accessed=2 * count * width,
            transcendentals=0,
        ),
        name="heads_in",
    )(order, weight, *blocks)


def out_kernel(rows, where, attended, resid, gain, *refs):
    *blocks, far_one, far_two, cross, middle, normed = refs
    count = len(blocks)
    half = HEAD_DIM // 2
    first_group = where[count] == 0
    total = resid[...].astype(jnp.float32)
    far_rows = [far_one[...], far_two[...], cross[: 4 * half], cross[4 * half :]]
    for index in range(0, count, 4):
        near_left, far_left = [], []
        for i in range(index, index + 4):
            columns = attended[where[i]].astype(jnp.float32)
            low, high = columns[:, :half], columns[:, half:]
            near_left.append(jnp.where(first_group, low, high))
            far_left.append(jnp.where(first_group, high, low))
        near = jnp.concatenate([blocks[i][rows:] for i in range(index, index + 4)], axis=0)
        total += mm(jnp.concatenate(near_left, axis=1).astype(jnp.bfloat16), near)
        total += mm(jnp.concatenate(far_left, axis=1).astype(jnp.bfloat16), far_rows[index // 4])
    middle[...] = total
    inverse = lax.rsqrt(jnp.mean(total * total, axis=-1, keepdims=True) + eps)
    normed[...] = (total * inverse * gain[...]).astype(normed.dtype)


def out_project(where, attended, resid, gain, rows, blocks, far):
    width = resid.shape[1]
    return pl.pallas_call(
        functools.partial(out_kernel, rows),
        in_specs=[scalars] + [vectors] * (3 + len(blocks) + len(far)),
        out_specs=[vectors] * 2,
        out_shape=[
            jax.ShapeDtypeStruct((rows, width), jnp.float32),
            jax.ShapeDtypeStruct((rows, width), jnp.bfloat16),
        ],
        cost_estimate=pl.CostEstimate(
            flops=2 * rows * width * width,
            bytes_accessed=2 * width * width,
            transcendentals=0,
        ),
        name="out_project",
    )(where, attended, resid, gain, *blocks, *far)


def out_back_kernel(rows, where, branch, *refs):
    *blocks, far_one, far_two, cross, out = refs
    count = len(blocks)
    half = HEAD_DIM // 2
    first_group = where[count] == 0
    far_rows = [far_one[...], far_two[...], cross[: 4 * half], cross[4 * half :]]
    for index in range(0, count, 4):
        near = jnp.concatenate([blocks[i][rows:] for i in range(index, index + 4)], axis=0)
        near = contract_cols(branch[...], near)
        far = contract_cols(branch[...], far_rows[index // 4])
        for i in range(index, index + 4):
            here = slice((i - index) * half, (i - index + 1) * half)
            low = jnp.where(first_group, near[:, here], far[:, here])
            high = jnp.where(first_group, far[:, here], near[:, here])
            out[where[i]] = jnp.concatenate([low, high], axis=1).astype(out.dtype)


def out_project_back(where, branch, rows, blocks, far):
    width = branch.shape[1]
    return pl.pallas_call(
        functools.partial(out_back_kernel, rows),
        in_specs=[scalars] + [vectors] * (1 + len(blocks) + len(far)),
        out_specs=vectors,
        out_shape=jax.ShapeDtypeStruct((len(blocks), rows, HEAD_DIM), jnp.bfloat16),
        cost_estimate=pl.CostEstimate(
            flops=2 * rows * width * width,
            bytes_accessed=2 * width * width,
            transcendentals=0,
        ),
        name="out_project_back",
    )(where, branch, *blocks, *far)


def turn(values, cosine, rope_sine):
    half = HEAD_DIM // 2
    first, second = values[:half], values[half:]
    return jnp.concatenate(
        [first * cosine - second * rope_sine, second * cosine + first * rope_sine], axis=0
    )


def attend_kernel(
    query_raw,
    key_raw,
    value_t,
    inverse,
    inverse_all,
    gains,
    cosine,
    rope_sine,
    cosine_all,
    rope_sine_all,
    key_seg,
    query_seg,
    query_t,
    query,
    key_t,
    key,
    out,
    out_t,
    log_total,
):
    @pl.when(pl.program_id(0) == 0)
    def _():
        turned = turn(
            key_raw[...] * inverse_all[1:2, :] * gains[:, 1:2], cosine_all[...], rope_sine_all[...]
        ).astype(jnp.bfloat16)
        key_t[...] = turned
        key[...] = turned.T

    turned = turn(
        query_raw[...] * inverse[0:1, :] * gains[:, 0:1], cosine[...], rope_sine[...]
    ).astype(jnp.bfloat16)
    query_t[...] = turned
    query[...] = turned.T
    scores = mm(key[...], turned) * score_scale
    scores = jnp.where(key_seg[:, :1] == query_seg[...], scores, negative)
    peak = jnp.max(scores, axis=0, keepdims=True)
    weights = jnp.exp(scores - peak)
    total = jnp.sum(weights, axis=0, keepdims=True)
    result = mm(value_t[...], weights.astype(jnp.bfloat16)) / total
    out_t[...] = result.astype(out_t.dtype)
    out[...] = result.T.astype(out.dtype)
    log_total[...] = peak + jnp.log(total)


def attend(query_raw, key_raw, value_t, inverse, gains, cosine, rope_sine, key_seg, query_seg):
    count = query_raw.shape[1]
    whole = lambda i: (0, 0)
    across = lambda rows: pl.BlockSpec((rows, query_block), lambda i: (0, i))
    down = pl.BlockSpec((query_block, HEAD_DIM), lambda i: (i, 0))
    all_of = lambda rows: pl.BlockSpec((rows, count), whole)
    low, half = jnp.bfloat16, HEAD_DIM // 2
    return pl.pallas_call(
        attend_kernel,
        grid=(count // query_block,),
        in_specs=[
            across(HEAD_DIM),
            all_of(HEAD_DIM),
            all_of(HEAD_DIM),
            across(2),
            all_of(2),
            pl.BlockSpec((HEAD_DIM, 2), whole),
            across(half),
            across(half),
            all_of(half),
            all_of(half),
            pl.BlockSpec((count, HEAD_DIM), whole),
            across(1),
        ],
        out_specs=[
            across(HEAD_DIM),
            down,
            all_of(HEAD_DIM),
            pl.BlockSpec((count, HEAD_DIM), whole),
            down,
            across(HEAD_DIM),
            across(1),
        ],
        out_shape=[
            jax.ShapeDtypeStruct((HEAD_DIM, count), low),
            jax.ShapeDtypeStruct((count, HEAD_DIM), low),
            jax.ShapeDtypeStruct((HEAD_DIM, count), low),
            jax.ShapeDtypeStruct((count, HEAD_DIM), low),
            jax.ShapeDtypeStruct((count, HEAD_DIM), low),
            jax.ShapeDtypeStruct((HEAD_DIM, count), low),
            jax.ShapeDtypeStruct((1, count), jnp.float32),
        ],
        cost_estimate=pl.CostEstimate(
            flops=4 * count * count * HEAD_DIM,
            bytes_accessed=count * HEAD_DIM * 24,
            transcendentals=count * count,
        ),
        name="attend",
    )(
        query_raw,
        key_raw,
        value_t,
        inverse,
        inverse,
        gains,
        cosine,
        rope_sine,
        cosine,
        rope_sine,
        key_seg,
        query_seg,
    )


def attend_back_kernel(
    key_seg,
    query_seg,
    log_total,
    query_t,
    query,
    upstream,
    key,
    key_t,
    value,
    query_raw,
    key_raw,
    inverse,
    inverse_all,
    gains,
    cosine,
    rope_sine,
    cosine_all,
    rope_sine_all,
    weighted_query,
    weighted_key,
    dvalue_t,
    inner_query,
    inner_key,
    gain_sums,
    dkey,
    dvalue,
):
    step = pl.program_id(0)

    @pl.when(step == 0)
    def _():
        dkey[...] = jnp.zeros_like(dkey)
        dvalue[...] = jnp.zeros_like(dvalue)
        gain_sums[...] = jnp.zeros_like(gain_sums)

    scores = mm(key[...], query_t[...]) * score_scale
    probs = jnp.where(key_seg[:, :1] == query_seg[...], jnp.exp(scores - log_total[...]), 0.0)
    dvalue[...] += mm(probs.astype(jnp.bfloat16), upstream[...])
    dprobs = contract_cols(value[...], upstream[...])
    delta = jnp.sum(probs * dprobs, axis=0, keepdims=True)
    dscores = (probs * (dprobs - delta)).astype(jnp.bfloat16)
    dkey[...] += mm(dscores, query[...])
    turned = turn(mm(key_t[...], dscores) * score_scale, cosine[...], -rope_sine[...])
    product = turned * (query_raw[...] * inverse[0:1, :])
    weighted_query[...] = turned * gains[:, 0:1]
    inner_query[...] = jnp.sum(product * gains[:, 0:1], axis=0, keepdims=True)
    gain_sums[:, 0:1] += jnp.sum(product, axis=1, keepdims=True)

    @pl.when(step == pl.num_programs(0) - 1)
    def _():
        turned = turn(dkey[...].T * score_scale, cosine_all[...], -rope_sine_all[...])
        product = turned * (key_raw[...] * inverse_all[1:2, :])
        weighted_key[...] = turned * gains[:, 1:2]
        inner_key[...] = jnp.sum(product * gains[:, 1:2], axis=0, keepdims=True)
        gain_sums[:, 1:2] = jnp.sum(product, axis=1, keepdims=True)
        dvalue_t[...] = dvalue[...].T.astype(dvalue_t.dtype)


def attend_back(
    key_seg,
    query_seg,
    log_total,
    query_t,
    query,
    upstream,
    key,
    key_t,
    value,
    query_raw,
    key_raw,
    inverse,
    gains,
    cosine,
    rope_sine,
):
    count = query.shape[0]
    whole = lambda i: (0, 0)
    across = lambda rows: pl.BlockSpec((rows, query_block), lambda i: (0, i))
    down = pl.BlockSpec((query_block, HEAD_DIM), lambda i: (i, 0))
    all_of = lambda rows: pl.BlockSpec((rows, count), whole)
    tall = pl.BlockSpec((count, HEAD_DIM), whole)
    half = HEAD_DIM // 2
    return pl.pallas_call(
        attend_back_kernel,
        grid=(count // query_block,),
        in_specs=[
            tall,
            across(1),
            across(1),
            across(HEAD_DIM),
            down,
            down,
            tall,
            all_of(HEAD_DIM),
            tall,
            across(HEAD_DIM),
            all_of(HEAD_DIM),
            across(2),
            all_of(2),
            pl.BlockSpec((HEAD_DIM, 2), whole),
            across(half),
            across(half),
            all_of(half),
            all_of(half),
        ],
        out_specs=[
            across(HEAD_DIM),
            all_of(HEAD_DIM),
            all_of(HEAD_DIM),
            across(1),
            all_of(1),
            pl.BlockSpec((HEAD_DIM, 2), whole),
        ],
        out_shape=[
            jax.ShapeDtypeStruct((HEAD_DIM, count), jnp.float32),
            jax.ShapeDtypeStruct((HEAD_DIM, count), jnp.float32),
            jax.ShapeDtypeStruct((HEAD_DIM, count), jnp.bfloat16),
            jax.ShapeDtypeStruct((1, count), jnp.float32),
            jax.ShapeDtypeStruct((1, count), jnp.float32),
            jax.ShapeDtypeStruct((HEAD_DIM, 2), jnp.float32),
        ],
        scratch_shapes=[
            pltpu.VMEM((count, HEAD_DIM), jnp.float32),
            pltpu.VMEM((count, HEAD_DIM), jnp.float32),
        ],
        cost_estimate=pl.CostEstimate(
            flops=10 * count * count * HEAD_DIM,
            bytes_accessed=count * HEAD_DIM * 40,
            transcendentals=count * count,
        ),
        name="attend_back",
    )(
        key_seg,
        query_seg,
        log_total,
        query_t,
        query,
        upstream,
        key,
        key_t,
        value,
        query_raw,
        key_raw,
        inverse,
        inverse,
        gains,
        cosine,
        rope_sine,
        cosine,
        rope_sine,
    )


def local(
    tokens,
    segments,
    routes,
    route_gates,
    attn_gain,
    query_gain,
    key_gain,
    ffn_gain,
    w_query,
    w_key,
    w_value,
    w_out,
    w_gate,
    w_up,
    w_down,
    cotangent,
):
    row_count, width = tokens.shape
    top_count = routes.shape[1]
    devices = lax.axis_size("expert")
    groups = lax.axis_size("dp")
    me = lax.axis_index("expert")
    my_group = lax.axis_index("dp")
    seq_length = row_count * devices
    part = width // devices
    sharing = HEAD_DIM // part
    head = me // sharing
    sub = me % sharing
    w_rows = w_query.shape[0]
    w_half = w_rows // 2

    grouped = devices == 16 and groups == 2
    order = arrival_order(me) if grouped else jnp.arange(devices, dtype=jnp.int32)
    where = jnp.concatenate([order, my_group[None].astype(jnp.int32)])

    def gather(block):
        return Rounds(gather_rounds(block) if grouped else gather_whole(block))

    def scatter(make):
        return Rounds((scatter_rounds if grouped else scatter_whole)(make, seq_length))

    def exchange(values):
        return lax.all_to_all(values, "expert", split_axis=0, concat_axis=0, tiled=True)

    def to_heads(rows):
        blocks = rows.reshape(rows.shape[0], HEADS, HEAD_DIM).transpose(1, 0, 2)
        return jnp.repeat(blocks, sharing, axis=0)

    def my_part(columns, axis):
        if sharing == 1:
            return columns
        return lax.dynamic_slice_in_dim(columns, sub * part, part, axis=axis)

    def by_half(values, axis):
        return jnp.where(my_group == 0, values, jnp.flip(values, axis))

    def dp_start(values):
        return swap(values, "dp", 1) if groups == 2 else lax.psum(values, "dp")

    def dp_end(values, arrived):
        total = arrived.astype(jnp.float32)
        return total + values.astype(jnp.float32) if groups == 2 else total

    waiting = []

    def weight_grad(left, right):
        pieces = 4 if grouped else 1
        step = left.shape[1] // pieces
        own = [
            contract_rows(left[:, i * step : (i + 1) * step], right).astype(jnp.bfloat16)
            for i in range(pieces)
        ]
        far = [dp_start(values) for values in own]
        waiting.extend((far, i) for i in range(pieces))
        return own, far

    def weight_total(own, far):
        return (merge(own, far) if groups == 2 else far[0].astype(jnp.float32))[None]

    def cross(*others):
        if not (waiting and grouped):
            return others
        far, i = waiting.pop(0)
        *others, far[i] = together(*others, far[i])
        return others

    def ride(rounds, *others):
        if not (waiting and grouped):
            return rounds.step(*others)
        far, i = waiting.pop(0)
        *others, far[i] = rounds.step(*others, far[i])
        return others

    resid_in = tokens.astype(jnp.float32)
    pre_in, normal_in, inverse_in = norm_rows(resid_in, attn_gain)
    normed_in = pre_in.astype(jnp.bfloat16)

    experts_all = devices * w_gate.shape[0]
    slots = min(row_count, row_count * top_count * 3 // (2 * experts_all))
    hits = routes[:, :, None] == jnp.arange(experts_all, dtype=jnp.int32)[None, None, :]
    gate_table = jnp.sum(jnp.where(hits, route_gates[:, :, None], 0.0), axis=1).T
    gate_high = lax.reduce_precision(gate_table, exponent_bits=8, mantissa_bits=7)
    gate_rows = jnp.pad(
        jnp.stack([gate_high, gate_table - gate_high], axis=1).astype(jnp.bfloat16),
        ((0, 0), (0, 14), (0, 3 * HEAD_DIM - row_count)),
    )
    if grouped:
        take = lambda w: lax.dynamic_slice_in_dim(w, my_group * w_half, w_half)
    else:
        take = lambda w: w
    sent_w = jnp.concatenate([to_heads(take(w)) for w in (w_query, w_key, w_value)], axis=2)
    taken = sent_w.shape[1]
    arrived = exchange(jnp.concatenate([sent_w, gate_rows], axis=1))

    if grouped:
        rounds = gather(jnp.concatenate([normed_in, take(w_out)], axis=0))
        rounds.step()
        rounds.step()
        (arrived,) = rounds.step(arrived)
        head_w = arrived[:, :taken]
        head_w_far = swap(head_w, "dp", 1)
        (head_w_far,) = rounds.step(head_w_far)
        blocks = rounds.finish()
        head_w = by_half(jnp.stack([head_w, head_w_far], axis=1), 1).reshape(width, 3 * HEAD_DIM)
        out_far = [
            swap(jnp.concatenate([block[row_count:] for block in some], axis=0), "dp", 1)
            for some in (blocks[:4], blocks[4:8])
        ]
    else:
        blocks = gather(normed_in).finish()
        head_w = arrived[:, :taken].reshape(width, 3 * HEAD_DIM)
        out_full = lax.all_gather(w_out, "expert", axis=0, tiled=True)

    gate_pair = arrived[:, taken : taken + 2, :row_count].astype(jnp.float32)
    gate_mine = (gate_pair[:, 0] + gate_pair[:, 1])[order]
    chosen = gate_mine > 0.0
    before = jnp.arange(row_count)[:, None] < jnp.arange(row_count)[None, :]
    rank = mm(chosen.astype(jnp.bfloat16), before.astype(jnp.bfloat16)).astype(jnp.int32)
    rank = jnp.where(chosen, rank, -1)
    slot = jnp.arange(slots, dtype=jnp.int32)
    picks = rank[:, None, :] == slot[None, :, None]
    slot_gate = jnp.sum(jnp.where(picks, gate_mine[:, None, :], 0.0), axis=2).reshape(-1, 1)
    picks = picks.astype(jnp.bfloat16)
    unpicks = (rank[:, :, None] == slot[None, None, :]).astype(jnp.bfloat16)
    ones = jnp.ones_like(slot_gate)

    key_seg = jnp.broadcast_to(segments[:, None], (seq_length, HEAD_DIM))
    query_seg = segments[None, :]
    cosine, rope_sine = rope_tables(jnp.arange(seq_length, dtype=jnp.int32))
    gains = jnp.stack(
        [
            lax.dynamic_slice_in_dim(query_gain, head * HEAD_DIM, HEAD_DIM),
            lax.dynamic_slice_in_dim(key_gain, head * HEAD_DIM, HEAD_DIM),
        ],
        axis=1,
    )

    cot_rounds = gather(cotangent)
    query_raw, key_raw, value, value_t, squares = heads_in(order, head_w, row_count, blocks)
    if sharing > 1:
        squares = jnp.stack(
            [jnp.sum(jnp.square(my_part(raw, 0)), axis=0) for raw in (query_raw, key_raw)]
        )
    (squares,) = cot_rounds.step(squares)
    squares = butterfly(squares, "expert")
    if grouped:
        squares, out_far[0] = cot_rounds.step(squares, out_far[0])
    inverse = lax.rsqrt(squares / width + eps)
    query_t, query, key_t, key, attended, attended_t, log_total = attend(
        query_raw, key_raw, value_t, inverse, gains, cosine, rope_sine, key_seg, query_seg
    )
    if grouped:
        attended, out_far[1] = cot_rounds.step(attended, out_far[1])
        out_cross = send(jnp.concatenate(out_far, axis=0), swap_core)

    attended_low = exchange(my_part(attended, 1).reshape(devices, row_count, part))
    (attended_low,) = cot_rounds.step(attended_low)
    if grouped:
        out_far.append(out_cross)
        middle, normed_mid = out_project(
            where, attended_low, tokens, ffn_gain[None, :], row_count, blocks, out_far
        )
    else:
        attended_low = attended_low.transpose(1, 0, 2).reshape(row_count, width)
        middle = resid_in + mm(attended_low, out_full)
        normed_mid = norm_rows(middle, ffn_gain)[0].astype(jnp.bfloat16)
    (normed_mid,) = cot_rounds.step(normed_mid)
    cot_blocks = cot_rounds.finish()

    mid_rounds = gather(normed_mid)
    grad_eo = pick(picks, slot_gate, cot_blocks)
    (grad_eo,) = mid_rounds.step(grad_eo)
    rows_in = pick(picks, ones, mid_rounds.finish())
    gate_in = mm(rows_in, w_gate[0])
    up_in = mm(rows_in, w_up[0])
    sigmoid_in = jax.nn.sigmoid(gate_in)
    silu_in = gate_in * sigmoid_in
    hidden = (silu_in * up_in).astype(jnp.bfloat16)
    grad_down, down_far = weight_grad(hidden, grad_eo)

    def give_back(rows):
        blocks = rows.reshape(devices, slots, width)

        def some(first, count):
            here = slice(first // row_count, (first + count) // row_count)
            return jnp.einsum(
                "bts,bsd->btd",
                unpicks[here],
                blocks[here],
                preferred_element_type=jnp.bfloat16,
            ).reshape(count, width)

        return some

    hidden_next, grad_eo_next = together(hidden, grad_eo, *grad_down)[:2]
    expert_out = (mm(hidden_next, w_down[0]) * slot_gate).astype(jnp.bfloat16)
    out_rounds = scatter(give_back(expert_out))
    grad_hidden = contract_cols(grad_eo_next, w_down[0])
    grad_up_pre = (grad_hidden * silu_in).astype(jnp.bfloat16)
    grad_gate_pre = (
        grad_hidden * up_in * sigmoid_in * (1.0 + gate_in * (1.0 - sigmoid_in))
    ).astype(jnp.bfloat16)
    grad_up_pre, grad_gate_pre = ride(out_rounds, grad_up_pre, grad_gate_pre)
    grad_rows = contract_cols(grad_gate_pre, w_gate[0])
    (grad_rows,) = out_rounds.step(grad_rows)
    grad_rows = (grad_rows + contract_cols(grad_up_pre, w_up[0])).astype(jnp.bfloat16)
    (grad_rows,) = ride(out_rounds, grad_rows)
    row_rounds = scatter(give_back(grad_rows))
    out_rounds.step()
    row_rounds.step()
    out_rounds.step()
    mixed = out_rounds.finish()
    activations = (middle + mixed).astype(jnp.bfloat16)

    grad_gate, gate_far = weight_grad(rows_in, grad_gate_pre)
    ride(row_rounds)
    row_rounds.step(*grad_gate)
    grad_up, up_far = weight_grad(rows_in, grad_up_pre)
    ride(row_rounds)
    row_rounds.step(*grad_up)
    grad_normed_mid = row_rounds.finish()

    grad_out = cotangent.astype(jnp.float32)
    _, normal_mid, inverse_mid = norm_rows(middle, ffn_gain)
    mid_back, grad_ffn_gain = norm_back(grad_normed_mid, normal_mid, inverse_mid, ffn_gain)
    grad_middle = grad_out + mid_back
    grad_branch = grad_middle.astype(jnp.bfloat16)
    (grad_branch,) = cross(grad_branch)
    if grouped:
        grad_columns = out_project_back(where, grad_branch, row_count, blocks, out_far)
    else:
        grad_columns = to_heads(contract_cols(grad_branch, out_full).astype(jnp.bfloat16))
    grad_attended = exchange(grad_columns).reshape(seq_length, HEAD_DIM)
    (grad_attended,) = cross(grad_attended)

    branch_rounds = gather(after(grad_branch, grad_attended))
    weighted_query, weighted_key, grad_value_t, inner_query, inner_key, gain_sums = attend_back(
        key_seg,
        query_seg,
        log_total,
        query_t,
        query,
        grad_attended,
        key,
        key_t,
        value,
        query_raw,
        key_raw,
        inverse,
        gains,
        cosine,
        rope_sine,
    )
    inner = jnp.concatenate([inner_query, inner_key], axis=0)
    if sharing > 1:
        inner = jnp.stack(
            [
                jnp.sum(my_part(weighted * raw * at, 0), axis=0)
                for weighted, raw, at in (
                    (weighted_query, query_raw, inverse[0:1]),
                    (weighted_key, key_raw, inverse[1:2]),
                )
            ]
        )
    (inner,) = ride(branch_rounds, inner)
    inner = butterfly(inner, "expert") / width
    (inner,) = branch_rounds.step(inner)
    grad_raw_t = jnp.concatenate(
        [
            my_part(
                (at * (weighted - raw * at * mean)).astype(jnp.bfloat16),
                0,
            )
            for weighted, raw, at, mean in (
                (weighted_query, query_raw, inverse[0:1], inner[0:1]),
                (weighted_key, key_raw, inverse[1:2], inner[1:2]),
            )
        ]
        + [my_part(grad_value_t, 0)],
        axis=0,
    )
    head_w_t = jnp.concatenate(
        [my_part(head_w[:, i * HEAD_DIM : (i + 1) * HEAD_DIM], 1).T for i in range(3)], axis=0
    )
    grad_w_t = stack_product(order, grad_raw_t, row_count, blocks)
    grad_attn_gain = jnp.sum(grad_w_t * head_w_t.astype(jnp.float32), axis=0) / attn_gain
    w_columns = exchange(
        grad_w_t.astype(jnp.bfloat16).reshape(3 * part, devices, w_rows).transpose(1, 0, 2)
    )
    (grad_raw_t,) = ride(branch_rounds, grad_raw_t)
    in_rounds = scatter(
        lambda first, count: project(order, grad_raw_t, head_w_t, row_count, first, count)
    )
    (w_columns,) = branch_rounds.step(w_columns)
    ride(in_rounds, *branch_rounds.sent)
    dense = [
        w_columns[:, i * part : (i + 1) * part].reshape(width, w_rows).T for i in range(3)
    ]
    branch_blocks = branch_rounds.finish()
    out_part = stack_product(
        order, my_part(attended_t, 0), row_count, branch_blocks
    ).astype(jnp.bfloat16)
    in_rounds.step()
    ride(in_rounds)
    out_part, *dense = in_rounds.step(out_part, *dense)
    dense_far = [dp_start(values) for values in dense]
    out_part_far = dp_start(out_part)
    ride(in_rounds)
    grad_normed_in = in_rounds.finish()
    in_back, _ = norm_back(grad_normed_in, normal_in, inverse_in, attn_gain)
    input_grad = (grad_middle + in_back).astype(jnp.bfloat16)

    def placed(values):
        return lax.dynamic_update_slice_in_dim(
            jnp.zeros((width,), jnp.float32), values, me * part, 0
        )

    gain_total = butterfly(
        butterfly(
            jnp.stack(
                [
                    grad_attn_gain,
                    placed(my_part(gain_sums[:, 0], 0)),
                    placed(my_part(gain_sums[:, 1], 0)),
                    grad_ffn_gain,
                ]
            ),
            "expert",
        ),
        "dp",
    )
    return (
        activations,
        input_grad,
        gain_total[0],
        gain_total[1],
        gain_total[2],
        gain_total[3],
        dp_end(dense[0], dense_far[0]),
        dp_end(dense[1], dense_far[1]),
        dp_end(dense[2], dense_far[2]),
        dp_end(out_part, out_part_far),
        weight_total(grad_gate, gate_far),
        weight_total(grad_up, up_far),
        weight_total(grad_down, down_far),
    )


def solution(mesh):
    in_specs = (
        P(("dp", "expert"), None),
        P("dp"),
        P(("dp", "expert"), None),
        P(("dp", "expert"), None),
        P(),
        P(),
        P(),
        P(),
        P("expert", None),
        P("expert", None),
        P("expert", None),
        P("expert", None),
        P("expert", None, None),
        P("expert", None, None),
        P("expert", None, None),
        P(("dp", "expert"), None),
    )
    out_specs = (
        P(("dp", "expert"), None),
        P(("dp", "expert"), None),
        P(),
        P(),
        P(),
        P(),
        P("expert", None),
        P("expert", None),
        P("expert", None),
        P("expert", None),
        P("expert", None, None),
        P("expert", None, None),
        P("expert", None, None),
    )
    return jax.shard_map(local, mesh=mesh, in_specs=in_specs, out_specs=out_specs, check_vma=False)
```

time: 995 us -> 862 us (0.87)
  waiting for transfers between devices: 546 us -> 334 us
  starting transfers between devices: 32.7 us -> 170 us
  Pallas kernels: 32.4 us -> 134 us
  blocking collectives: 97.5 us -> 0 us
  matrix products: 161 us -> 106 us
  between operations: 15.3 us -> 3.08 us
    all_gather x5 -> x0, waiting for transfers between devices: 199 us -> none  [gather(): return lax.all_gather(values, 'expert', axis=0, tiled=True)]
    ppermute x0 -> x99, waiting for transfers between devices: none -> 178 us  [send(): return lax.ppermute(values, 'expert', pairs)]
    ppermute x0 -> x99, starting transfers between devices: none -> 117 us  [send(): return lax.ppermute(values, 'expert', pairs)]
    ppermute x17 -> x32, waiting for transfers between devices: 243 us -> 139 us  [swap(): return lax.ppermute(values, axis, [(i, i ^ step) for i in range(count)])]
    reduce_scatter x3 -> x0, waiting for transfers between devices: 103 us -> none  [scatter(): return lax.psum_scatter(rows, 'expert', scatter_dimension=0, tiled=True)]
    pallas_call x1 -> x13, Pallas kernels: 12.7 us -> 112 us  [the longest x3 21.5 us: merge(): pl.pallas_call(merge_kernel, grid=(len(own),), in_specs=[pl.BlockSpec((ro...]
    all_to_all x3 -> x0, blocking collectives: 97.5 us -> none  [exchange(): lax.all_to_all(values, 'expert', split_axis=0, concat_axis=0, tiled=True)]
    broadcast_in_dim x3 -> x0, other arithmetic: 27.6 us -> none  [the longest x1 9.83 us: local(): dp_total(contract_rows(rows_in, grad_gate_pre).astype(jnp.bfloat16))[None]]
  transfers between devices with their start and end apart: 27 -> 135, of which waited for: 18 -> 49; matrix products, arithmetic and copies ran while one was open for 18% -> 17% of each run, Pallas kernels for 3% -> 13%
where the time goes in v2:
time: 862 us; the launch traced here: 853 us
  waiting for transfers between devices  334 us (39%)
  starting transfers between devices  170 us (20%)
  Pallas kernels  134 us (16%)
  matrix products  106 us (12%)
  other arithmetic  64 us (7%)
  local copies, waits for them, and re-layouts  42.3 us (5%)
    ppermute x99, waiting for transfers between devices, send(): return lax.ppermute(values, 'expert', pairs)  178 us
    ppermute x32, waiting for transfers between devices, swap(): return lax.ppermute(values, axis, [(i, i ^ step) for i in range(count)])  139 us
    ppermute x99, starting transfers between devices, send(): return lax.ppermute(values, 'expert', pairs)  117 us
    dot_general x3, matrix products, contract_cols(): lax.dot_general(left, right, (((1,), (1,)), ((), ())), preferred_element_...  36.5 us
    ppermute x32, starting transfers between devices, swap(): return lax.ppermute(values, axis, [(i, i ^ step) for i in range(count)])  32.2 us
    dot_general x12, matrix products, contract_rows(): lax.dot_general(left, right, (((0,), (0,)), ((), ())), preferred_element_...  31 us
    dot_general x4, matrix products, mm(): return jnp.dot(left, right, preferred_element_type=jnp.float32)  27 us
    pallas_call x1, Pallas kernels, attend_back(): pl.pallas_call(attend_back_kernel, grid=(count // query_block,), in_specs...  22 us
  transfers between devices with their start and end apart: 135, of which 49 were waited for; matrix products, arithmetic and copies ran while one was open for 17% of the time, Pallas kernels for 13%

profile of v2, /device:TPU:0, one launch (start us, length us, event | category | flops | bytes accessed | tf_op | source)
XLA Modules:
  0.0 852.8 jit_solution(13682046077779409521)
XLA Ops:
  10.0 14.2 %collective-permute-done.3.refs_1_ = bf16[192,2048]{1,0:T(8,128)(2,1)S(1)} collective-permute-done((bf16[192,2048]{1,0:T(8,128)(2,1)S(1)}, bf16[192,2048]{1,0:T(8,128)(2,1)S(1)}, u32[]{:S(2)}, u32[]{:S(2)}) %collective-permute-start.3) | collective-permute-done | bytes 786464 | tf_op jit(solution)/shard_map/ppermute | solution.py:98
  48.5 12.4 %collective-permute-done.7 = bf16[192,2048]{1,0:T(8,128)(2,1)} collective-permute-done((bf16[192,2048]{1,0:T(8,128)(2,1)}, bf16[192,2048]{1,0:T(8,128)(2,1)}, u32[]{:S(2)}, u32[]{:S(2)}) %collective-permute-start.7) | collective-permute-done | bytes 786464 | tf_op jit(solution)/shard_map/ppermute | solution.py:98
  65.4 12.8 %collective-permute-done.11.refs_6_ = bf16[192,2048]{1,0:T(8,128)(2,1)} collective-permute-done((bf16[192,2048]{1,0:T(8,128)(2,1)S(1)}, bf16[192,2048]{1,0:T(8,128)(2,1)}, u32[]{:S(2)}, u32[]{:S(2)}) %collective-permute-start.11) | collective-permute-done | bytes 786464 | tf_op jit(solution)/shard_map/ppermute | solution.py:98
  91.5 12.8 %collective-permute-done.19 = bf16[16,64,384]{2,1,0:T(8,128)(2,1)} collective-permute-done((bf16[16,64,384]{2,1,0:T(8,128)(2,1)}, bf16[16,64,384]{2,1,0:T(8,128)(2,1)}, u32[]{:S(2)}, u32[]{:S(2)}) %collective-permute-start.19) | collective-permute-done | bytes 786464 | tf_op jit(solution)/shard_map/ppermute | solution.py:58
  112.2 11.3 %heads_in.1 = (f32[128,2048]{1,0:T(8,128)}, f32[128,2048]{1,0:T(8,128)}, bf16[2048,128]{1,0:T(8,128)(2,1)}, bf16[128,2048]{1,0:T(8,128)(2,1)}, f32[2,2048]{1,0:T(2,128)}) custom-call(s32[16]{0:T(128)} %pad_add_fusion.order, bf16[2048,384]{1,0:T(8,128)(2,1)} %bitcast.225, bf16[192,2048]{1,0:T(8,128)(2,1)} %copy-done.4, bf16[192,2048]{1,0:T(8,128)(2,1)} %copy-done.6, ...), custom_call_target="tpu_custom_call" | custom-call | flops 3221225472 | bytes 8388608 | tf_op jit(solution)/shard_map/heads_in/pallas_call | solution.py:376
  156.7 14.7 %attend.1 = (bf16[128,2048]{1,0:T(8,128)(2,1)}, bf16[2048,128]{1,0:T(8,128)(2,1)}, bf16[128,2048]{1,0:T(8,128)(2,1)}, bf16[2048,128]{1,0:T(8,128)(2,1)}, bf16[20...) custom-call(f32[128,2048]{1,0:T(8,128)} %get-tuple-element.189.query_raw, ...), custom_call_target="tpu_custom_call" | custom-call | flops 2147483648 | bytes 6291456 | tf_op jit(solution)/shard_map/attend/pallas_call | solution.py:530
  186.0 14.3 %collective-permute-done.35.refs_7_ = bf16[128,2048]{1,0:T(8,128)(2,1)} collective-permute-done((bf16[128,2048]{1,0:T(8,128)(2,1)S(1)}, bf16[128,2048]{1,0:T(8,128)(2,1)}, u32[]{:S(2)}, u32[]{:S(2)}) %collective-permute-start.35) | collective-permute-done | bytes 524320 | tf_op jit(solution)/shard_map/ppermute | solution.py:98
  229.6 14.8 %collective-permute-done.46 = bf16[128,2048]{1,0:T(8,128)(2,1)S(1)} collective-permute-done((bf16[128,2048]{1,0:T(8,128)(2,1)S(1)}, bf16[128,2048]{1,0:T(8,128)(2,1)S(1)}, u32[]{:S(2)}, u32[]{:S(2)}) %collective-permute-start.46) | collective-permute-done | bytes 524320 | tf_op jit(solution)/shard_map/ppermute | solution.py:98
  261.4 10.8 %collective-permute-done.53.refs_7_ = bf16[128,2048]{1,0:T(8,128)(2,1)} collective-permute-done((bf16[128,2048]{1,0:T(8,128)(2,1)S(1)}, bf16[128,2048]{1,0:T(8,128)(2,1)}, u32[]{:S(2)}, u32[]{:S(2)}) %collective-permute-start.53) | collective-permute-done | bytes 524320 | tf_op jit(solution)/shard_map/ppermute | solution.py:98
  285.4 10.6 %fusion.10 = f32[1536,1024]{1,0:T(8,128)S(1)} fusion(bf16[1536,2048]{1,0:T(8,128)(2,1)} %pick.3, bf16[1,2048,1024]{2,1,0:T(8,128)(2,1)} %param.29), kind=kOutput, calls=%fused_computation.17 | convolution fusion | flops 6442450944 | bytes 16777216 | tf_op jit(solution)/shard_map/dot_general | solution.py:41
  329.7 14.4 %multiply_convert_fusion.1 = (bf16[1536,1024]{1,0:T(8,128)(2,1)}, bf16[1536,1024]{1,0:T(8,128)(2,1)}) fusion(f32[1536,1024]{1,0:T(8,128)} %copy-done.92, f32[1536,1024]{1,0:T(8,128)} %get-tuple-element.381, bf16[1536,2048]{1,0:T(8,128)(2,1)S(1)} %bitcast.224, bf16[1,1024,2048]{2,1,0:T(8,128)(2,1)} %param.31), kind=kOutput, calls=%fused_computation.3 | convolution fusion | flops 6462898176 | bytes 29360128 | tf_op jit(solution)/shard_map/dot_general | solution.py:51
  354.0 9.9 %fusion.8 = f32[1536,2048]{1,0:T(8,128)S(1)} fusion(bf16[1536,1024]{1,0:T(8,128)(2,1)} %get-tuple-element.233, bf16[1,2048,1024]{2,1,0:T(8,128)(2,1)} %param.29), kind=kOutput, calls=%fused_computation.15 | convolution fusion | flops 6442450944 | bytes 19922944 | tf_op jit(solution)/shard_map/dot_general | solution.py:51
  364.4 12.2 %fusion.4 = f32[1536,2048]{1,0:T(8,128)} fusion(bf16[1536,1024]{1,0:T(8,128)(2,1)} %get-tuple-element.236, bf16[1,2048,1024]{2,1,0:T(8,128)(2,1)} %param.30), kind=kOutput, calls=%fused_computation.11 | convolution fusion | flops 6442450944 | bytes 19922944 | tf_op jit(solution)/shard_map/dot_general | solution.py:51
  493.6 16.3 %collective-permute-done.83.refs_4_ = bf16[512,1024]{1,0:T(8,128)(2,1)S(1)} collective-permute-done((bf16[512,1024]{1,0:T(8,128)(2,1)S(1)}, bf16[512,1024]{1,0:T(8,128)(2,1)S(1)}, u32[]{:S(2)}, u32[]{:S(2)}) %collective-permute-start.83) | collective-permute-done | bytes 1048608 | tf_op jit(solution)/shard_map/ppermute | solution.py:58
  526.2 12.9 %all-to-all-done.2 = bf16[16,128,128]{2,1,0:T(8,128)(2,1)S(1)} async-done(((bf16[16,128,128]{2,1,0:T(8,128)(2,1)}), bf16[16,128,128]{2,1,0:T(8,128)(2,1)S(1)}, u32[]{:S(2)}, u32[]{:S(2)}) %all-to-all-start.2) | async-done | bytes 524320 | tf_op jit(solution)/shard_map/all_to_all | solution.py:784
  543.0 22.0 %attend_back.1 = (f32[128,2048]{1,0:T(8,128)}, f32[128,2048]{1,0:T(8,128)}, bf16[128,2048]{1,0:T(8,128)(2,1)}, f32[1,2048]{1,0:T(1,128)}, f32[1,2048]{1,0:T(1,128)}, /*index=5*/f32[128,2]{1,0:T(8,128)}) custom-call(s32[2048,128]{1,0:T(8,128)} %broadcast_in_dim.47.key_seg, s32[1,2048]{1,0:T(1,128)} %bitcast.269, f32[1,2048]{1,0:T(1,128)} %get-tuple-element.258.log_total, ...), custom_call_target="tpu_custom_call" | custom-call | flops 5368709120 | bytes 10485760 | tf_op jit(solution)/shard_map/attend_back/pallas_call | solution.py:670
  583.3 10.1 %collective-permute-done.96 = f32[2,2048]{1,0:T(2,128)S(1)} collective-permute-done((f32[2,2048]{1,0:T(2,128)S(1)}, f32[2,2048]{1,0:T(2,128)S(1)}, u32[]{:S(2)}, u32[]{:S(2)}) %collective-permute-start.96) | collective-permute-done | bytes 16416 | tf_op jit(solution)/shard_map/ppermute | solution.py:58
  600.1 17.5 %collective-permute-done.101.refs_7_ = bf16[512,1024]{1,0:T(8,128)(2,1)S(1)} collective-permute-done((bf16[512,1024]{1,0:T(8,128)(2,1)S(1)}, bf16[512,1024]{1,0:T(8,128)(2,1)S(1)}, u32[]{:S(2)}, u32[]{:S(2)}) %collective-permute-start.101) | collective-permute-done | bytes 1048608 | tf_op jit(solution)/shard_map/ppermute | solution.py:58
  626.5 10.2 %stack_product.2 = f32[384,2048]{1,0:T(8,128)} custom-call(s32[16]{0:T(128)} %pad_add_fusion.order, bf16[384,2048]{1,0:T(8,128)(2,1)} %pad_maximum_fusion.2.left_t.left_next_t, bf16[192,2048]{1,0:T(8,128)(2,1)} %copy-done.4, bf16[192,2048]{1,0:T(8,128)(2,1)} %copy-done.6, bf16[192,2048]{1,0:T(8,128)(2,1)} %copy-done.2, bf16[192,2048]{1,0:T(8,128)(2,1)} %copy-done.3, ...), custom_call_target="tpu_custom_call" | custom-call | flops 3221225472 | bytes 8388608 | tf_op jit(solution)/shard_map/stack_product/pallas_call | solution.py:341
  650.9 22.2 %collective-permute-done.103.refs_7_ = bf16[128,2048]{1,0:T(8,128)(2,1)S(1)} collective-permute-done((bf16[128,2048]{1,0:T(8,128)(2,1)S(1)}, bf16[128,2048]{1,0:T(8,128)(2,1)S(1)}, u32[]{:S(2)}, u32[]{:S(2)}) %collective-permute-start.103) | collective-permute-done | bytes 524320 | tf_op jit(solution)/shard_map/ppermute | solution.py:98
  691.3 11.0 %collective-permute-done.112 = bf16[128,2048]{1,0:T(8,128)(2,1)S(1)} collective-permute-done((bf16[128,2048]{1,0:T(8,128)(2,1)S(1)}, bf16[128,2048]{1,0:T(8,128)(2,1)S(1)}, u32[]{:S(2)}, u32[]{:S(2)}) %collective-permute-start.112) | collective-permute-done | bytes 524320 | tf_op jit(solution)/shard_map/ppermute | solution.py:98
  714.2 10.0 %collective-permute-done.123 = f32[4,2048]{1,0:T(4,128)S(1)} collective-permute-done((f32[4,2048]{1,0:T(4,128)S(1)}, f32[4,2048]{1,0:T(4,128)S(1)}, u32[]{:S(2)}, u32[]{:S(2)}) %collective-permute-start.123) | collective-permute-done | bytes 32800 | tf_op jit(solution)/shard_map/ppermute | solution.py:58
  780.0 9.9 %collective-permute-done.129 = bf16[128,2048]{1,0:T(8,128)(2,1)S(1)} collective-permute-done((bf16[128,2048]{1,0:T(8,128)(2,1)S(1)}, bf16[128,2048]{1,0:T(8,128)(2,1)S(1)}, u32[]{:S(2)}, u32[]{:S(2)}) %collective-permute-start.129) | collective-permute-done | bytes 524320 | tf_op jit(solution)/shard_map/ppermute | solution.py:58
  814.4 26.5 %collective-permute-done.126 = bf16[128,2048]{1,0:T(8,128)(2,1)S(1)} collective-permute-done((bf16[128,2048]{1,0:T(8,128)(2,1)S(1)}, bf16[128,2048]{1,0:T(8,128)(2,1)S(1)}, u32[]{:S(2)}, u32[]{:S(2)}) %collective-permute-start.126) | collective-permute-done | bytes 524320 | tf_op jit(solution)/shard_map/ppermute | solution.py:58
  (610 shorter events, 515.9 us)
Async XLA Ops:
  9.7 31.2 %collective-permute-start.9 = (bf16[192,2048]{1,0:T(8,128)(2,1)S(1)}, bf16[192,2048]{1,0:T(8,128)(2,1)}, u32[]{:S(2)}, u32[]{:S(2)}) collective-permute-start(bf16[192,2048]{1,0:T(8,128)(2,1)S(1)} %pad_maximum_fusion.7.refs_0_), channel_id=1, source_target_pairs={{0,1},{1,0},{2,3},{3,2},{4,5},{5,4},{6,7},{7,6},{8,9},{9,8},{10,11... | collective-permute-start | bytes 2359304 | tf_op jit(solution)/shard_map/ppermute | solution.py:98
  30.2 30.6 %collective-permute-start.7 = (bf16[192,2048]{1,0:T(8,128)(2,1)}, bf16[192,2048]{1,0:T(8,128)(2,1)}, u32[]{:S(2)}, u32[]{:S(2)}) collective-permute-start(bf16[192,2048]{1,0:T(8,128)(2,1)} %collective-permute-done.4), channel_id=1, source_target_pairs={{4,0},{5,1},{6,2},{7,3},{8,12},{9,13},{10,14},{11,15},{20,16},{21,... | collective-permute-start | bytes 2359304 | tf_op jit(solution)/shard_map/ppermute | solution.py:98
  32.9 32.5 %all-to-all-start = ((bf16[16,80,384]{2,1,0:T(8,128)(2,1)}), bf16[16,80,384]{2,1,0:T(8,128)(2,1)}, u32[]{:S(2)}, u32[]{:S(2)}) async-start(bf16[16,80,384]{2,1,0:T(8,128)(2,1)} %copy.81), calls=%async_computation | async-start | bytes 1966080 | tf_op jit(solution)/shard_map/all_to_all | solution.py:784
  64.5 26.9 %collective-permute-start.17 = (bf16[192,2048]{1,0:T(8,128)(2,1)}, bf16[192,2048]{1,0:T(8,128)(2,1)}, u32[]{:S(2)}, u32[]{:S(2)}) collective-permute-start(bf16[192,2048]{1,0:T(8,128)(2,1)} %collective-permute-done.8.refs_5_), channel_id=1, source_target_pairs={{0,1},{1,0},{2,3},{3,2},{4,5},{5,4},{6,7},{7,6},{8,9},{9,8},{10,11... | collective-permute-start | bytes 2359304 | tf_op jit(solution)/shard_map/ppermute | solution.py:98
  91.4 32.1 %collective-permute-start = (bf16[128,2048]{1,0:T(8,128)(2,1)S(1)}, bf16[128,2048]{1,0:T(8,128)(2,1)}, u32[]{:S(2)}, u32[]{:S(2)}) collective-permute-start(bf16[128,2048]{1,0:T(8,128)(2,1)S(1)} %copy-done.16), channel_id=1, source_target_pairs={{0,4},{1,5},{2,6},{3,7},{4,0},{5,1},{6,2},{7,3},{8,12},{9,13},{10,... | collective-permute-start | bytes 1572872 | tf_op jit(solution)/shard_map/ppermute | solution.py:98
  107.7 39.7 %collective-permute-start.24 = (bf16[128,2048]{1,0:T(8,128)(2,1)S(1)}, bf16[128,2048]{1,0:T(8,128)(2,1)}, u32[]{:S(2)}, u32[]{:S(2)}) collective-permute-start(bf16[128,2048]{1,0:T(8,128)(2,1)S(1)} %copy-done.16), channel_id=1, source_target_pairs={{0,1},{1,0},{2,3},{3,2},{4,5},{5,4},{6,7},{7,6},{8,9},{9,8},{10,11... | collective-permute-start | bytes 1572872 | tf_op jit(solution)/shard_map/ppermute | solution.py:98
  174.5 27.3 %collective-permute-start.40 = (bf16[512,2048]{1,0:T(8,128)(2,1)}, bf16[512,2048]{1,0:T(8,128)(2,1)}, u32[]{:S(2)}, u32[]{:S(2)}) collective-permute-start(bf16[512,2048]{1,0:T(8,128)(2,1)} %pad_maximum_fusion), channel_id=1, source_target_pairs={{0,1},{1,0},{2,3},{3,2},{4,5},{5,4},{6,7},{7,6},{8,9},{9,8},{10,11... | collective-permute-start | bytes 6291464 | tf_op jit(solution)/shard_map/ppermute | solution.py:98
  329.4 56.7 %collective-permute-start.65 = (bf16[256,2048]{1,0:T(8,128)(2,1)S(1)}, bf16[256,2048]{1,0:T(8,128)(2,1)}, u32[]{:S(2)}, u32[]{:S(2)}) collective-permute-start(bf16[256,2048]{1,0:T(8,128)(2,1)S(1)} %convolution_convert_fusion.2.refs_1_), channel_id=1, source_target_pairs={{0,16},{16,0},{1,17},{17,1},{2,18},{18,2},{3,19},{19,3},{4,20},{20... | collective-permute-start | bytes 3145736 | tf_op jit(solution)/shard_map/ppermute | solution.py:58
  396.4 27.8 %collective-permute-start.75 = (bf16[256,2048]{1,0:T(8,128)(2,1)S(1)}, bf16[256,2048]{1,0:T(8,128)(2,1)}, u32[]{:S(2)}, u32[]{:S(2)}) collective-permute-start(bf16[256,2048]{1,0:T(8,128)(2,1)S(1)} %copy-done.24), channel_id=1, source_target_pairs={{0,16},{16,0},{1,17},{17,1},{2,18},{18,2},{3,19},{19,3},{4,20},{20... | collective-permute-start | bytes 3145736 | tf_op jit(solution)/shard_map/ppermute | solution.py:58
  439.1 34.9 %collective-permute-start.69 = (bf16[128,2048]{1,0:T(8,128)(2,1)S(1)}, bf16[128,2048]{1,0:T(8,128)(2,1)S(1)}, u32[]{:S(2)}, u32[]{:S(2)}) collective-permute-start(bf16[128,2048]{1,0:T(8,128)(2,1)S(1)} %add_convert_fusion.24), channel_id=1, source_target_pairs={{4,8},{5,9},{6,10},{7,11},{8,4},{9,5},{10,6},{11,7},{20,24},{21,25... | collective-permute-start | bytes 1572872 | tf_op jit(solution)/shard_map/ppermute | solution.py:98
  484.1 42.1 %collective-permute-start.84 = (bf16[512,1024]{1,0:T(8,128)(2,1)}, bf16[512,1024]{1,0:T(8,128)(2,1)S(1)}, u32[]{:S(2)}, u32[]{:S(2)}) collective-permute-start(bf16[512,1024]{1,0:T(8,128)(2,1)} %convolution_convert_fusion.10.refs_1_), channel_id=1, source_target_pairs={{0,16},{16,0},{1,17},{17,1},{2,18},{18,2},{3,19},{19,3},{4,20},{20... | collective-permute-start | bytes 3145736 | tf_op jit(solution)/shard_map/ppermute | solution.py:58
  524.7 41.1 %collective-permute-start.88 = (bf16[512,1024]{1,0:T(8,128)(2,1)}, bf16[512,1024]{1,0:T(8,128)(2,1)}, u32[]{:S(2)}, u32[]{:S(2)}) collective-permute-start(bf16[512,1024]{1,0:T(8,128)(2,1)} %convolution_convert_fusion.9.refs_2_), channel_id=1, source_target_pairs={{0,16},{16,0},{1,17},{17,1},{2,18},{18,2},{3,19},{19,3},{4,20},{20... | collective-permute-start | bytes 3145736 | tf_op jit(solution)/shard_map/ppermute | solution.py:58
  626.5 59.4 %collective-permute-start.102 = (bf16[1024,2048]{1,0:T(8,128)(2,1)}, bf16[1024,2048]{1,0:T(8,128)(2,1)}, u32[]{:S(2)}, u32[]{:S(2)}) collective-permute-start(bf16[1024,2048]{1,0:T(8,128)(2,1)} %project.3), channel_id=1, source_target_pairs={{0,1},{1,0},{2,3},{3,2},{4,5},{5,4},{6,7},{7,6},{8,9},{9,8},{10,11... | collective-permute-start | bytes 12582920 | tf_op jit(solution)/shard_map/ppermute | solution.py:98
  641.8 36.4 %all-to-all-start.3 = ((bf16[16,384,128]{2,1,0:T(8,128)(2,1)}), bf16[16,384,128]{2,1,0:T(8,128)(2,1)S(1)}, u32[]{:S(2)}, u32[]{:S(2)}) async-start(bf16[16,384,128]{2,1,0:T(8,128)(2,1)} %bitcast.230), calls=%async_computation.3 | async-start | bytes 3145728 | tf_op jit(solution)/shard_map/all_to_all | solution.py:784
  650.4 35.4 %collective-permute-start.109 = (bf16[512,1024]{1,0:T(8,128)(2,1)}, bf16[512,1024]{1,0:T(8,128)(2,1)}, u32[]{:S(2)}, u32[]{:S(2)}) collective-permute-start(bf16[512,1024]{1,0:T(8,128)(2,1)} %convolution_convert_fusion.7.refs_0_), channel_id=1, source_target_pairs={{0,16},{16,0},{1,17},{17,1},{2,18},{18,2},{3,19},{19,3},{4,20},{20... | collective-permute-start | bytes 3145736 | tf_op jit(solution)/shard_map/ppermute | solution.py:58
  690.0 48.4 %collective-permute-start.114 = (bf16[512,1024]{1,0:T(8,128)(2,1)}, bf16[512,1024]{1,0:T(8,128)(2,1)}, u32[]{:S(2)}, u32[]{:S(2)}) collective-permute-start(bf16[512,1024]{1,0:T(8,128)(2,1)} %convolution_convert_fusion.6.refs_1_), channel_id=1, source_target_pairs={{0,16},{16,0},{1,17},{17,1},{2,18},{18,2},{3,19},{19,3},{4,20},{20... | collective-permute-start | bytes 3145736 | tf_op jit(solution)/shard_map/ppermute | solution.py:58
  705.1 33.3 %collective-permute-start.111 = (bf16[128,2048]{1,0:T(8,128)(2,1)}, bf16[128,2048]{1,0:T(8,128)(2,1)}, u32[]{:S(2)}, u32[]{:S(2)}) collective-permute-start(bf16[128,2048]{1,0:T(8,128)(2,1)} %get-tuple-element.331), channel_id=1, source_target_pairs={{0,2},{1,3},{2,0},{3,1},{4,6},{5,7},{6,4},{7,5},{8,10},{9,11},{10,... | collective-permute-start | bytes 1572872 | tf_op jit(solution)/shard_map/ppermute | solution.py:98
  706.9 31.6 %collective-permute-start.113 = (bf16[128,2048]{1,0:T(8,128)(2,1)S(1)}, bf16[128,2048]{1,0:T(8,128)(2,1)}, u32[]{:S(2)}, u32[]{:S(2)}) collective-permute-start(bf16[128,2048]{1,0:T(8,128)(2,1)S(1)} %get-tuple-element.330), channel_id=1, source_target_pairs={{0,4},{1,5},{2,6},{3,7},{12,8},{13,9},{14,10},{15,11},{16,20},{17,... | collective-permute-start | bytes 1572872 | tf_op jit(solution)/shard_map/ppermute | solution.py:98
  729.6 70.3 %collective-permute-start.120 = (bf16[512,1024]{1,0:T(8,128)(2,1)}, bf16[512,1024]{1,0:T(8,128)(2,1)}, u32[]{:S(2)}, u32[]{:S(2)}) collective-permute-start(bf16[512,1024]{1,0:T(8,128)(2,1)} %convolution_convert_fusion.5.refs_2_), channel_id=1, source_target_pairs={{0,16},{16,0},{1,17},{17,1},{2,18},{18,2},{3,19},{19,3},{4,20},{20... | collective-permute-start | bytes 3145736 | tf_op jit(solution)/shard_map/ppermute | solution.py:58
  740.4 32.4 %collective-permute-start.117 = (bf16[128,2048]{1,0:T(8,128)(2,1)}, bf16[128,2048]{1,0:T(8,128)(2,1)}, u32[]{:S(2)}, u32[]{:S(2)}) collective-permute-start(bf16[128,2048]{1,0:T(8,128)(2,1)} %add_convert_fusion.5), channel_id=1, source_target_pairs={{4,8},{5,9},{6,10},{7,11},{8,4},{9,5},{10,6},{11,7},{20,24},{21,25... | collective-permute-start | bytes 1572872 | tf_op jit(solution)/shard_map/ppermute | solution.py:98
  744.9 28.0 %collective-permute-start.115 = (bf16[128,2048]{1,0:T(8,128)(2,1)}, bf16[128,2048]{1,0:T(8,128)(2,1)}, u32[]{:S(2)}, u32[]{:S(2)}) collective-permute-start(bf16[128,2048]{1,0:T(8,128)(2,1)} %get-tuple-element.329), channel_id=1, source_target_pairs={{0,2},{1,3},{2,0},{3,1},{4,6},{5,7},{6,4},{7,5},{8,10},{9,11},{10,... | collective-permute-start | bytes 1572872 | tf_op jit(solution)/shard_map/ppermute | solution.py:98
  774.0 27.6 %collective-permute-start.118 = (bf16[128,2048]{1,0:T(8,128)(2,1)S(1)}, bf16[128,2048]{1,0:T(8,128)(2,1)S(1)}, u32[]{:S(2)}, u32[]{:S(2)}) collective-permute-start(bf16[128,2048]{1,0:T(8,128)(2,1)S(1)} %add_convert_fusion.4), channel_id=1, source_target_pairs={{4,8},{5,9},{6,10},{7,11},{8,4},{9,5},{10,6},{11,7},{20,24},{21,25... | collective-permute-start | bytes 1572872 | tf_op jit(solution)/shard_map/ppermute | solution.py:98
  799.9 45.2 %collective-permute-start.130 = (bf16[512,1024]{1,0:T(8,128)(2,1)S(1)}, bf16[512,1024]{1,0:T(8,128)(2,1)}, u32[]{:S(2)}, u32[]{:S(2)}) collective-permute-start(bf16[512,1024]{1,0:T(8,128)(2,1)S(1)} %copy-done.35), channel_id=1, source_target_pairs={{0,16},{16,0},{1,17},{17,1},{2,18},{18,2},{3,19},{19,3},{4,20},{20... | collective-permute-start | bytes 3145736 | tf_op jit(solution)/shard_map/ppermute | solution.py:58
  801.6 39.3 %collective-permute-start.126 = (bf16[128,2048]{1,0:T(8,128)(2,1)S(1)}, bf16[128,2048]{1,0:T(8,128)(2,1)S(1)}, u32[]{:S(2)}, u32[]{:S(2)}) collective-permute-start(bf16[128,2048]{1,0:T(8,128)(2,1)S(1)} %bitcast.243), channel_id=1, source_target_pairs={{0,16},{16,0},{1,17},{17,1},{2,18},{18,2},{3,19},{19,3},{4,20},{20... | collective-permute-start | bytes 1572872 | tf_op jit(solution)/shard_map/ppermute | solution.py:58
  (208 other events, 3542.6 us)

commit v3 on v2

--- a/solution.py
+++ b/solution.py
@@ -121,16 +121,24 @@
             self.result, self.sent, self.over = stop.value, (), True
 
     def step(self, *others):
-        values = together(*self.sent, *others) if self.sent or others else ()
-        count = len(self.sent)
-        if not self.over:
-            self._go(values[:count])
-        return values[count:]
+        return step_all([self], *others)
 
     def finish(self):
         while not self.over:
             self.step()
         return self.result
+
+
+def step_all(rounds, *others):
+    sent = [values for one in rounds for values in one.sent]
+    values = together(*sent, *others) if sent or others else ()
+    at = 0
+    for one in rounds:
+        count = len(one.sent)
+        if not one.over:
+            one._go(values[at : at + count])
+        at += count
+    return values[at:]
 
 
 def gather_rounds(block):
@@ -192,8 +200,8 @@
     return (left.astype(jnp.float32) + right.astype(jnp.float32)).astype(jnp.bfloat16)
 
 
-def scatter_rounds(make, count):
-    (far,) = yield (send(make(count // 2, count // 2), swap_core),)
+def scatter_rounds(make, count, tie):
+    (far,) = yield (send(tie(make(count // 2, count // 2)), swap_core),)
     close = make(0, count // 2)
     rows = count // 16
 
@@ -226,11 +234,11 @@
     )
 
 
-def scatter_whole(make, count):
+def scatter_whole(make, count, tie):
     yield ()
-    return lax.psum_scatter(make(0, count), "expert", scatter_dimension=0, tiled=True).astype(
-        jnp.float32
-    )
+    return lax.psum_scatter(
+        tie(make(0, count)), "expert", scatter_dimension=0, tiled=True
+    ).astype(jnp.float32)
 
 
 def pick_kernel(picks, scale, *refs):
@@ -256,33 +264,41 @@
     )(picks, scale, *blocks)
 
 
-def merge_kernel(*refs):
-    *pairs, out = refs
-    count = len(pairs) // 2
+def merge_kernel(count, parts, *refs):
+    pairs, outs = refs[: 2 * count], refs[-parts:]
+    width = outs[0].shape[1]
     for index in range(count):
 
         @pl.when(pl.program_id(0) == index)
         def _():
-            out[...] = pairs[index][...].astype(jnp.float32) + pairs[count + index][...].astype(
+            total = pairs[index][...].astype(jnp.float32) + pairs[count + index][...].astype(
                 jnp.float32
             )
-
-
-def merge(own, far):
+            for i, out in enumerate(outs):
+                out[...] = total[:, i * width : (i + 1) * width]
+
+
+def merge(own, far, parts, pieces=None, before=None):
+    count = len(own)
+    begin = pieces if before else 0
+    before = before or []
+    pieces = begin + count if before else pieces or count
     rows, width = own[0].shape
     return pl.pallas_call(
-        merge_kernel,
-        grid=(len(own),),
-        in_specs=[pl.BlockSpec((rows, width), lambda i: (0, 0))] * (2 * len(own)),
-        out_specs=pl.BlockSpec((rows, width), lambda i: (i, 0)),
-        out_shape=jax.ShapeDtypeStruct((len(own) * rows, width), jnp.float32),
+        functools.partial(merge_kernel, count, parts),
+        grid=(count,),
+        in_specs=[pl.BlockSpec((rows, width), lambda i: (0, 0))] * (2 * count)
+        + [pl.BlockSpec(memory_space=pl.ANY)] * len(before),
+        out_specs=[pl.BlockSpec((rows, width // parts), lambda i: (begin + i, 0))] * parts,
+        out_shape=[jax.ShapeDtypeStruct((pieces * rows, width // parts), jnp.float32)] * parts,
+        input_output_aliases={2 * count + i: i for i in range(len(before))},
         cost_estimate=pl.CostEstimate(
-            flops=len(own) * rows * width,
-            bytes_accessed=8 * len(own) * rows * width,
+            flops=count * rows * width,
+            bytes_accessed=8 * count * rows * width,
             transcendentals=0,
         ),
         name="merge",
-    )(*own, *far)
+    )(*own, *far, *before)
 
 
 def project_kernel(order, left_t, left_next_t, right, out):
@@ -393,13 +409,46 @@
     )(order, weight, *blocks)
 
 
-def out_kernel(rows, where, attended, resid, gain, *refs):
-    *blocks, far_one, far_two, cross, middle, normed = refs
-    count = len(blocks)
+def tail_kernel(*refs):
+    *blocks, out = refs
+    rows = blocks[0].shape[0]
+    for index, block in enumerate(blocks):
+        out[index * rows : (index + 1) * rows, :] = block[...]
+
+
+def tail_specs(blocks, rows, tail):
+    width = blocks[0].shape[1]
+    return [pl.BlockSpec((tail, width), lambda i: (rows // tail, 0))] * len(blocks)
+
+
+def tails(blocks, rows, tail):
+    width = blocks[0].shape[1]
+    return pl.pallas_call(
+        tail_kernel,
+        grid=(1,),
+        in_specs=tail_specs(blocks, rows, tail),
+        out_specs=pl.BlockSpec((len(blocks) * tail, width), lambda i: (0, 0)),
+        out_shape=jax.ShapeDtypeStruct((len(blocks) * tail, width), jnp.bfloat16),
+        name="tails",
+    )(*blocks)
+
+
+def four(refs, index):
+    return jnp.concatenate([ref[...] for ref in refs[index : index + 4]], axis=0)
+
+
+def far_four(far, cross, index):
+    rows = far.shape[0] // 2
+    ref, at = (far, index // 4) if index < 8 else (cross, index // 4 - 2)
+    return ref[at * rows : (at + 1) * rows, :]
+
+
+def out_kernel(where, attended, resid, gain, *refs):
+    *near, far, cross, middle, normed = refs
+    count = len(near)
     half = HEAD_DIM // 2
     first_group = where[count] == 0
     total = resid[...].astype(jnp.float32)
-    far_rows = [far_one[...], far_two[...], cross[: 4 * half], cross[4 * half :]]
     for index in range(0, count, 4):
         near_left, far_left = [], []
         for i in range(index, index + 4):
@@ -407,20 +456,30 @@
             low, high = columns[:, :half], columns[:, half:]
             near_left.append(jnp.where(first_group, low, high))
             far_left.append(jnp.where(first_group, high, low))
-        near = jnp.concatenate([blocks[i][rows:] for i in range(index, index + 4)], axis=0)
-        total += mm(jnp.concatenate(near_left, axis=1).astype(jnp.bfloat16), near)
-        total += mm(jnp.concatenate(far_left, axis=1).astype(jnp.bfloat16), far_rows[index // 4])
+        total += mm(jnp.concatenate(near_left, axis=1).astype(jnp.bfloat16), four(near, index))
+        total += mm(
+            jnp.concatenate(far_left, axis=1).astype(jnp.bfloat16), far_four(far, cross, index)
+        )
     middle[...] = total
     inverse = lax.rsqrt(jnp.mean(total * total, axis=-1, keepdims=True) + eps)
     normed[...] = (total * inverse * gain[...]).astype(normed.dtype)
 
 
-def out_project(where, attended, resid, gain, rows, blocks, far):
-    width = resid.shape[1]
+def whole_specs(*arrays):
+    return [pl.BlockSpec(array.shape, lambda i, rank=array.ndim: (0,) * rank) for array in arrays]
+
+
+def out_project(where, attended, resid, gain, blocks, far, cross):
+    rows, width = resid.shape
+    tail = blocks[0].shape[0] - rows
     return pl.pallas_call(
-        functools.partial(out_kernel, rows),
-        in_specs=[scalars] + [vectors] * (3 + len(blocks) + len(far)),
-        out_specs=[vectors] * 2,
+        out_kernel,
+        grid=(1,),
+        in_specs=[scalars]
+        + whole_specs(attended, resid, gain)
+        + tail_specs(blocks, rows, tail)
+        + whole_specs(far, cross),
+        out_specs=whole_specs(resid, resid),
         out_shape=[
             jax.ShapeDtypeStruct((rows, width), jnp.float32),
             jax.ShapeDtypeStruct((rows, width), jnp.bfloat16),
@@ -431,19 +490,17 @@
             transcendentals=0,
         ),
         name="out_project",
-    )(where, attended, resid, gain, *blocks, *far)
-
-
-def out_back_kernel(rows, where, branch, *refs):
-    *blocks, far_one, far_two, cross, out = refs
-    count = len(blocks)
+    )(where, attended, resid, gain, *blocks, far, cross)
+
+
+def out_back_kernel(where, branch, *refs):
+    *near_refs, far_ref, cross, out = refs
+    count = len(near_refs)
     half = HEAD_DIM // 2
     first_group = where[count] == 0
-    far_rows = [far_one[...], far_two[...], cross[: 4 * half], cross[4 * half :]]
     for index in range(0, count, 4):
-        near = jnp.concatenate([blocks[i][rows:] for i in range(index, index + 4)], axis=0)
-        near = contract_cols(branch[...], near)
-        far = contract_cols(branch[...], far_rows[index // 4])
+        near = contract_cols(branch[...], four(near_refs, index))
+        far = contract_cols(branch[...], far_four(far_ref, cross, index))
         for i in range(index, index + 4):
             here = slice((i - index) * half, (i - index + 1) * half)
             low = jnp.where(first_group, near[:, here], far[:, here])
@@ -451,20 +508,26 @@
             out[where[i]] = jnp.concatenate([low, high], axis=1).astype(out.dtype)
 
 
-def out_project_back(where, branch, rows, blocks, far):
-    width = branch.shape[1]
+def out_project_back(where, branch, blocks, far, cross):
+    rows, width = branch.shape
+    tail = blocks[0].shape[0] - rows
+    shape = (len(blocks), rows, HEAD_DIM)
     return pl.pallas_call(
-        functools.partial(out_back_kernel, rows),
-        in_specs=[scalars] + [vectors] * (1 + len(blocks) + len(far)),
-        out_specs=vectors,
-        out_shape=jax.ShapeDtypeStruct((len(blocks), rows, HEAD_DIM), jnp.bfloat16),
+        out_back_kernel,
+        grid=(1,),
+        in_specs=[scalars]
+        + whole_specs(branch)
+        + tail_specs(blocks, rows, tail)
+        + whole_specs(far, cross),
+        out_specs=pl.BlockSpec(shape, lambda i: (0, 0, 0)),
+        out_shape=jax.ShapeDtypeStruct(shape, jnp.bfloat16),
         cost_estimate=pl.CostEstimate(
             flops=2 * rows * width * width,
             bytes_accessed=2 * width * width,
             transcendentals=0,
         ),
         name="out_project_back",
-    )(where, branch, *blocks, *far)
+    )(where, branch, *blocks, far, cross)
 
 
 def turn(values, cosine, rope_sine):
@@ -777,8 +840,8 @@
     def gather(block):
         return Rounds(gather_rounds(block) if grouped else gather_whole(block))
 
-    def scatter(make):
-        return Rounds((scatter_rounds if grouped else scatter_whole)(make, seq_length))
+    def scatter(make, tie=lambda addends: addends):
+        return Rounds((scatter_rounds if grouped else scatter_whole)(make, seq_length, tie))
 
     def exchange(values):
         return lax.all_to_all(values, "expert", split_axis=0, concat_axis=0, tiled=True)
@@ -805,7 +868,7 @@
     waiting = []
 
     def weight_grad(left, right):
-        pieces = 4 if grouped else 1
+        pieces = left.shape[1] // 256 if grouped else 1
         step = left.shape[1] // pieces
         own = [
             contract_rows(left[:, i * step : (i + 1) * step], right).astype(jnp.bfloat16)
@@ -815,9 +878,6 @@
         waiting.extend((far, i) for i in range(pieces))
         return own, far
 
-    def weight_total(own, far):
-        return (merge(own, far) if groups == 2 else far[0].astype(jnp.float32))[None]
-
     def cross(*others):
         if not (waiting and grouped):
             return others
@@ -853,20 +913,27 @@
     taken = sent_w.shape[1]
     arrived = exchange(jnp.concatenate([sent_w, gate_rows], axis=1))
 
+    key_seg = jnp.broadcast_to(segments[:, None], (seq_length, HEAD_DIM))
+    query_seg = segments[None, :]
+    cosine, rope_sine = rope_tables(jnp.arange(seq_length, dtype=jnp.int32))
+    gains = jnp.stack(
+        [
+            lax.dynamic_slice_in_dim(query_gain, head * HEAD_DIM, HEAD_DIM),
+            lax.dynamic_slice_in_dim(key_gain, head * HEAD_DIM, HEAD_DIM),
+        ],
+        axis=1,
+    )
     if grouped:
         rounds = gather(jnp.concatenate([normed_in, take(w_out)], axis=0))
-        rounds.step()
         rounds.step()
         (arrived,) = rounds.step(arrived)
         head_w = arrived[:, :taken]
         head_w_far = swap(head_w, "dp", 1)
+        rounds.step(key_seg, cosine, rope_sine, gains)
         (head_w_far,) = rounds.step(head_w_far)
         blocks = rounds.finish()
         head_w = by_half(jnp.stack([head_w, head_w_far], axis=1), 1).reshape(width, 3 * HEAD_DIM)
-        out_far = [
-            swap(jnp.concatenate([block[row_count:] for block in some], axis=0), "dp", 1)
-            for some in (blocks[:4], blocks[4:8])
-        ]
+        out_far = swap(tails(blocks[: devices // 2], row_count, w_half), "dp", 1)
     else:
         blocks = gather(normed_in).finish()
         head_w = arrived[:, :taken].reshape(width, 3 * HEAD_DIM)
@@ -884,17 +951,8 @@
     picks = picks.astype(jnp.bfloat16)
     unpicks = (rank[:, :, None] == slot[None, None, :]).astype(jnp.bfloat16)
     ones = jnp.ones_like(slot_gate)
-
-    key_seg = jnp.broadcast_to(segments[:, None], (seq_length, HEAD_DIM))
-    query_seg = segments[None, :]
-    cosine, rope_sine = rope_tables(jnp.arange(seq_length, dtype=jnp.int32))
-    gains = jnp.stack(
-        [
-            lax.dynamic_slice_in_dim(query_gain, head * HEAD_DIM, HEAD_DIM),
-            lax.dynamic_slice_in_dim(key_gain, head * HEAD_DIM, HEAD_DIM),
-        ],
-        axis=1,
-    )
+    ff = w_gate.shape[2]
+    w_both = jnp.concatenate([w_gate[0], w_up[0]], axis=1)
 
     cot_rounds = gather(cotangent)
     query_raw, key_raw, value, value_t, squares = heads_in(order, head_w, row_count, blocks)
@@ -904,22 +962,20 @@
         )
     (squares,) = cot_rounds.step(squares)
     squares = butterfly(squares, "expert")
-    if grouped:
-        squares, out_far[0] = cot_rounds.step(squares, out_far[0])
+    (squares,) = cot_rounds.step(squares)
     inverse = lax.rsqrt(squares / width + eps)
     query_t, query, key_t, key, attended, attended_t, log_total = attend(
         query_raw, key_raw, value_t, inverse, gains, cosine, rope_sine, key_seg, query_seg
     )
     if grouped:
-        attended, out_far[1] = cot_rounds.step(attended, out_far[1])
-        out_cross = send(jnp.concatenate(out_far, axis=0), swap_core)
+        attended, out_far = cot_rounds.step(attended, out_far)
+        out_cross = send(out_far, swap_core)
 
     attended_low = exchange(my_part(attended, 1).reshape(devices, row_count, part))
     (attended_low,) = cot_rounds.step(attended_low)
     if grouped:
-        out_far.append(out_cross)
         middle, normed_mid = out_project(
-            where, attended_low, tokens, ffn_gain[None, :], row_count, blocks, out_far
+            where, attended_low, tokens, ffn_gain[None, :], blocks, out_far, out_cross
         )
     else:
         attended_low = attended_low.transpose(1, 0, 2).reshape(row_count, width)
@@ -930,55 +986,60 @@
 
     mid_rounds = gather(normed_mid)
     grad_eo = pick(picks, slot_gate, cot_blocks)
-    (grad_eo,) = mid_rounds.step(grad_eo)
+    head_w_t = jnp.concatenate(
+        [my_part(head_w[:, i * HEAD_DIM : (i + 1) * HEAD_DIM], 1).T for i in range(3)], axis=0
+    )
+    grad_eo, head_w_t = mid_rounds.step(grad_eo, head_w_t)
     rows_in = pick(picks, ones, mid_rounds.finish())
-    gate_in = mm(rows_in, w_gate[0])
-    up_in = mm(rows_in, w_up[0])
+    gate_up = mm(rows_in, w_both)
+    gate_in, up_in = gate_up[:, :ff], gate_up[:, ff:]
     sigmoid_in = jax.nn.sigmoid(gate_in)
     silu_in = gate_in * sigmoid_in
     hidden = (silu_in * up_in).astype(jnp.bfloat16)
     grad_down, down_far = weight_grad(hidden, grad_eo)
 
-    def give_back(rows):
-        blocks = rows.reshape(devices, slots, width)
-
+    def give_back(produce):
         def some(first, count):
             here = slice(first // row_count, (first + count) // row_count)
+            rows = produce(slice(here.start * slots, here.stop * slots))
             return jnp.einsum(
                 "bts,bsd->btd",
                 unpicks[here],
-                blocks[here],
+                rows.astype(jnp.bfloat16).reshape(-1, slots, width),
                 preferred_element_type=jnp.bfloat16,
             ).reshape(count, width)
 
         return some
 
     hidden_next, grad_eo_next = together(hidden, grad_eo, *grad_down)[:2]
-    expert_out = (mm(hidden_next, w_down[0]) * slot_gate).astype(jnp.bfloat16)
-    out_rounds = scatter(give_back(expert_out))
+    mix_rounds = scatter(
+        give_back(lambda some: mm(hidden_next[some], w_down[0]) * slot_gate[some])
+    )
     grad_hidden = contract_cols(grad_eo_next, w_down[0])
-    grad_up_pre = (grad_hidden * silu_in).astype(jnp.bfloat16)
-    grad_gate_pre = (
-        grad_hidden * up_in * sigmoid_in * (1.0 + gate_in * (1.0 - sigmoid_in))
-    ).astype(jnp.bfloat16)
-    grad_up_pre, grad_gate_pre = ride(out_rounds, grad_up_pre, grad_gate_pre)
-    grad_rows = contract_cols(grad_gate_pre, w_gate[0])
-    (grad_rows,) = out_rounds.step(grad_rows)
-    grad_rows = (grad_rows + contract_cols(grad_up_pre, w_up[0])).astype(jnp.bfloat16)
-    (grad_rows,) = ride(out_rounds, grad_rows)
-    row_rounds = scatter(give_back(grad_rows))
-    out_rounds.step()
-    row_rounds.step()
-    out_rounds.step()
-    mixed = out_rounds.finish()
-    activations = (middle + mixed).astype(jnp.bfloat16)
-
-    grad_gate, gate_far = weight_grad(rows_in, grad_gate_pre)
-    ride(row_rounds)
-    row_rounds.step(*grad_gate)
-    grad_up, up_far = weight_grad(rows_in, grad_up_pre)
-    ride(row_rounds)
-    row_rounds.step(*grad_up)
+    grad_pre = jnp.concatenate(
+        [
+            (
+                grad_hidden * up_in * sigmoid_in * (1.0 + gate_in * (1.0 - sigmoid_in))
+            ).astype(jnp.bfloat16),
+            (grad_hidden * silu_in).astype(jnp.bfloat16),
+        ],
+        axis=1,
+    )
+    (grad_pre,) = ride(mix_rounds, grad_pre)
+    row_rounds = scatter(
+        give_back(lambda some: contract_cols(grad_pre[some], w_both)),
+        lambda addends: ride(mix_rounds, addends)[0],
+    )
+    grad_both, both_far = weight_grad(rows_in, grad_pre)
+    far, i = waiting.pop(0) if grouped else (None, 0)
+    if grouped:
+        (far[i], *_) = step_all([row_rounds, mix_rounds], far[i], *grad_both[:1])
+    else:
+        row_rounds.step()
+    ride(row_rounds, *mix_rounds.sent, *grad_both[1:2])
+    row_rounds.step(*grad_both[2:4])
+    ride(row_rounds, *grad_both[4:5])
+    ride(row_rounds, *grad_both[5:6])
     grad_normed_mid = row_rounds.finish()
 
     grad_out = cotangent.astype(jnp.float32)
@@ -986,15 +1047,23 @@
     mid_back, grad_ffn_gain = norm_back(grad_normed_mid, normal_mid, inverse_mid, ffn_gain)
     grad_middle = grad_out + mid_back
     grad_branch = grad_middle.astype(jnp.bfloat16)
-    (grad_branch,) = cross(grad_branch)
     if grouped:
-        grad_columns = out_project_back(where, grad_branch, row_count, blocks, out_far)
+        grad_columns = out_project_back(where, grad_branch, blocks, out_far, out_cross)
+        (grad_columns,) = ride(mix_rounds, grad_columns)
     else:
         grad_columns = to_heads(contract_cols(grad_branch, out_full).astype(jnp.bfloat16))
     grad_attended = exchange(grad_columns).reshape(seq_length, HEAD_DIM)
-    (grad_attended,) = cross(grad_attended)
-
-    branch_rounds = gather(after(grad_branch, grad_attended))
+    if groups == 2:
+        (down_total,) = merge(grad_down, down_far, 1)
+        grad_attended, down_total, *_ = cross(grad_attended, down_total, *grad_both[6:])
+    else:
+        down_total = down_far[0].astype(jnp.float32)
+    mixed = mix_rounds.finish()
+    activations = (middle + mixed).astype(jnp.bfloat16)
+    branch_all = lax.all_gather(
+        after(grad_branch, grad_attended), "expert", axis=0, tiled=True
+    )
+
     weighted_query, weighted_key, grad_value_t, inner_query, inner_key, gain_sums = attend_back(
         key_seg,
         query_seg,
@@ -1023,9 +1092,9 @@
                 )
             ]
         )
-    (inner,) = ride(branch_rounds, inner)
+    (inner,) = cross(inner)
     inner = butterfly(inner, "expert") / width
-    (inner,) = branch_rounds.step(inner)
+    (inner,) = cross(inner)
     grad_raw_t = jnp.concatenate(
         [
             my_part(
@@ -1040,56 +1109,55 @@
         + [my_part(grad_value_t, 0)],
         axis=0,
     )
-    head_w_t = jnp.concatenate(
-        [my_part(head_w[:, i * HEAD_DIM : (i + 1) * HEAD_DIM], 1).T for i in range(3)], axis=0
+    in_rounds = scatter(
+        lambda first, count: project(order, grad_raw_t, head_w_t, row_count, first, count)
     )
     grad_w_t = stack_product(order, grad_raw_t, row_count, blocks)
     grad_attn_gain = jnp.sum(grad_w_t * head_w_t.astype(jnp.float32), axis=0) / attn_gain
     w_columns = exchange(
         grad_w_t.astype(jnp.bfloat16).reshape(3 * part, devices, w_rows).transpose(1, 0, 2)
     )
-    (grad_raw_t,) = ride(branch_rounds, grad_raw_t)
-    in_rounds = scatter(
-        lambda first, count: project(order, grad_raw_t, head_w_t, row_count, first, count)
-    )
-    (w_columns,) = branch_rounds.step(w_columns)
-    ride(in_rounds, *branch_rounds.sent)
-    dense = [
-        w_columns[:, i * part : (i + 1) * part].reshape(width, w_rows).T for i in range(3)
-    ]
-    branch_blocks = branch_rounds.finish()
-    out_part = stack_product(
-        order, my_part(attended_t, 0), row_count, branch_blocks
-    ).astype(jnp.bfloat16)
-    in_rounds.step()
     ride(in_rounds)
-    out_part, *dense = in_rounds.step(out_part, *dense)
-    dense_far = [dp_start(values) for values in dense]
-    out_part_far = dp_start(out_part)
-    ride(in_rounds)
-    grad_normed_in = in_rounds.finish()
-    in_back, _ = norm_back(grad_normed_in, normal_in, inverse_in, attn_gain)
-    input_grad = (grad_middle + in_back).astype(jnp.bfloat16)
 
     def placed(values):
         return lax.dynamic_update_slice_in_dim(
             jnp.zeros((width,), jnp.float32), values, me * part, 0
         )
 
-    gain_total = butterfly(
-        butterfly(
-            jnp.stack(
-                [
-                    grad_attn_gain,
-                    placed(my_part(gain_sums[:, 0], 0)),
-                    placed(my_part(gain_sums[:, 1], 0)),
-                    grad_ffn_gain,
-                ]
-            ),
-            "expert",
-        ),
-        "dp",
-    )
+    gain_parts = jnp.stack(
+        [
+            grad_attn_gain,
+            placed(my_part(gain_sums[:, 0], 0)),
+            placed(my_part(gain_sums[:, 1], 0)),
+            grad_ffn_gain,
+        ]
+    )
+    out_part = mm(my_part(attended_t, 0), branch_all).astype(jnp.bfloat16)
+    gain_parts, out_part = ride(in_rounds, gain_parts, out_part)
+    out_part_far = dp_start(out_part)
+    if groups == 2:
+        both_total = merge(grad_both[:4], both_far[:4], 2, len(grad_both))
+        w_columns, *both_total = in_rounds.step(w_columns, *both_total)
+    else:
+        in_rounds.step()
+    dense = [
+        w_columns[:, i * part : (i + 1) * part].reshape(width, w_rows).T for i in range(3)
+    ]
+    dense = in_rounds.step(*dense)
+    dense_far = [dp_start(values) for values in dense]
+    if groups == 2:
+        both_total = merge(grad_both[4:], both_far[4:], 2, 4, both_total)
+        gate_total, up_total = in_rounds.step(*both_total)
+    else:
+        in_rounds.step()
+        both_total = both_far[0].astype(jnp.float32)
+        gate_total, up_total = both_total[:, :ff], both_total[:, ff:]
+    grad_normed_in = in_rounds.finish()
+    grad_normed_in, gain_parts = together(grad_normed_in, gain_parts)
+    gain_total = butterfly(butterfly(gain_parts, "expert"), "dp")
+    in_back, _ = norm_back(grad_normed_in, normal_in, inverse_in, attn_gain)
+    input_grad = (grad_middle + in_back).astype(jnp.bfloat16)
+
     return (
         activations,
         input_grad,
@@ -1101,9 +1169,9 @@
         dp_end(dense[1], dense_far[1]),
         dp_end(dense[2], dense_far[2]),
         dp_end(out_part, out_part_far),
-        weight_total(grad_gate, gate_far),
-        weight_total(grad_up, up_far),
-        weight_total(grad_down, down_far),
+        gate_total[None],
+        up_total[None],
+        down_total[None],
     )
 
 

time: 862 us -> 773 us (0.90)
  waiting for transfers between devices: 334 us -> 225 us
  matrix products: 106 us -> 122 us
  other arithmetic: 64 us -> 78.1 us
  local copies, waits for them, and re-layouts: 42.3 us -> 28.7 us
  between operations: 3.08 us -> 16 us
    ppermute x32 -> x31, waiting for transfers between devices: 139 us -> 46.7 us  [swap(): return lax.ppermute(values, axis, [(i, i ^ step) for i in range(count)])]
    all_to_all x4, waiting for transfers between devices: 16.8 us -> 0.01 us  [exchange(): lax.all_to_all(values, 'expert', split_axis=0, concat_axis=0, tiled=True)]
    convert_element_type x18, other arithmetic: 16.1 us -> 31.6 us  [add_low(): (left.astype(jnp.float32) + right.astype(jnp.float32)).astype(jnp.bfloat16)]
    ppermute x99 -> x82, starting transfers between devices: 117 us -> 106 us  [send(): return lax.ppermute(values, 'expert', pairs)]
    slice x9 -> x1, local copies, waits for them, and re-layouts: 9.09 us -> 0.01 us  [local(): slot_gate[some]]
    dot_general x4 -> x5, matrix products: 27 us -> 32.6 us  [mm(): return jnp.dot(left, right, preferred_element_type=jnp.float32)]
    ppermute x32 -> x31, starting transfers between devices: 32.2 us -> 35.2 us  [swap(): return lax.ppermute(values, axis, [(i, i ^ step) for i in range(count)])]
    pallas_call x5 -> x6, Pallas kernels: 40.2 us -> 38.5 us  [the longest x3 21.6 us: merge(): pl.pallas_call(functools.partial(merge_kernel, count, parts), grid=(count...]
  transfers between devices with their start and end apart: 135 -> 118, of which waited for: 49 -> 39; matrix products, arithmetic and copies ran while one was open for 17% -> 24% of each run, Pallas kernels for 13% -> 16%
where the time goes in v3:
time: 773 us; the launch traced here: 762 us
  waiting for transfers between devices  225 us (29%)
  starting transfers between devices  165 us (21%)
  Pallas kernels  127 us (16%)
  matrix products  122 us (16%)
  other arithmetic  78.1 us (10%)
  local copies, waits for them, and re-layouts  28.7 us (4%)
  between operations  16 us (2%)
    ppermute x82, waiting for transfers between devices, send(): return lax.ppermute(values, 'expert', pairs)  178 us
    ppermute x82, starting transfers between devices, send(): return lax.ppermute(values, 'expert', pairs)  106 us
    ppermute x31, waiting for transfers between devices, swap(): return lax.ppermute(values, axis, [(i, i ^ step) for i in range(count)])  46.7 us
    dot_general x12, matrix products, contract_rows(): lax.dot_general(left, right, (((0,), (0,)), ((), ())), preferred_element_...  37 us
    ppermute x31, starting transfers between devices, swap(): return lax.ppermute(values, axis, [(i, i ^ step) for i in range(count)])  35.2 us
    dot_general x3, matrix products, contract_cols(): lax.dot_general(left, right, (((1,), (1,)), ((), ())), preferred_element_...  35.1 us
    dot_general x5, matrix products, mm(): return jnp.dot(left, right, preferred_element_type=jnp.float32)  32.6 us
    convert_element_type x18, other arithmetic, add_low(): (left.astype(jnp.float32) + right.astype(jnp.float32)).astype(jnp.bfloat16)  31.6 us
  transfers between devices with their start and end apart: 118, of which 39 were waited for; matrix products, arithmetic and copies ran while one was open for 24% of the time, Pallas kernels for 16%

profile of v3, /device:TPU:0, one launch (start us, length us, event | category | flops | bytes accessed | tf_op | source)
XLA Modules:
  0.0 761.6 jit_solution(7789347791331578992)
XLA Ops:
  10.6 7.4 all-to-all-start
  23.6 30.2 %collective-permute-done.3.refs_1_ = bf16[192,2048]{1,0:T(8,128)(2,1)S(1)} collective-permute-done((bf16[192,2048]{1,0:T(8,128)(2,1)S(1)}, bf16[192,2048]{1,0:T(8,128)(2,1)S(1)}, u32[]{:S(2)}, u32[]{:S(2)}) %collective-permute-start.3) | collective-permute-done | bytes 786464 | tf_op jit(solution)/shard_map/ppermute | solution.py:98
  59.5 22.4 %collective-permute-done.7 = bf16[192,2048]{1,0:T(8,128)(2,1)} collective-permute-done((bf16[192,2048]{1,0:T(8,128)(2,1)}, bf16[192,2048]{1,0:T(8,128)(2,1)}, u32[]{:S(2)}, u32[]{:S(2)}) %collective-permute-start.7) | collective-permute-done | bytes 786464 | tf_op jit(solution)/shard_map/ppermute | solution.py:98
  93.3 8.9 %collective-permute-done.10 = bf16[192,2048]{1,0:T(8,128)(2,1)S(1)} collective-permute-done((bf16[192,2048]{1,0:T(8,128)(2,1)}, bf16[192,2048]{1,0:T(8,128)(2,1)S(1)}, u32[]{:S(2)}, u32[]{:S(2)}) %collective-permute-start.10) | collective-permute-done | bytes 786464 | tf_op jit(solution)/shard_map/ppermute | solution.py:98
  113.1 8.9 %collective-permute-done.14.refs_7_ = bf16[192,2048]{1,0:T(8,128)(2,1)} collective-permute-done((bf16[192,2048]{1,0:T(8,128)(2,1)S(1)}, bf16[192,2048]{1,0:T(8,128)(2,1)}, u32[]{:S(2)}, u32[]{:S(2)}) %collective-permute-start.14) | collective-permute-done | bytes 786464 | tf_op jit(solution)/shard_map/ppermute | solution.py:98
  131.8 11.3 %heads_in.1 = (f32[128,2048]{1,0:T(8,128)}, f32[128,2048]{1,0:T(8,128)}, bf16[2048,128]{1,0:T(8,128)(2,1)}, bf16[128,2048]{1,0:T(8,128)(2,1)}, f32[2,2048]{1,0:T(2,128)}) custom-call(s32[16]{0:T(128)} %pad_add_fusion.order, bf16[2048,384]{1,0:T(8,128)(2,1)} %bitcast.221, bf16[192,2048]{1,0:T(8,128)(2,1)} %copy-done.3, bf16[192,2048]{1,0:T(8,128)(2,1)} %copy-done.7, ...), custom_call_target="tpu_custom_call" | custom-call | flops 3221225472 | bytes 8388608 | tf_op jit(solution)/shard_map/heads_in/pallas_call | solution.py:392
  162.1 13.3 %collective-permute-done.22 = bf16[128,2048]{1,0:T(8,128)(2,1)} collective-permute-done((bf16[128,2048]{1,0:T(8,128)(2,1)}, bf16[128,2048]{1,0:T(8,128)(2,1)}, u32[]{:S(2)}, u32[]{:S(2)}) %collective-permute-start.22) | collective-permute-done | bytes 524320 | tf_op jit(solution)/shard_map/ppermute | solution.py:98
  179.1 14.7 %attend.1 = (bf16[128,2048]{1,0:T(8,128)(2,1)}, bf16[2048,128]{1,0:T(8,128)(2,1)}, bf16[128,2048]{1,0:T(8,128)(2,1)}, bf16[2048,128]{1,0:T(8,128)(2,1)}, bf16[20...) custom-call(f32[128,2048]{1,0:T(8,128)} %get-tuple-element.185.query_raw, ...), custom_call_target="tpu_custom_call" | custom-call | flops 2147483648 | bytes 6291456 | tf_op jit(solution)/shard_map/attend/pallas_call | solution.py:593
  207.5 14.5 %collective-permute-done.34.refs_7_ = bf16[128,2048]{1,0:T(8,128)(2,1)} collective-permute-done((bf16[128,2048]{1,0:T(8,128)(2,1)S(1)}, bf16[128,2048]{1,0:T(8,128)(2,1)}, u32[]{:S(2)}, u32[]{:S(2)}) %collective-permute-start.34) | collective-permute-done | bytes 524320 | tf_op jit(solution)/shard_map/ppermute | solution.py:98
  238.9 8.2 %pick.2 = bf16[1536,2048]{1,0:T(8,128)(2,1)} custom-call(bf16[16,96,128]{2,1,0:T(8,128)(2,1)} %fusion.55.picks, f32[1536,1]{1,0:T(8,128)} %reshape.372.scale, bf16[128,2048]{1,0:T(8,128)(2,1)} %refs_0_.1, bf16[128,2048]{1,0:T(8,128)(2,1)} %copy-done.40, bf16[128,2048]{1,0:T(8,128)(2,1)} %copy-done.30, bf16[128,2048]{1,0:T(8,128)(2,1)} %copy-done.31, ...), custom_call_target="tpu_custom_call" | custom-call | flops 805306368 | bytes 14680064 | tf_op jit(solution)/shard_map/pick/pallas_call | solution.py:255
  253.7 14.5 %collective-permute-done.45 = bf16[128,2048]{1,0:T(8,128)(2,1)S(1)} collective-permute-done((bf16[128,2048]{1,0:T(8,128)(2,1)}, bf16[128,2048]{1,0:T(8,128)(2,1)S(1)}, u32[]{:S(2)}, u32[]{:S(2)}) %collective-permute-start.45) | collective-permute-done | bytes 524320 | tf_op jit(solution)/shard_map/ppermute | solution.py:98
  270.7 12.3 %collective-permute-done.48 = bf16[128,2048]{1,0:T(8,128)(2,1)S(1)} collective-permute-done((bf16[128,2048]{1,0:T(8,128)(2,1)S(1)}, bf16[128,2048]{1,0:T(8,128)(2,1)S(1)}, u32[]{:S(2)}, u32[]{:S(2)}) %collective-permute-start.48) | collective-permute-done | bytes 524320 | tf_op jit(solution)/shard_map/ppermute | solution.py:98
  284.0 10.5 %collective-permute-done.52.refs_7_ = bf16[128,2048]{1,0:T(8,128)(2,1)S(1)} collective-permute-done((bf16[128,2048]{1,0:T(8,128)(2,1)S(1)}, bf16[128,2048]{1,0:T(8,128)(2,1)S(1)}, u32[]{:S(2)}, u32[]{:S(2)}) %collective-permute-start.52) | collective-permute-done | bytes 524320 | tf_op jit(solution)/shard_map/ppermute | solution.py:98
  298.2 8.4 %pick.3 = bf16[1536,2048]{1,0:T(8,128)(2,1)} custom-call(bf16[16,96,128]{2,1,0:T(8,128)(2,1)} %fusion.55.picks, f32[1536,1]{1,0:T(8,128)} %broadcast_in_dim.82.scale, bf16[128,2048]{1,0:T(8,128)(2,1)} %get-tuple-element.199.refs_0_, bf16[128,2048]{1,0:T(8,128)(2,1)} %collective-permute-done.41.refs_1_, bf16[128,2048]{1,0:T(8,128)(2,1)} %copy-done.32, ...), custom_call_target="tpu_custom_call" | custom-call | flops 805306368 | bytes 14680064 | tf_op jit(solution)/shard_map/pick/pallas_call | solution.py:255
  306.6 18.5 %fusion.13 = f32[1536,2048]{1,0:T(8,128)S(1)} fusion(bf16[1536,2048]{1,0:T(8,128)(2,1)} %pick.3, bf16[2048,1024]{1,0:T(8,128)(2,1)} %bitcast.257, bf16[2048,1024]{1,0:T(8,128)(2,1)} %bitcast.260), kind=kOutput, calls=%fused_computation.33 | convolution fusion | flops 12901679104 | bytes 27262976 | tf_op jit(solution)/shard_map/dot_general | solution.py:41
  354.8 13.8 %multiply_convert_fusion.1 = (bf16[1536,1024]{1,0:T(8,128)(2,1)}, bf16[1536,1024]{1,0:T(8,128)(2,1)}) fusion(f32[1536,2048]{1,0:T(8,128)} %copy-done.15, bf16[1536,2048]{1,0:T(8,128)(2,1)S(1)} %bitcast.218, bf16[1,1024,2048]{2,1,0:T(8,128)(2,1)S(1)} %copy-done.70), kind=kOutput, calls=%fused_computation.4 | convolution fusion | flops 6462898176 | bytes 29360128 | tf_op jit(solution)/shard_map/dot_general | solution.py:51
  380.0 10.6 %convolution_convert_fusion.1 = bf16[768,2048]{1,0:T(8,128)(2,1)} fusion(bf16[1536,2048]{1,0:T(8,128)(2,1)S(1)} %pad_maximum_fusion.1, bf16[2048,1024]{1,0:T(8,128)(2,1)} %bitcast.258, bf16[2048,1024]{1,0:T(8,128)(2,1)} %bitcast.261), kind=kOutput, calls=%fused_computation.17 | convolution fusion | flops 6460801024 | bytes 14680064 | tf_op jit(solution)/shard_map/dot_general | solution.py:51
  400.4 10.7 %convolution_convert_fusion = bf16[768,2048]{1,0:T(8,128)(2,1)} fusion(bf16[1536,2048]{1,0:T(8,128)(2,1)S(1)} %pad_maximum_fusion.1, bf16[2048,1024]{1,0:T(8,128)(2,1)} %bitcast.259, bf16[2048,1024]{1,0:T(8,128)(2,1)} %bitcast.262), kind=kOutput, calls=%fused_computation.16 | convolution fusion | flops 6460801024 | bytes 14680064 | tf_op jit(solution)/shard_map/dot_general | solution.py:51
  541.9 21.9 %attend_back.1 = (f32[128,2048]{1,0:T(8,128)}, f32[128,2048]{1,0:T(8,128)}, bf16[128,2048]{1,0:T(8,128)(2,1)}, f32[1,2048]{1,0:T(1,128)}, f32[1,2048]{1,0:T(1,128)}, /*index=5*/f32[128,2]{1,0:T(8,128)}) custom-call(s32[2048,128]{1,0:T(8,128)} %broadcast_in_dim.47.key_seg, s32[1,2048]{1,0:T(1,128)} %bitcast.252, f32[1,2048]{1,0:T(1,128)} %get-tuple-element.249.log_total, ...), custom_call_target="tpu_custom_call" | custom-call | flops 5368709120 | bytes 10485760 | tf_op jit(solution)/shard_map/attend_back/pallas_call | solution.py:733
  580.2 7.7 %collective-permute-done.91.refs_5_ = bf16[256,2048]{1,0:T(8,128)(2,1)} collective-permute-done((bf16[256,2048]{1,0:T(8,128)(2,1)}, bf16[256,2048]{1,0:T(8,128)(2,1)}, u32[]{:S(2)}, u32[]{:S(2)}) %collective-permute-start.91) | collective-permute-done | bytes 1048608 | tf_op jit(solution)/shard_map/ppermute | solution.py:58
  601.7 10.2 %stack_product.1 = f32[384,2048]{1,0:T(8,128)} custom-call(s32[16]{0:T(128)} %pad_add_fusion.order, bf16[384,2048]{1,0:T(8,128)(2,1)} %pad_maximum_fusion.7.left_t.left_next_t, bf16[192,2048]{1,0:T(8,128)(2,1)} %copy-done.3, bf16[192,2048]{1,0:T(8,128)(2,1)} %copy-done.7, bf16[192,2048]{1,0:T(8,128)(2,1)} %copy-done.4, bf16[192,2048]{1,0:T(8,128)(2,1)} %copy-done.5, ...), custom_call_target="tpu_custom_call" | custom-call | flops 3221225472 | bytes 8388608 | tf_op jit(solution)/shard_map/stack_product/pallas_call | solution.py:357
  640.0 7.9 %collective-permute-done.97.refs_7_ = bf16[256,2048]{1,0:T(8,128)(2,1)} collective-permute-done((bf16[256,2048]{1,0:T(8,128)(2,1)}, bf16[256,2048]{1,0:T(8,128)(2,1)}, u32[]{:S(2)}, u32[]{:S(2)}) %collective-permute-start.97) | collective-permute-done | bytes 1048608 | tf_op jit(solution)/shard_map/ppermute | solution.py:58
  704.5 7.5 collective-permute-start.103
  738.8 8.2 %collective-permute-done.110 = bf16[128,2048]{1,0:T(8,128)(2,1)S(1)} collective-permute-done((bf16[128,2048]{1,0:T(8,128)(2,1)S(1)}, bf16[128,2048]{1,0:T(8,128)(2,1)S(1)}, u32[]{:S(2)}, u32[]{:S(2)}) %collective-permute-start.110) | collective-permute-done | bytes 524320 | tf_op jit(solution)/shard_map/ppermute | solution.py:58
  (523 shorter events, 443.4 us)
Async XLA Ops:
  10.6 71.3 %all-to-all-start = ((bf16[16,80,384]{2,1,0:T(8,128)(2,1)}), bf16[16,80,384]{2,1,0:T(8,128)(2,1)}, u32[]{:S(2)}, u32[]{:S(2)}) async-start(bf16[16,80,384]{2,1,0:T(8,128)(2,1)} %copy.91), calls=%async_computation | async-start | bytes 1966080 | tf_op jit(solution)/shard_map/all_to_all | solution.py:847
  18.6 35.2 %collective-permute-start.3 = (bf16[192,2048]{1,0:T(8,128)(2,1)S(1)}, bf16[192,2048]{1,0:T(8,128)(2,1)S(1)}, u32[]{:S(2)}, u32[]{:S(2)}) collective-permute-start(bf16[192,2048]{1,0:T(8,128)(2,1)S(1)} %pad_maximum_fusion.9.refs_0_), channel_id=1, source_target_pairs={{0,4},{1,5},{2,6},{3,7},{4,0},{5,1},{6,2},{7,3},{8,12},{9,13},{10,... | collective-permute-start | bytes 2359304 | tf_op jit(solution)/shard_map/ppermute | solution.py:98
  20.5 33.2 %collective-permute-start.4 = (bf16[192,2048]{1,0:T(8,128)(2,1)S(1)}, bf16[192,2048]{1,0:T(8,128)(2,1)}, u32[]{:S(2)}, u32[]{:S(2)}) collective-permute-start(bf16[192,2048]{1,0:T(8,128)(2,1)S(1)} %pad_maximum_fusion.9.refs_0_), channel_id=1, source_target_pairs={{4,8},{5,9},{6,10},{7,11},{8,4},{9,5},{10,6},{11,7},{20,24},{21,25... | collective-permute-start | bytes 2359304 | tf_op jit(solution)/shard_map/ppermute | solution.py:98
  22.2 31.6 %collective-permute-start.5 = (bf16[192,2048]{1,0:T(8,128)(2,1)S(1)}, bf16[192,2048]{1,0:T(8,128)(2,1)}, u32[]{:S(2)}, u32[]{:S(2)}) collective-permute-start(bf16[192,2048]{1,0:T(8,128)(2,1)S(1)} %pad_maximum_fusion.9.refs_0_), channel_id=1, source_target_pairs={{0,2},{1,3},{2,0},{3,1},{4,6},{5,7},{6,4},{7,5},{8,10},{9,11},{10,... | collective-permute-start | bytes 2359304 | tf_op jit(solution)/shard_map/ppermute | solution.py:98
  23.6 35.4 %collective-permute-start.9 = (bf16[192,2048]{1,0:T(8,128)(2,1)S(1)}, bf16[192,2048]{1,0:T(8,128)(2,1)S(1)}, u32[]{:S(2)}, u32[]{:S(2)}) collective-permute-start(bf16[192,2048]{1,0:T(8,128)(2,1)S(1)} %pad_maximum_fusion.9.refs_0_), channel_id=1, source_target_pairs={{0,1},{1,0},{2,3},{3,2},{4,5},{5,4},{6,7},{7,6},{8,9},{9,8},{10,11... | collective-permute-start | bytes 2359304 | tf_op jit(solution)/shard_map/ppermute | solution.py:98
  58.9 32.3 %collective-permute-start.12 = (bf16[192,2048]{1,0:T(8,128)(2,1)S(1)}, bf16[192,2048]{1,0:T(8,128)(2,1)}, u32[]{:S(2)}, u32[]{:S(2)}) collective-permute-start(bf16[192,2048]{1,0:T(8,128)(2,1)S(1)} %collective-permute-done.3.refs_1_), channel_id=1, source_target_pairs={{0,1},{1,0},{2,3},{3,2},{4,5},{5,4},{6,7},{7,6},{8,9},{9,8},{10,11... | collective-permute-start | bytes 2359304 | tf_op jit(solution)/shard_map/ppermute | solution.py:98
  59.0 32.8 %collective-permute-start.13 = (bf16[192,2048]{1,0:T(8,128)(2,1)}, bf16[192,2048]{1,0:T(8,128)(2,1)}, u32[]{:S(2)}, u32[]{:S(2)}) collective-permute-start(bf16[192,2048]{1,0:T(8,128)(2,1)} %collective-permute-done.5.refs_4_), channel_id=1, source_target_pairs={{0,1},{1,0},{2,3},{3,2},{4,5},{5,4},{6,7},{7,6},{8,9},{9,8},{10,11... | collective-permute-start | bytes 2359304 | tf_op jit(solution)/shard_map/ppermute | solution.py:98
  107.9 35.2 %collective-permute-start = (bf16[128,2048]{1,0:T(8,128)(2,1)S(1)}, bf16[128,2048]{1,0:T(8,128)(2,1)S(1)}, u32[]{:S(2)}, u32[]{:S(2)}) collective-permute-start(bf16[128,2048]{1,0:T(8,128)(2,1)S(1)} %copy-done.19), channel_id=1, source_target_pairs={{0,4},{1,5},{2,6},{3,7},{4,0},{5,1},{6,2},{7,3},{8,12},{9,13},{10,... | collective-permute-start | bytes 1572872 | tf_op jit(solution)/shard_map/ppermute | solution.py:98
  127.2 66.7 %collective-permute-start.33 = (bf16[512,2048]{1,0:T(8,128)(2,1)}, bf16[512,2048]{1,0:T(8,128)(2,1)}, u32[]{:S(2)}, u32[]{:S(2)}) collective-permute-start(bf16[512,2048]{1,0:T(8,128)(2,1)} %tails.1), channel_id=1, source_target_pairs={{0,16},{16,0},{1,17},{17,1},{2,18},{18,2},{3,19},{19,3},{4,20},{20... | collective-permute-start | bytes 6291464 | tf_op jit(solution)/shard_map/ppermute | solution.py:58
  161.6 32.3 %collective-permute-start.31 = (bf16[128,2048]{1,0:T(8,128)(2,1)S(1)}, bf16[128,2048]{1,0:T(8,128)(2,1)S(1)}, u32[]{:S(2)}, u32[]{:S(2)}) collective-permute-start(bf16[128,2048]{1,0:T(8,128)(2,1)S(1)} %collective-permute-done.refs_1_), channel_id=1, source_target_pairs={{0,1},{1,0},{2,3},{3,2},{4,5},{5,4},{6,7},{7,6},{8,9},{9,8},{10,11... | collective-permute-start | bytes 1572872 | tf_op jit(solution)/shard_map/ppermute | solution.py:98
  161.9 32.0 %collective-permute-start.32 = (bf16[128,2048]{1,0:T(8,128)(2,1)}, bf16[128,2048]{1,0:T(8,128)(2,1)S(1)}, u32[]{:S(2)}, u32[]{:S(2)}) collective-permute-start(bf16[128,2048]{1,0:T(8,128)(2,1)} %collective-permute-done.2.refs_4_), channel_id=1, source_target_pairs={{0,1},{1,0},{2,3},{3,2},{4,5},{5,4},{6,7},{7,6},{8,9},{9,8},{10,11... | collective-permute-start | bytes 1572872 | tf_op jit(solution)/shard_map/ppermute | solution.py:98
  340.9 37.2 %collective-permute-start.59 = (bf16[256,2048]{1,0:T(8,128)(2,1)}, bf16[256,2048]{1,0:T(8,128)(2,1)}, u32[]{:S(2)}, u32[]{:S(2)}) collective-permute-start(bf16[256,2048]{1,0:T(8,128)(2,1)} %convolution_convert_fusion.13.refs_0_), channel_id=1, source_target_pairs={{0,16},{16,0},{1,17},{17,1},{2,18},{18,2},{3,19},{19,3},{4,20},{20... | collective-permute-start | bytes 3145736 | tf_op jit(solution)/shard_map/ppermute | solution.py:58
  341.4 54.6 %collective-permute-start.62 = (bf16[256,2048]{1,0:T(8,128)(2,1)}, bf16[256,2048]{1,0:T(8,128)(2,1)}, u32[]{:S(2)}, u32[]{:S(2)}) collective-permute-start(bf16[256,2048]{1,0:T(8,128)(2,1)} %convolution_convert_fusion.12.refs_1_), channel_id=1, source_target_pairs={{0,16},{16,0},{1,17},{17,1},{2,18},{18,2},{3,19},{19,3},{4,20},{20... | collective-permute-start | bytes 3145736 | tf_op jit(solution)/shard_map/ppermute | solution.py:58
  396.0 35.9 %collective-permute-start.63 = (bf16[1024,2048]{1,0:T(8,128)(2,1)}, bf16[1024,2048]{1,0:T(8,128)(2,1)}, u32[]{:S(2)}, u32[]{:S(2)}) collective-permute-start(bf16[1024,2048]{1,0:T(8,128)(2,1)} %bitcast.40), channel_id=1, source_target_pairs={{0,1},{1,0},{2,3},{3,2},{4,5},{5,4},{6,7},{7,6},{8,9},{9,8},{10,11... | collective-permute-start | bytes 12582920 | tf_op jit(solution)/shard_map/ppermute | solution.py:98
  397.0 47.9 %collective-permute-start.73 = (bf16[256,2048]{1,0:T(8,128)(2,1)S(1)}, bf16[256,2048]{1,0:T(8,128)(2,1)}, u32[]{:S(2)}, u32[]{:S(2)}) collective-permute-start(bf16[256,2048]{1,0:T(8,128)(2,1)S(1)} %copy-done.25), channel_id=1, source_target_pairs={{0,16},{16,0},{1,17},{17,1},{2,18},{18,2},{3,19},{19,3},{4,20},{20... | collective-permute-start | bytes 3145736 | tf_op jit(solution)/shard_map/ppermute | solution.py:58
  444.9 38.0 %collective-permute-start.78 = (bf16[256,2048]{1,0:T(8,128)(2,1)S(1)}, bf16[256,2048]{1,0:T(8,128)(2,1)S(1)}, u32[]{:S(2)}, u32[]{:S(2)}) collective-permute-start(bf16[256,2048]{1,0:T(8,128)(2,1)S(1)} %convolution_convert_fusion.9.refs_0_), channel_id=1, source_target_pairs={{0,16},{16,0},{1,17},{17,1},{2,18},{18,2},{3,19},{19,3},{4,20},{20... | collective-permute-start | bytes 3145736 | tf_op jit(solution)/shard_map/ppermute | solution.py:58
  448.6 51.7 %collective-permute-start.81 = (bf16[256,2048]{1,0:T(8,128)(2,1)S(1)}, bf16[256,2048]{1,0:T(8,128)(2,1)S(1)}, u32[]{:S(2)}, u32[]{:S(2)}) collective-permute-start(bf16[256,2048]{1,0:T(8,128)(2,1)S(1)} %convolution_convert_fusion.8.refs_1_), channel_id=1, source_target_pairs={{0,16},{16,0},{1,17},{17,1},{2,18},{18,2},{3,19},{19,3},{4,20},{20... | collective-permute-start | bytes 3145736 | tf_op jit(solution)/shard_map/ppermute | solution.py:58
  483.0 33.2 %collective-permute-start.82 = (bf16[256,2048]{1,0:T(8,128)(2,1)}, bf16[256,2048]{1,0:T(8,128)(2,1)}, u32[]{:S(2)}, u32[]{:S(2)}) collective-permute-start(bf16[256,2048]{1,0:T(8,128)(2,1)} %convolution_convert_fusion.7.refs_2_), channel_id=1, source_target_pairs={{0,16},{16,0},{1,17},{17,1},{2,18},{18,2},{3,19},{19,3},{4,20},{20... | collective-permute-start | bytes 3145736 | tf_op jit(solution)/shard_map/ppermute | solution.py:58
  500.2 39.5 %collective-permute-start.85 = (bf16[256,2048]{1,0:T(8,128)(2,1)}, bf16[256,2048]{1,0:T(8,128)(2,1)}, u32[]{:S(2)}, u32[]{:S(2)}) collective-permute-start(bf16[256,2048]{1,0:T(8,128)(2,1)} %convolution_convert_fusion.6.refs_3_), channel_id=1, source_target_pairs={{0,16},{16,0},{1,17},{17,1},{2,18},{18,2},{3,19},{19,3},{4,20},{20... | collective-permute-start | bytes 3145736 | tf_op jit(solution)/shard_map/ppermute | solution.py:58
  520.5 114.0 %all-gather.2.cloned.1.call-start = ((), (), s32[]{:S(2)}) async-start(), calls=%async_computation.4 | async-start | bytes 8912896 | tf_op jit(solution)/shard_map/all_gather | solution.py:1063
  540.3 47.6 %collective-permute-start.91 = (bf16[256,2048]{1,0:T(8,128)(2,1)}, bf16[256,2048]{1,0:T(8,128)(2,1)}, u32[]{:S(2)}, u32[]{:S(2)}) collective-permute-start(bf16[256,2048]{1,0:T(8,128)(2,1)} %convolution_convert_fusion.4.refs_1_), channel_id=1, source_target_pairs={{0,16},{16,0},{1,17},{17,1},{2,18},{18,2},{3,19},{19,3},{4,20},{20... | collective-permute-start | bytes 3145736 | tf_op jit(solution)/shard_map/ppermute | solution.py:58
  600.0 48.0 %collective-permute-start.97 = (bf16[256,2048]{1,0:T(8,128)(2,1)}, bf16[256,2048]{1,0:T(8,128)(2,1)}, u32[]{:S(2)}, u32[]{:S(2)}) collective-permute-start(bf16[256,2048]{1,0:T(8,128)(2,1)} %convolution_convert_fusion.2.refs_3_), channel_id=1, source_target_pairs={{0,16},{16,0},{1,17},{17,1},{2,18},{18,2},{3,19},{19,3},{4,20},{20... | collective-permute-start | bytes 3145736 | tf_op jit(solution)/shard_map/ppermute | solution.py:58
  617.4 58.0 %all-to-all-start.3 = ((bf16[16,384,128]{2,1,0:T(8,128)(2,1)}), bf16[16,384,128]{2,1,0:T(8,128)(2,1)S(1)}, u32[]{:S(2)}, u32[]{:S(2)}) async-start(bf16[16,384,128]{2,1,0:T(8,128)(2,1)} %bitcast.226), calls=%async_computation.3 | async-start | bytes 3145728 | tf_op jit(solution)/shard_map/all_to_all | solution.py:847
  666.3 36.7 %collective-permute-start.60 = (bf16[128,2048]{1,0:T(8,128)(2,1)}, bf16[128,2048]{1,0:T(8,128)(2,1)}, u32[]{:S(2)}, u32[]{:S(2)}) collective-permute-start(bf16[128,2048]{1,0:T(8,128)(2,1)} %get-tuple-element.325), channel_id=1, source_target_pairs={{0,2},{1,3},{2,0},{3,1},{4,6},{5,7},{6,4},{7,5},{8,10},{9,11},{10,... | collective-permute-start | bytes 1572872 | tf_op jit(solution)/shard_map/ppermute | solution.py:98
  (169 other events, 2866.2 us)
Sparse Core Ops, SparseCore 0:
  539.9 75.2 all-gather.1

commit v4 on v3

--- a/solution.py
+++ b/solution.py
@@ -297,6 +297,7 @@
             bytes_accessed=8 * count * rows * width,
             transcendentals=0,
         ),
+        compiler_params=pltpu.CompilerParams(vmem_limit_bytes=28 * 2**20),
         name="merge",
     )(*own, *far, *before)
 
@@ -327,6 +328,7 @@
             bytes_accessed=2 * (count * (depth + width) + depth * width),
             transcendentals=0,
         ),
+        compiler_params=pltpu.CompilerParams(vmem_limit_bytes=28 * 2**20),
         name="project",
     )(order, left_t, left_t, right)
 
@@ -364,6 +366,7 @@
             bytes_accessed=2 * len(blocks) * rows * width,
             transcendentals=0,
         ),
+        compiler_params=pltpu.CompilerParams(vmem_limit_bytes=28 * 2**20),
         name="stack_product",
     )(order, left_t, *blocks)
 
@@ -926,11 +929,11 @@
     if grouped:
         rounds = gather(jnp.concatenate([normed_in, take(w_out)], axis=0))
         rounds.step()
+        rounds.step(key_seg, cosine, rope_sine, gains)
         (arrived,) = rounds.step(arrived)
         head_w = arrived[:, :taken]
         head_w_far = swap(head_w, "dp", 1)
-        rounds.step(key_seg, cosine, rope_sine, gains)
-        (head_w_far,) = rounds.step(head_w_far)
+        rounds.step()
         blocks = rounds.finish()
         head_w = by_half(jnp.stack([head_w, head_w_far], axis=1), 1).reshape(width, 3 * HEAD_DIM)
         out_far = swap(tails(blocks[: devices // 2], row_count, w_half), "dp", 1)
@@ -962,7 +965,6 @@
         )
     (squares,) = cot_rounds.step(squares)
     squares = butterfly(squares, "expert")
-    (squares,) = cot_rounds.step(squares)
     inverse = lax.rsqrt(squares / width + eps)
     query_t, query, key_t, key, attended, attended_t, log_total = attend(
         query_raw, key_raw, value_t, inverse, gains, cosine, rope_sine, key_seg, query_seg
@@ -972,7 +974,6 @@
         out_cross = send(out_far, swap_core)
 
     attended_low = exchange(my_part(attended, 1).reshape(devices, row_count, part))
-    (attended_low,) = cot_rounds.step(attended_low)
     if grouped:
         middle, normed_mid = out_project(
             where, attended_low, tokens, ffn_gain[None, :], blocks, out_far, out_cross
@@ -982,15 +983,15 @@
         middle = resid_in + mm(attended_low, out_full)
         normed_mid = norm_rows(middle, ffn_gain)[0].astype(jnp.bfloat16)
     (normed_mid,) = cot_rounds.step(normed_mid)
-    cot_blocks = cot_rounds.finish()
 
     mid_rounds = gather(normed_mid)
-    grad_eo = pick(picks, slot_gate, cot_blocks)
     head_w_t = jnp.concatenate(
         [my_part(head_w[:, i * HEAD_DIM : (i + 1) * HEAD_DIM], 1).T for i in range(3)], axis=0
     )
-    grad_eo, head_w_t = mid_rounds.step(grad_eo, head_w_t)
+    (head_w_t,) = mid_rounds.step(head_w_t)
     rows_in = pick(picks, ones, mid_rounds.finish())
+    (rows_in,) = cot_rounds.step(rows_in)
+    grad_eo = pick(picks, slot_gate, cot_rounds.finish())
     gate_up = mm(rows_in, w_both)
     gate_in, up_in = gate_up[:, :ff], gate_up[:, ff:]
     sigmoid_in = jax.nn.sigmoid(gate_in)
@@ -1133,28 +1134,28 @@
         ]
     )
     out_part = mm(my_part(attended_t, 0), branch_all).astype(jnp.bfloat16)
-    gain_parts, out_part = ride(in_rounds, gain_parts, out_part)
+    out_part, w_columns = in_rounds.step(out_part, w_columns)
     out_part_far = dp_start(out_part)
-    if groups == 2:
-        both_total = merge(grad_both[:4], both_far[:4], 2, len(grad_both))
-        w_columns, *both_total = in_rounds.step(w_columns, *both_total)
-    else:
-        in_rounds.step()
     dense = [
         w_columns[:, i * part : (i + 1) * part].reshape(width, w_rows).T for i in range(3)
     ]
-    dense = in_rounds.step(*dense)
     dense_far = [dp_start(values) for values in dense]
     if groups == 2:
+        both_total = merge(grad_both[:4], both_far[:4], 2, len(grad_both))
+        gain_parts, *both_total = ride(in_rounds, gain_parts, *both_total)
         both_total = merge(grad_both[4:], both_far[4:], 2, 4, both_total)
-        gate_total, up_total = in_rounds.step(*both_total)
     else:
         in_rounds.step()
         both_total = both_far[0].astype(jnp.float32)
-        gate_total, up_total = both_total[:, :ff], both_total[:, ff:]
+        both_total = (both_total[:, :ff], both_total[:, ff:])
+    out_part_far, dense_far[0] = in_rounds.step(out_part_far, dense_far[0])
+    dense_far[1], *both_total = in_rounds.step(dense_far[1], *both_total)
+    gate_total, up_total = both_total
     grad_normed_in = in_rounds.finish()
     grad_normed_in, gain_parts = together(grad_normed_in, gain_parts)
-    gain_total = butterfly(butterfly(gain_parts, "expert"), "dp")
+    gain_parts = butterfly(gain_parts, "expert")
+    gain_parts, dense_far[2], gate_total = together(gain_parts, dense_far[2], gate_total)
+    gain_total = butterfly(gain_parts, "dp")
     in_back, _ = norm_back(grad_normed_in, normal_in, inverse_in, attn_gain)
     input_grad = (grad_middle + in_back).astype(jnp.bfloat16)
 

time: 773 us -> 746 us (0.965)
  waiting for transfers between devices: 225 us -> 201 us
  local copies, waits for them, and re-layouts: 28.7 us -> 47.5 us
  Pallas kernels: 127 us -> 112 us
    ppermute x82, waiting for transfers between devices: 178 us -> 147 us  [send(): return lax.ppermute(values, 'expert', pairs)]
    unnamed x158 -> x234, local copies, waits for them, and re-layouts: 10.3 us -> 23.5 us
    all_to_all x4, waiting for transfers between devices: 0.01 us -> 8.85 us  [exchange(): lax.all_to_all(values, 'expert', split_axis=0, concat_axis=0, tiled=True)]
  transfers between devices with their start and end apart: 118 -> 118, of which waited for: 39 -> 42; matrix products, arithmetic and copies ran while one was open for 24% -> 29% of each run, Pallas kernels for 16% -> 14%
where the time goes in v4:
time: 746 us; the launch traced here: 735 us
  waiting for transfers between devices  201 us (27%)
  starting transfers between devices  158 us (21%)
  matrix products  124 us (17%)
  Pallas kernels  112 us (15%)
  other arithmetic  75.4 us (10%)
  local copies, waits for them, and re-layouts  47.5 us (6%)
  between operations  16.1 us (2%)
    ppermute x82, waiting for transfers between devices, send(): return lax.ppermute(values, 'expert', pairs)  147 us
    ppermute x82, starting transfers between devices, send(): return lax.ppermute(values, 'expert', pairs)  103 us
    ppermute x31, waiting for transfers between devices, swap(): return lax.ppermute(values, axis, [(i, i ^ step) for i in range(count)])  45.3 us
    dot_general x12, matrix products, contract_rows(): lax.dot_general(left, right, (((0,), (0,)), ((), ())), preferred_element_...  38.5 us
    dot_general x3, matrix products, contract_cols(): lax.dot_general(left, right, (((1,), (1,)), ((), ())), preferred_element_...  37.6 us
    ppermute x31, starting transfers between devices, swap(): return lax.ppermute(values, axis, [(i, i ^ step) for i in range(count)])  33.5 us
    dot_general x5, matrix products, mm(): return jnp.dot(left, right, preferred_element_type=jnp.float32)  32.6 us
    convert_element_type x18, other arithmetic, add_low(): (left.astype(jnp.float32) + right.astype(jnp.float32)).astype(jnp.bfloat16)  26.2 us
  transfers between devices with their start and end apart: 118, of which 42 were waited for; matrix products, arithmetic and copies ran while one was open for 29% of the time, Pallas kernels for 14%

profile of v4, /device:TPU:0, one launch (start us, length us, event | category | flops | bytes accessed | tf_op | source)
XLA Modules:
  0.0 735.1 jit_solution(3154205634033509624)
XLA Ops:
  25.1 6.7 collective-permute-done.3.refs_1_
  47.2 19.9 %collective-permute-done.7 = bf16[192,2048]{1,0:T(8,128)(2,1)S(1)} collective-permute-done((bf16[192,2048]{1,0:T(8,128)(2,1)}, bf16[192,2048]{1,0:T(8,128)(2,1)S(1)}, u32[]{:S(2)}, u32[]{:S(2)}) %collective-permute-start.7) | collective-permute-done | bytes 786464 | tf_op jit(solution)/shard_map/ppermute | solution.py:98
  73.0 20.4 %collective-permute-done.10 = bf16[192,2048]{1,0:T(8,128)(2,1)} collective-permute-done((bf16[192,2048]{1,0:T(8,128)(2,1)}, bf16[192,2048]{1,0:T(8,128)(2,1)}, u32[]{:S(2)}, u32[]{:S(2)}) %collective-permute-start.10) | collective-permute-done | bytes 786464 | tf_op jit(solution)/shard_map/ppermute | solution.py:98
  100.8 11.6 %collective-permute-done.15.refs_7_ = bf16[192,2048]{1,0:T(8,128)(2,1)S(1)} collective-permute-done((bf16[192,2048]{1,0:T(8,128)(2,1)S(1)}, bf16[192,2048]{1,0:T(8,128)(2,1)S(1)}, u32[]{:S(2)}, u32[]{:S(2)}) %collective-permute-start.15) | collective-permute-done | bytes 786464 | tf_op jit(solution)/shard_map/ppermute | solution.py:98
  130.6 11.3 %heads_in.1 = (f32[128,2048]{1,0:T(8,128)}, f32[128,2048]{1,0:T(8,128)}, bf16[2048,128]{1,0:T(8,128)(2,1)}, bf16[128,2048]{1,0:T(8,128)(2,1)}, f32[2,2048]{1,0:T(2,128)}) custom-call(s32[16]{0:T(128)} %pad_add_fusion.order, bf16[2048,384]{1,0:T(8,128)(2,1)} %bitcast.222, bf16[192,2048]{1,0:T(8,128)(2,1)} %copy-done.2, bf16[192,2048]{1,0:T(8,128)(2,1)} %copy-done.8, ...), custom_call_target="tpu_custom_call" | custom-call | flops 3221225472 | bytes 8388608 | tf_op jit(solution)/shard_map/heads_in/pallas_call | solution.py:395
  158.3 14.7 %attend.1 = (bf16[128,2048]{1,0:T(8,128)(2,1)}, bf16[2048,128]{1,0:T(8,128)(2,1)}, bf16[128,2048]{1,0:T(8,128)(2,1)}, bf16[2048,128]{1,0:T(8,128)(2,1)}, bf16[20...) custom-call(f32[128,2048]{1,0:T(8,128)} %get-tuple-element.179.query_raw, ...), custom_call_target="tpu_custom_call" | custom-call | flops 2147483648 | bytes 6291456 | tf_op jit(solution)/shard_map/attend/pallas_call | solution.py:596
  185.8 8.8 %all-to-all-done.1.attended = bf16[16,128,128]{2,1,0:T(8,128)(2,1)S(1)} async-done(((bf16[16,128,128]{2,1,0:T(8,128)(2,1)}), bf16[16,128,128]{2,1,0:T(8,128)(2,1)S(1)}, u32[]{:S(2)}, u32[]{:S(2)}) %all-to-all-start.1) | async-done | bytes 524320 | tf_op jit(solution)/shard_map/all_to_all | solution.py:850
  223.6 12.6 %collective-permute-done.44 = bf16[128,2048]{1,0:T(8,128)(2,1)S(1)} collective-permute-done((bf16[128,2048]{1,0:T(8,128)(2,1)}, bf16[128,2048]{1,0:T(8,128)(2,1)S(1)}, u32[]{:S(2)}, u32[]{:S(2)}) %collective-permute-start.44) | collective-permute-done | bytes 524320 | tf_op jit(solution)/shard_map/ppermute | solution.py:98
  240.8 9.5 %collective-permute-done.47 = bf16[128,2048]{1,0:T(8,128)(2,1)S(1)} collective-permute-done((bf16[128,2048]{1,0:T(8,128)(2,1)S(1)}, bf16[128,2048]{1,0:T(8,128)(2,1)S(1)}, u32[]{:S(2)}, u32[]{:S(2)}) %collective-permute-start.47) | collective-permute-done | bytes 524320 | tf_op jit(solution)/shard_map/ppermute | solution.py:98
  252.8 8.6 %collective-permute-done.51.refs_7_ = bf16[128,2048]{1,0:T(8,128)(2,1)} collective-permute-done((bf16[128,2048]{1,0:T(8,128)(2,1)S(1)}, bf16[128,2048]{1,0:T(8,128)(2,1)}, u32[]{:S(2)}, u32[]{:S(2)}) %collective-permute-start.51) | collective-permute-done | bytes 524320 | tf_op jit(solution)/shard_map/ppermute | solution.py:98
  269.5 8.2 %pick.2 = bf16[1536,2048]{1,0:T(8,128)(2,1)} custom-call(bf16[16,96,128]{2,1,0:T(8,128)(2,1)} %fusion.55.picks, f32[1536,1]{1,0:T(8,128)} %broadcast_in_dim.82.scale, bf16[128,2048]{1,0:T(8,128)(2,1)} %get-tuple-element.194.refs_0_, bf16[128,2048]{1,0:T(8,128)(2,1)} %collective-permute-done.40.refs_1_, bf16[128,2048]{1,0:T(8,128)(2,1)} %copy-done.77, ...), custom_call_target="tpu_custom_call" | custom-call | flops 805306368 | bytes 14680064 | tf_op jit(solution)/shard_map/pick/pallas_call | solution.py:255
  280.5 18.1 %fusion.13 = f32[1536,2048]{1,0:T(8,128)S(1)} fusion(bf16[1536,2048]{1,0:T(8,128)(2,1)} %pick.2, bf16[2048,1024]{1,0:T(8,128)(2,1)} %bitcast.255, bf16[2048,1024]{1,0:T(8,128)(2,1)} %bitcast.258), kind=kOutput, calls=%fused_computation.33 | convolution fusion | flops 12901679104 | bytes 27262976 | tf_op jit(solution)/shard_map/dot_general | solution.py:41
  304.8 8.3 %pick.3 = bf16[1536,2048]{1,0:T(8,128)(2,1)} custom-call(bf16[16,96,128]{2,1,0:T(8,128)(2,1)} %fusion.55.picks, f32[1536,1]{1,0:T(8,128)} %reshape.372.scale, bf16[128,2048]{1,0:T(8,128)(2,1)} %refs_0_.1, bf16[128,2048]{1,0:T(8,128)(2,1)} %copy-done.84, bf16[128,2048]{1,0:T(8,128)(2,1)} %copy-done.75, bf16[128,2048]{1,0:T(8,128)(2,1)} %broadcast_select_fusion.4.refs_3_, ...), custom_call_target="tpu_custom_call" | custom-call | flops 805306368 | bytes 14680064 | tf_op jit(solution)/shard_map/pick/pallas_call | solution.py:255
  338.6 17.1 %multiply_convert_fusion.1 = (bf16[1536,1024]{1,0:T(8,128)(2,1)}, bf16[1536,1024]{1,0:T(8,128)(2,1)}) fusion(f32[1536,2048]{1,0:T(8,128)} %copy-done.62, bf16[1536,2048]{1,0:T(8,128)(2,1)} %pick.3, bf16[1,1024,2048]{2,1,0:T(8,128)(2,1)} %param.31), kind=kOutput, calls=%fused_computation.4 | convolution fusion | flops 6462898176 | bytes 29360128 | tf_op jit(solution)/shard_map/dot_general | solution.py:51
  355.6 6.5 pad_maximum_fusion.1
  369.0 10.5 %convolution_convert_fusion.1 = bf16[768,2048]{1,0:T(8,128)(2,1)} fusion(bf16[1536,2048]{1,0:T(8,128)(2,1)S(1)} %copy-done.55, bf16[2048,1024]{1,0:T(8,128)(2,1)} %bitcast.256, bf16[2048,1024]{1,0:T(8,128)(2,1)} %bitcast.259), kind=kOutput, calls=%fused_computation.17 | convolution fusion | flops 6460801024 | bytes 14680064 | tf_op jit(solution)/shard_map/dot_general | solution.py:51
  390.4 10.1 %convolution_convert_fusion = bf16[768,2048]{1,0:T(8,128)(2,1)} fusion(bf16[1536,2048]{1,0:T(8,128)(2,1)S(1)} %copy-done.55, bf16[2048,1024]{1,0:T(8,128)(2,1)S(1)} %bitcast.257, bf16[2048,1024]{1,0:T(8,128)(2,1)} %bitcast.260), kind=kOutput, calls=%fused_computation.16 | convolution fusion | flops 6460801024 | bytes 14680064 | tf_op jit(solution)/shard_map/dot_general | solution.py:51
  437.2 7.9 %collective-permute-done.72 = bf16[128,2048]{1,0:T(8,128)(2,1)S(1)} collective-permute-done((bf16[128,2048]{1,0:T(8,128)(2,1)S(1)}, bf16[128,2048]{1,0:T(8,128)(2,1)S(1)}, u32[]{:S(2)}, u32[]{:S(2)}) %collective-permute-start.72) | collective-permute-done | bytes 524320 | tf_op jit(solution)/shard_map/ppermute | solution.py:98
  496.0 7.4 %out_project_back.1 = bf16[16,128,128]{2,1,0:T(8,128)(2,1)} custom-call(s32[17]{0:T(128)} %concatenate.60.where, bf16[128,2048]{1,0:T(8,128)(2,1)} %fusion.82.branch, bf16[192,2048]{1,0:T(8,128)(2,1)} %copy-done.2, bf16[192,2048]{1,0:T(8,128)(2,1)} %copy-done.8, bf16[192,2048]{1,0:T(8,128)(2,1)} %copy-done.4, bf16[192,2048]{1,0:T(8,128)(2,1)} %copy-done.6, ...), custom_call_target="tpu_custom_call" | custom-call | flops 1073741824 | bytes 8388608 | tf_op jit(solution)/shard_map/out_project_back/pallas_call | solution.py:518
  527.4 21.9 %attend_back.1 = (f32[128,2048]{1,0:T(8,128)}, f32[128,2048]{1,0:T(8,128)}, bf16[128,2048]{1,0:T(8,128)(2,1)}, f32[1,2048]{1,0:T(1,128)}, f32[1,2048]{1,0:T(1,128)}, /*index=5*/f32[128,2]{1,0:T(8,128)}) custom-call(s32[2048,128]{1,0:T(8,128)} %broadcast_in_dim.45.key_seg, s32[1,2048]{1,0:T(1,128)} %bitcast.250, f32[1,2048]{1,0:T(1,128)} %get-tuple-element.244.log_total, ...), custom_call_target="tpu_custom_call" | custom-call | flops 5368709120 | bytes 10485760 | tf_op jit(solution)/shard_map/attend_back/pallas_call | solution.py:736
  565.5 7.4 %collective-permute-done.91.refs_5_ = bf16[256,2048]{1,0:T(8,128)(2,1)} collective-permute-done((bf16[256,2048]{1,0:T(8,128)(2,1)}, bf16[256,2048]{1,0:T(8,128)(2,1)}, u32[]{:S(2)}, u32[]{:S(2)}) %collective-permute-start.91) | collective-permute-done | bytes 1048608 | tf_op jit(solution)/shard_map/ppermute | solution.py:58
  589.7 6.5 all-to-all-start.3
  611.2 11.2 %collective-permute-done.93.refs_6_ = bf16[256,2048]{1,0:T(8,128)(2,1)S(1)} collective-permute-done((bf16[256,2048]{1,0:T(8,128)(2,1)}, bf16[256,2048]{1,0:T(8,128)(2,1)S(1)}, u32[]{:S(2)}, u32[]{:S(2)}) %collective-permute-start.93) | collective-permute-done | bytes 1048608 | tf_op jit(solution)/shard_map/ppermute | solution.py:58
  633.2 6.8 collective-permute-done.96
  (597 shorter events, 446.9 us)
Async XLA Ops:
  16.5 30.1 %collective-permute-start.9 = (bf16[192,2048]{1,0:T(8,128)(2,1)S(1)}, bf16[192,2048]{1,0:T(8,128)(2,1)S(1)}, u32[]{:S(2)}, u32[]{:S(2)}) collective-permute-start(bf16[192,2048]{1,0:T(8,128)(2,1)S(1)} %pad_maximum_fusion.9.refs_0_), channel_id=1, source_target_pairs={{0,1},{1,0},{2,3},{3,2},{4,5},{5,4},{6,7},{7,6},{8,9},{9,8},{10,11... | collective-permute-start | bytes 2359304 | tf_op jit(solution)/shard_map/ppermute | solution.py:98
  19.2 53.8 %all-to-all-start = ((bf16[16,80,384]{2,1,0:T(8,128)(2,1)}), bf16[16,80,384]{2,1,0:T(8,128)(2,1)}, u32[]{:S(2)}, u32[]{:S(2)}) async-start(bf16[16,80,384]{2,1,0:T(8,128)(2,1)} %copy.91), calls=%async_computation | async-start | bytes 1966080 | tf_op jit(solution)/shard_map/all_to_all | solution.py:850
  39.9 27.2 %collective-permute-start.8 = (bf16[192,2048]{1,0:T(8,128)(2,1)S(1)}, bf16[192,2048]{1,0:T(8,128)(2,1)}, u32[]{:S(2)}, u32[]{:S(2)}) collective-permute-start(bf16[192,2048]{1,0:T(8,128)(2,1)S(1)} %collective-permute-done.3.refs_1_), channel_id=1, source_target_pairs={{0,2},{1,3},{2,0},{3,1},{4,6},{5,7},{6,4},{7,5},{8,10},{9,11},{10,... | collective-permute-start | bytes 2359304 | tf_op jit(solution)/shard_map/ppermute | solution.py:98
  71.5 27.7 %collective-permute-start.16 = (bf16[192,2048]{1,0:T(8,128)(2,1)S(1)}, bf16[192,2048]{1,0:T(8,128)(2,1)}, u32[]{:S(2)}, u32[]{:S(2)}) collective-permute-start(bf16[192,2048]{1,0:T(8,128)(2,1)S(1)} %broadcast_select_fusion.1.refs_2_), channel_id=1, source_target_pairs={{0,1},{1,0},{2,3},{3,2},{4,5},{5,4},{6,7},{7,6},{8,9},{9,8},{10,11... | collective-permute-start | bytes 2359304 | tf_op jit(solution)/shard_map/ppermute | solution.py:98
  72.4 28.4 %collective-permute-start.18 = (bf16[192,2048]{1,0:T(8,128)(2,1)}, bf16[192,2048]{1,0:T(8,128)(2,1)}, u32[]{:S(2)}, u32[]{:S(2)}) collective-permute-start(bf16[192,2048]{1,0:T(8,128)(2,1)} %collective-permute-done.8.refs_5_), channel_id=1, source_target_pairs={{0,1},{1,0},{2,3},{3,2},{4,5},{5,4},{6,7},{7,6},{8,9},{9,8},{10,11... | collective-permute-start | bytes 2359304 | tf_op jit(solution)/shard_map/ppermute | solution.py:98
  117.3 55.8 %collective-permute-start.29 = (bf16[512,2048]{1,0:T(8,128)(2,1)}, bf16[512,2048]{1,0:T(8,128)(2,1)}, u32[]{:S(2)}, u32[]{:S(2)}) collective-permute-start(bf16[512,2048]{1,0:T(8,128)(2,1)} %tails.1), channel_id=1, source_target_pairs={{0,16},{16,0},{1,17},{17,1},{2,18},{18,2},{3,19},{19,3},{4,20},{20... | collective-permute-start | bytes 6291464 | tf_op jit(solution)/shard_map/ppermute | solution.py:58
  324.3 41.3 %collective-permute-start.59 = (bf16[256,2048]{1,0:T(8,128)(2,1)S(1)}, bf16[256,2048]{1,0:T(8,128)(2,1)S(1)}, u32[]{:S(2)}, u32[]{:S(2)}) collective-permute-start(bf16[256,2048]{1,0:T(8,128)(2,1)S(1)} %convolution_convert_fusion.13.refs_0_), channel_id=1, source_target_pairs={{0,16},{16,0},{1,17},{17,1},{2,18},{18,2},{3,19},{19,3},{4,20},{20... | collective-permute-start | bytes 3145736 | tf_op jit(solution)/shard_map/ppermute | solution.py:58
  324.9 59.9 %collective-permute-start.62 = (bf16[256,2048]{1,0:T(8,128)(2,1)S(1)}, bf16[256,2048]{1,0:T(8,128)(2,1)S(1)}, u32[]{:S(2)}, u32[]{:S(2)}) collective-permute-start(bf16[256,2048]{1,0:T(8,128)(2,1)S(1)} %convolution_convert_fusion.12.refs_1_), channel_id=1, source_target_pairs={{0,16},{16,0},{1,17},{17,1},{2,18},{18,2},{3,19},{19,3},{4,20},{20... | collective-permute-start | bytes 3145736 | tf_op jit(solution)/shard_map/ppermute | solution.py:58
  338.6 27.0 %collective-permute-start.58 = (bf16[1024,2048]{1,0:T(8,128)(2,1)}, bf16[1024,2048]{1,0:T(8,128)(2,1)S(1)}, u32[]{:S(2)}, u32[]{:S(2)}) collective-permute-start(bf16[1024,2048]{1,0:T(8,128)(2,1)} %bitcast.35), channel_id=1, source_target_pairs={{0,1},{1,0},{2,3},{3,2},{4,5},{5,4},{6,7},{7,6},{8,9},{9,8},{10,11... | collective-permute-start | bytes 12582920 | tf_op jit(solution)/shard_map/ppermute | solution.py:98
  384.9 36.4 %collective-permute-start.63 = (bf16[1024,2048]{1,0:T(8,128)(2,1)}, bf16[1024,2048]{1,0:T(8,128)(2,1)}, u32[]{:S(2)}, u32[]{:S(2)}) collective-permute-start(bf16[1024,2048]{1,0:T(8,128)(2,1)} %bitcast.40), channel_id=1, source_target_pairs={{0,1},{1,0},{2,3},{3,2},{4,5},{5,4},{6,7},{7,6},{8,9},{9,8},{10,11... | collective-permute-start | bytes 12582920 | tf_op jit(solution)/shard_map/ppermute | solution.py:98
  385.3 28.8 %collective-permute-start.66 = (bf16[256,2048]{1,0:T(8,128)(2,1)S(1)}, bf16[256,2048]{1,0:T(8,128)(2,1)S(1)}, u32[]{:S(2)}, u32[]{:S(2)}) collective-permute-start(bf16[256,2048]{1,0:T(8,128)(2,1)S(1)} %convolution_convert_fusion.11.refs_2_), channel_id=1, source_target_pairs={{0,16},{16,0},{1,17},{17,1},{2,18},{18,2},{3,19},{19,3},{4,20},{20... | collective-permute-start | bytes 3145736 | tf_op jit(solution)/shard_map/ppermute | solution.py:58
  386.0 47.3 %collective-permute-start.73 = (bf16[256,2048]{1,0:T(8,128)(2,1)S(1)}, bf16[256,2048]{1,0:T(8,128)(2,1)S(1)}, u32[]{:S(2)}, u32[]{:S(2)}) collective-permute-start(bf16[256,2048]{1,0:T(8,128)(2,1)S(1)} %convolution_convert_fusion.10.refs_3_), channel_id=1, source_target_pairs={{0,16},{16,0},{1,17},{17,1},{2,18},{18,2},{3,19},{19,3},{4,20},{20... | collective-permute-start | bytes 3145736 | tf_op jit(solution)/shard_map/ppermute | solution.py:58
  433.2 37.2 %collective-permute-start.78 = (bf16[256,2048]{1,0:T(8,128)(2,1)S(1)}, bf16[256,2048]{1,0:T(8,128)(2,1)S(1)}, u32[]{:S(2)}, u32[]{:S(2)}) collective-permute-start(bf16[256,2048]{1,0:T(8,128)(2,1)S(1)} %convolution_convert_fusion.9.refs_0_), channel_id=1, source_target_pairs={{0,16},{16,0},{1,17},{17,1},{2,18},{18,2},{3,19},{19,3},{4,20},{20... | collective-permute-start | bytes 3145736 | tf_op jit(solution)/shard_map/ppermute | solution.py:58
  436.7 51.1 %collective-permute-start.81 = (bf16[256,2048]{1,0:T(8,128)(2,1)S(1)}, bf16[256,2048]{1,0:T(8,128)(2,1)S(1)}, u32[]{:S(2)}, u32[]{:S(2)}) collective-permute-start(bf16[256,2048]{1,0:T(8,128)(2,1)S(1)} %convolution_convert_fusion.8.refs_1_), channel_id=1, source_target_pairs={{0,16},{16,0},{1,17},{17,1},{2,18},{18,2},{3,19},{19,3},{4,20},{20... | collective-permute-start | bytes 3145736 | tf_op jit(solution)/shard_map/ppermute | solution.py:58
  470.5 33.9 %collective-permute-start.82 = (bf16[256,2048]{1,0:T(8,128)(2,1)}, bf16[256,2048]{1,0:T(8,128)(2,1)}, u32[]{:S(2)}, u32[]{:S(2)}) collective-permute-start(bf16[256,2048]{1,0:T(8,128)(2,1)} %convolution_convert_fusion.7.refs_2_), channel_id=1, source_target_pairs={{0,16},{16,0},{1,17},{17,1},{2,18},{18,2},{3,19},{19,3},{4,20},{20... | collective-permute-start | bytes 3145736 | tf_op jit(solution)/shard_map/ppermute | solution.py:58
  488.8 36.5 %collective-permute-start.85 = (bf16[256,2048]{1,0:T(8,128)(2,1)}, bf16[256,2048]{1,0:T(8,128)(2,1)}, u32[]{:S(2)}, u32[]{:S(2)}) collective-permute-start(bf16[256,2048]{1,0:T(8,128)(2,1)} %convolution_convert_fusion.6.refs_3_), channel_id=1, source_target_pairs={{0,16},{16,0},{1,17},{17,1},{2,18},{18,2},{3,19},{19,3},{4,20},{20... | collective-permute-start | bytes 3145736 | tf_op jit(solution)/shard_map/ppermute | solution.py:58
  508.7 118.8 %all-gather.2.cloned.1.call-start = ((), (), s32[]{:S(2)}) async-start(), calls=%async_computation.4 | async-start | bytes 8912896 | tf_op jit(solution)/shard_map/all_gather | solution.py:1064
  526.0 46.9 %collective-permute-start.91 = (bf16[256,2048]{1,0:T(8,128)(2,1)}, bf16[256,2048]{1,0:T(8,128)(2,1)}, u32[]{:S(2)}, u32[]{:S(2)}) collective-permute-start(bf16[256,2048]{1,0:T(8,128)(2,1)} %convolution_convert_fusion.4.refs_1_), channel_id=1, source_target_pairs={{0,16},{16,0},{1,17},{17,1},{2,18},{18,2},{3,19},{19,3},{4,20},{20... | collective-permute-start | bytes 3145736 | tf_op jit(solution)/shard_map/ppermute | solution.py:58
  581.6 41.8 %collective-permute-start.92 = (bf16[1024,2048]{1,0:T(8,128)(2,1)}, bf16[1024,2048]{1,0:T(8,128)(2,1)}, u32[]{:S(2)}, u32[]{:S(2)}) collective-permute-start(bf16[1024,2048]{1,0:T(8,128)(2,1)} %project.3), channel_id=1, source_target_pairs={{0,1},{1,0},{2,3},{3,2},{4,5},{5,4},{6,7},{7,6},{8,9},{9,8},{10,11... | collective-permute-start | bytes 12582920 | tf_op jit(solution)/shard_map/ppermute | solution.py:98
  589.7 43.5 %all-to-all-start.3 = ((bf16[16,384,128]{2,1,0:T(8,128)(2,1)}), bf16[16,384,128]{2,1,0:T(8,128)(2,1)}, u32[]{:S(2)}, u32[]{:S(2)}) async-start(bf16[16,384,128]{2,1,0:T(8,128)(2,1)} %bitcast.227), calls=%async_computation.3 | async-start | bytes 3145728 | tf_op jit(solution)/shard_map/all_to_all | solution.py:850
  596.6 65.1 %collective-permute-start.98 = (bf16[256,2048]{1,0:T(8,128)(2,1)}, bf16[256,2048]{1,0:T(8,128)(2,1)}, u32[]{:S(2)}, u32[]{:S(2)}) collective-permute-start(bf16[256,2048]{1,0:T(8,128)(2,1)} %convolution_convert_fusion.2.refs_3_), channel_id=1, source_target_pairs={{0,16},{16,0},{1,17},{17,1},{2,18},{18,2},{3,19},{19,3},{4,20},{20... | collective-permute-start | bytes 3145736 | tf_op jit(solution)/shard_map/ppermute | solution.py:58
  601.7 67.4 %collective-permute-start.60 = (bf16[128,2048]{1,0:T(8,128)(2,1)}, bf16[128,2048]{1,0:T(8,128)(2,1)}, u32[]{:S(2)}, u32[]{:S(2)}) collective-permute-start(bf16[128,2048]{1,0:T(8,128)(2,1)} %get-tuple-element.323), channel_id=1, source_target_pairs={{0,2},{1,3},{2,0},{3,1},{4,6},{5,7},{6,4},{7,5},{8,10},{9,11},{10,... | collective-permute-start | bytes 1572872 | tf_op jit(solution)/shard_map/ppermute | solution.py:98
  604.6 65.1 %collective-permute-start.83 = (bf16[128,2048]{1,0:T(8,128)(2,1)}, bf16[128,2048]{1,0:T(8,128)(2,1)}, u32[]{:S(2)}, u32[]{:S(2)}) collective-permute-start(bf16[128,2048]{1,0:T(8,128)(2,1)} %add_convert_fusion.17), channel_id=1, source_target_pairs={{4,8},{5,9},{6,10},{7,11},{8,4},{9,5},{10,6},{11,7},{20,24},{21,25... | collective-permute-start | bytes 1572872 | tf_op jit(solution)/shard_map/ppermute | solution.py:98
  688.4 34.9 %collective-permute-start.111 = (bf16[128,2048]{1,0:T(8,128)(2,1)S(1)}, bf16[128,2048]{1,0:T(8,128)(2,1)S(1)}, u32[]{:S(2)}, u32[]{:S(2)}) collective-permute-start(bf16[128,2048]{1,0:T(8,128)(2,1)S(1)} %bitcast.228), channel_id=1, source_target_pairs={{0,16},{16,0},{1,17},{17,1},{2,18},{18,2},{3,19},{19,3},{4,20},{20... | collective-permute-start | bytes 1572872 | tf_op jit(solution)/shard_map/ppermute | solution.py:58
  (207 other events, 2939.9 us)
Sparse Core Ops, SparseCore 0:
  525.4 74.7 all-gather.1

commit v5 on v4

--- a/solution.py
+++ b/solution.py
@@ -69,8 +69,13 @@
 def butterfly(values, axis):
     step = 1
     while step < lax.axis_size(axis):
-        values = values + swap(values, axis, step)
-        step *= 2
+        if 2 * step < lax.axis_size(axis):
+            one, two, three = [swap(values, axis, times * step) for times in (1, 2, 3)]
+            values = (values + one) + (two + three)
+            step *= 4
+        else:
+            values = values + swap(values, axis, step)
+            step *= 2
     return values
 
 
@@ -200,9 +205,13 @@
     return (left.astype(jnp.float32) + right.astype(jnp.float32)).astype(jnp.bfloat16)
 
 
-def scatter_rounds(make, count, tie):
-    (far,) = yield (send(tie(make(count // 2, count // 2)), swap_core),)
-    close = make(0, count // 2)
+def scatter_rounds(make, count, tie, both_first):
+    far = send(tie(make(count // 2, count // 2)), swap_core)
+    if both_first:
+        far, close = yield (far, make(0, count // 2))
+    else:
+        (far,) = yield (far,)
+        close = make(0, count // 2)
     rows = count // 16
 
     def both(j, k):
@@ -234,7 +243,7 @@
     )
 
 
-def scatter_whole(make, count, tie):
+def scatter_whole(make, count, tie, both_first):
     yield ()
     return lax.psum_scatter(
         tie(make(0, count)), "expert", scatter_dimension=0, tiled=True
@@ -843,8 +852,9 @@
     def gather(block):
         return Rounds(gather_rounds(block) if grouped else gather_whole(block))
 
-    def scatter(make, tie=lambda addends: addends):
-        return Rounds((scatter_rounds if grouped else scatter_whole)(make, seq_length, tie))
+    def scatter(make, tie=lambda addends: addends, both_first=False):
+        kind = scatter_rounds if grouped else scatter_whole
+        return Rounds(kind(make, seq_length, tie, both_first))
 
     def exchange(values):
         return lax.all_to_all(values, "expert", split_axis=0, concat_axis=0, tiled=True)
@@ -1095,7 +1105,6 @@
         )
     (inner,) = cross(inner)
     inner = butterfly(inner, "expert") / width
-    (inner,) = cross(inner)
     grad_raw_t = jnp.concatenate(
         [
             my_part(
@@ -1111,14 +1120,16 @@
         axis=0,
     )
     in_rounds = scatter(
-        lambda first, count: project(order, grad_raw_t, head_w_t, row_count, first, count)
-    )
+        lambda first, count: project(order, grad_raw_t, head_w_t, row_count, first, count),
+        both_first=True,
+    )
+    (grad_raw_t,) = in_rounds.step(grad_raw_t)
     grad_w_t = stack_product(order, grad_raw_t, row_count, blocks)
     grad_attn_gain = jnp.sum(grad_w_t * head_w_t.astype(jnp.float32), axis=0) / attn_gain
+    (grad_w_t,) = ride(in_rounds, grad_w_t)
     w_columns = exchange(
         grad_w_t.astype(jnp.bfloat16).reshape(3 * part, devices, w_rows).transpose(1, 0, 2)
     )
-    ride(in_rounds)
 
     def placed(values):
         return lax.dynamic_update_slice_in_dim(
@@ -1134,22 +1145,25 @@
         ]
     )
     out_part = mm(my_part(attended_t, 0), branch_all).astype(jnp.bfloat16)
-    out_part, w_columns = in_rounds.step(out_part, w_columns)
+    out_part, w_columns = ride(in_rounds, out_part, w_columns)
     out_part_far = dp_start(out_part)
     dense = [
         w_columns[:, i * part : (i + 1) * part].reshape(width, w_rows).T for i in range(3)
     ]
-    dense_far = [dp_start(values) for values in dense]
     if groups == 2:
-        both_total = merge(grad_both[:4], both_far[:4], 2, len(grad_both))
-        gain_parts, *both_total = ride(in_rounds, gain_parts, *both_total)
+        both_total = list(merge(grad_both[:4], both_far[:4], 2, len(grad_both)))
+        gain_parts, both_total[0], both_total[1], *dense = ride(
+            in_rounds, gain_parts, *both_total, *dense
+        )
         both_total = merge(grad_both[4:], both_far[4:], 2, 4, both_total)
     else:
         in_rounds.step()
         both_total = both_far[0].astype(jnp.float32)
         both_total = (both_total[:, :ff], both_total[:, ff:])
-    out_part_far, dense_far[0] = in_rounds.step(out_part_far, dense_far[0])
-    dense_far[1], *both_total = in_rounds.step(dense_far[1], *both_total)
+    dense_far = [dp_start(values) for values in dense]
+    out_part_far, dense_far[0], *both_total = in_rounds.step(
+        out_part_far, dense_far[0], *both_total
+    )
     gate_total, up_total = both_total
     grad_normed_in = in_rounds.finish()
     grad_normed_in, gain_parts = together(grad_normed_in, gain_parts)

time: 746 us -> 736 us (0.987)
  waiting for transfers between devices: 201 us -> 193 us
    ppermute x31 -> x37, waiting for transfers between devices: 45.3 us -> 34.6 us  [swap(): return lax.ppermute(values, axis, [(i, i ^ step) for i in range(count)])]
    unnamed x234 -> x220, local copies, waits for them, and re-layouts: 23.5 us -> 18.9 us
    ppermute x31 -> x37, starting transfers between devices: 33.5 us -> 36.8 us  [swap(): return lax.ppermute(values, axis, [(i, i ^ step) for i in range(count)])]
  transfers between devices with their start and end apart: 118 -> 124, of which waited for: 42 -> 38; matrix products, arithmetic and copies ran while one was open for 29% -> 29% of each run, Pallas kernels for 14% -> 14%
where the time goes in v5:
time: 736 us; the launch traced here: 725 us
  waiting for transfers between devices  193 us (26%)
  starting transfers between devices  165 us (22%)
  matrix products  120 us (16%)
  Pallas kernels  112 us (15%)
  other arithmetic  77.6 us (11%)
  local copies, waits for them, and re-layouts  40.5 us (6%)
  between operations  16.3 us (2%)
    ppermute x82, waiting for transfers between devices, send(): return lax.ppermute(values, 'expert', pairs)  150 us
    ppermute x82, starting transfers between devices, send(): return lax.ppermute(values, 'expert', pairs)  109 us
    dot_general x12, matrix products, contract_rows(): lax.dot_general(left, right, (((0,), (0,)), ((), ())), preferred_element_...  38.4 us
    ppermute x37, starting transfers between devices, swap(): return lax.ppermute(values, axis, [(i, i ^ step) for i in range(count)])  36.8 us
    dot_general x3, matrix products, contract_cols(): lax.dot_general(left, right, (((1,), (1,)), ((), ())), preferred_element_...  35.9 us
    ppermute x37, waiting for transfers between devices, swap(): return lax.ppermute(values, axis, [(i, i ^ step) for i in range(count)])  34.6 us
    dot_general x5, matrix products, mm(): return jnp.dot(left, right, preferred_element_type=jnp.float32)  32.6 us
    convert_element_type x18, other arithmetic, add_low(): (left.astype(jnp.float32) + right.astype(jnp.float32)).astype(jnp.bfloat16)  30.2 us
  transfers between devices with their start and end apart: 124, of which 38 were waited for; matrix products, arithmetic and copies ran while one was open for 29% of the time, Pallas kernels for 14%

profile of v5, /device:TPU:0, one launch (start us, length us, event | category | flops | bytes accessed | tf_op | source)
XLA Modules:
  0.0 725.1 jit_solution(14500864729937182645)
XLA Ops:
  25.1 6.7 collective-permute-done.3.refs_1_
  31.8 6.5 collective-permute-done.5.refs_4_
  47.2 19.9 %collective-permute-done.7 = bf16[192,2048]{1,0:T(8,128)(2,1)S(1)} collective-permute-done((bf16[192,2048]{1,0:T(8,128)(2,1)}, bf16[192,2048]{1,0:T(8,128)(2,1)S(1)}, u32[]{:S(2)}, u32[]{:S(2)}) %collective-permute-start.7) | collective-permute-done | bytes 786464 | tf_op jit(solution)/shard_map/ppermute | solution.py:103
  72.9 20.5 %collective-permute-done.10 = bf16[192,2048]{1,0:T(8,128)(2,1)} collective-permute-done((bf16[192,2048]{1,0:T(8,128)(2,1)}, bf16[192,2048]{1,0:T(8,128)(2,1)}, u32[]{:S(2)}, u32[]{:S(2)}) %collective-permute-start.10) | collective-permute-done | bytes 786464 | tf_op jit(solution)/shard_map/ppermute | solution.py:103
  105.3 7.3 %collective-permute-done.15.refs_7_ = bf16[192,2048]{1,0:T(8,128)(2,1)} collective-permute-done((bf16[192,2048]{1,0:T(8,128)(2,1)S(1)}, bf16[192,2048]{1,0:T(8,128)(2,1)}, u32[]{:S(2)}, u32[]{:S(2)}) %collective-permute-start.15) | collective-permute-done | bytes 786464 | tf_op jit(solution)/shard_map/ppermute | solution.py:103
  124.6 11.3 %heads_in.1 = (f32[128,2048]{1,0:T(8,128)}, f32[128,2048]{1,0:T(8,128)}, bf16[2048,128]{1,0:T(8,128)(2,1)}, bf16[128,2048]{1,0:T(8,128)(2,1)}, f32[2,2048]{1,0:T(2,128)}) custom-call(s32[16]{0:T(128)} %pad_add_fusion.order, bf16[2048,384]{1,0:T(8,128)(2,1)} %bitcast.218, bf16[192,2048]{1,0:T(8,128)(2,1)} %copy-done.2, bf16[192,2048]{1,0:T(8,128)(2,1)} %copy-done.10, ...), custom_call_target="tpu_custom_call" | custom-call | flops 3221225472 | bytes 8388608 | tf_op jit(solution)/shard_map/heads_in/pallas_call | solution.py:404
  155.1 14.7 %attend.1 = (bf16[128,2048]{1,0:T(8,128)(2,1)}, bf16[2048,128]{1,0:T(8,128)(2,1)}, bf16[128,2048]{1,0:T(8,128)(2,1)}, bf16[2048,128]{1,0:T(8,128)(2,1)}, bf16[20...) custom-call(f32[128,2048]{1,0:T(8,128)} %get-tuple-element.183.query_raw, ...), custom_call_target="tpu_custom_call" | custom-call | flops 2147483648 | bytes 6291456 | tf_op jit(solution)/shard_map/attend/pallas_call | solution.py:605
  181.7 8.8 %all-to-all-done.1.attended = bf16[16,128,128]{2,1,0:T(8,128)(2,1)S(1)} async-done(((bf16[16,128,128]{2,1,0:T(8,128)(2,1)}), bf16[16,128,128]{2,1,0:T(8,128)(2,1)S(1)}, u32[]{:S(2)}, u32[]{:S(2)}) %all-to-all-start.1) | async-done | bytes 524320 | tf_op jit(solution)/shard_map/all_to_all | solution.py:860
  192.0 6.5 out_project.1
  219.5 12.6 %collective-permute-done.46 = bf16[128,2048]{1,0:T(8,128)(2,1)S(1)} collective-permute-done((bf16[128,2048]{1,0:T(8,128)(2,1)}, bf16[128,2048]{1,0:T(8,128)(2,1)S(1)}, u32[]{:S(2)}, u32[]{:S(2)}) %collective-permute-start.46) | collective-permute-done | bytes 524320 | tf_op jit(solution)/shard_map/ppermute | solution.py:103
  236.7 9.5 %collective-permute-done.49 = bf16[128,2048]{1,0:T(8,128)(2,1)S(1)} collective-permute-done((bf16[128,2048]{1,0:T(8,128)(2,1)S(1)}, bf16[128,2048]{1,0:T(8,128)(2,1)S(1)}, u32[]{:S(2)}, u32[]{:S(2)}) %collective-permute-start.49) | collective-permute-done | bytes 524320 | tf_op jit(solution)/shard_map/ppermute | solution.py:103
  248.7 8.6 %collective-permute-done.53.refs_7_ = bf16[128,2048]{1,0:T(8,128)(2,1)} collective-permute-done((bf16[128,2048]{1,0:T(8,128)(2,1)S(1)}, bf16[128,2048]{1,0:T(8,128)(2,1)}, u32[]{:S(2)}, u32[]{:S(2)}) %collective-permute-start.53) | collective-permute-done | bytes 524320 | tf_op jit(solution)/shard_map/ppermute | solution.py:103
  265.3 8.2 %pick.2 = bf16[1536,2048]{1,0:T(8,128)(2,1)} custom-call(bf16[16,96,128]{2,1,0:T(8,128)(2,1)} %fusion.55.picks, f32[1536,1]{1,0:T(8,128)} %broadcast_in_dim.82.scale, bf16[128,2048]{1,0:T(8,128)(2,1)} %get-tuple-element.198.refs_0_, bf16[128,2048]{1,0:T(8,128)(2,1)} %collective-permute-done.42.refs_1_, bf16[128,2048]{1,0:T(8,128)(2,1)} %copy-done.72, ...), custom_call_target="tpu_custom_call" | custom-call | flops 805306368 | bytes 14680064 | tf_op jit(solution)/shard_map/pick/pallas_call | solution.py:264
  276.3 18.3 %fusion.13 = f32[1536,2048]{1,0:T(8,128)S(1)} fusion(bf16[1536,2048]{1,0:T(8,128)(2,1)} %pick.2, bf16[2048,1024]{1,0:T(8,128)(2,1)} %bitcast.253, bf16[2048,1024]{1,0:T(8,128)(2,1)} %bitcast.256), kind=kOutput, calls=%fused_computation.33 | convolution fusion | flops 12901679104 | bytes 27262976 | tf_op jit(solution)/shard_map/dot_general | solution.py:41
  300.8 8.3 %pick.3 = bf16[1536,2048]{1,0:T(8,128)(2,1)} custom-call(bf16[16,96,128]{2,1,0:T(8,128)(2,1)} %fusion.55.picks, f32[1536,1]{1,0:T(8,128)} %reshape.372.scale, bf16[128,2048]{1,0:T(8,128)(2,1)} %refs_0_.1, bf16[128,2048]{1,0:T(8,128)(2,1)} %collective-permute-done.refs_1_, bf16[128,2048]{1,0:T(8,128)(2,1)} %copy-done.71, ...), custom_call_target="tpu_custom_call" | custom-call | flops 805306368 | bytes 14680064 | tf_op jit(solution)/shard_map/pick/pallas_call | solution.py:264
  334.4 16.5 %multiply_convert_fusion.1 = (bf16[1536,1024]{1,0:T(8,128)(2,1)S(1)}, bf16[1536,1024]{1,0:T(8,128)(2,1)}) fusion(f32[1536,2048]{1,0:T(8,128)} %copy-done.60, bf16[1536,2048]{1,0:T(8,128)(2,1)} %pick.3, bf16[1,1024,2048]{2,1,0:T(8,128)(2,1)} %param.31), kind=kOutput, calls=%fused_computation.4 | convolution fusion | flops 6462898176 | bytes 29360128 | tf_op jit(solution)/shard_map/dot_general | solution.py:51
  364.4 9.3 %convolution_convert_fusion.1 = bf16[768,2048]{1,0:T(8,128)(2,1)S(1)} fusion(bf16[1536,2048]{1,0:T(8,128)(2,1)S(1)} %copy-done.53, bf16[2048,1024]{1,0:T(8,128)(2,1)} %bitcast.254, bf16[2048,1024]{1,0:T(8,128)(2,1)} %bitcast.257), kind=kOutput, calls=%fused_computation.17 | convolution fusion | flops 6460801024 | bytes 14680064 | tf_op jit(solution)/shard_map/dot_general | solution.py:51
  382.8 10.1 %convolution_convert_fusion = bf16[768,2048]{1,0:T(8,128)(2,1)} fusion(bf16[1536,2048]{1,0:T(8,128)(2,1)S(1)} %copy-done.53, bf16[2048,1024]{1,0:T(8,128)(2,1)S(1)} %bitcast.255, bf16[2048,1024]{1,0:T(8,128)(2,1)} %bitcast.258), kind=kOutput, calls=%fused_computation.16 | convolution fusion | flops 6460801024 | bytes 14680064 | tf_op jit(solution)/shard_map/dot_general | solution.py:51
  431.3 8.5 %collective-permute-done.74 = bf16[128,2048]{1,0:T(8,128)(2,1)S(1)} collective-permute-done((bf16[128,2048]{1,0:T(8,128)(2,1)S(1)}, bf16[128,2048]{1,0:T(8,128)(2,1)S(1)}, u32[]{:S(2)}, u32[]{:S(2)}) %collective-permute-start.74) | collective-permute-done | bytes 524320 | tf_op jit(solution)/shard_map/ppermute | solution.py:103
  491.8 7.4 %out_project_back.1 = bf16[16,128,128]{2,1,0:T(8,128)(2,1)} custom-call(s32[17]{0:T(128)} %concatenate.60.where, bf16[128,2048]{1,0:T(8,128)(2,1)} %fusion.82.branch, bf16[192,2048]{1,0:T(8,128)(2,1)} %copy-done.2, bf16[192,2048]{1,0:T(8,128)(2,1)} %copy-done.10, bf16[192,2048]{1,0:T(8,128)(2,1)} %copy-done.4, bf16[192,2048]{1,0:T(8,128)(2,1)} %copy-done.6, ...), custom_call_target="tpu_custom_call" | custom-call | flops 1073741824 | bytes 8388608 | tf_op jit(solution)/shard_map/out_project_back/pallas_call | solution.py:527
  520.2 21.9 %attend_back.1 = (f32[128,2048]{1,0:T(8,128)}, f32[128,2048]{1,0:T(8,128)}, bf16[128,2048]{1,0:T(8,128)(2,1)}, f32[1,2048]{1,0:T(1,128)}, f32[1,2048]{1,0:T(1,128)}, /*index=5*/f32[128,2]{1,0:T(8,128)}) custom-call(s32[2048,128]{1,0:T(8,128)} %broadcast_in_dim.45.key_seg, s32[1,2048]{1,0:T(1,128)} %bitcast.248, f32[1,2048]{1,0:T(1,128)} %get-tuple-element.248.log_total, ...), custom_call_target="tpu_custom_call" | custom-call | flops 5368709120 | bytes 10485760 | tf_op jit(solution)/shard_map/attend_back/pallas_call | solution.py:745
  582.4 9.2 %collective-permute-done.99.refs_5_ = bf16[256,2048]{1,0:T(8,128)(2,1)S(1)} collective-permute-done((bf16[256,2048]{1,0:T(8,128)(2,1)S(1)}, bf16[256,2048]{1,0:T(8,128)(2,1)S(1)}, u32[]{:S(2)}, u32[]{:S(2)}) %collective-permute-start.99) | collective-permute-done | bytes 1048608 | tf_op jit(solution)/shard_map/ppermute | solution.py:58
  628.3 13.2 %collective-permute-done.97 = bf16[128,2048]{1,0:T(8,128)(2,1)} collective-permute-done((bf16[128,2048]{1,0:T(8,128)(2,1)}, bf16[128,2048]{1,0:T(8,128)(2,1)}, u32[]{:S(2)}, u32[]{:S(2)}) %collective-permute-start.97) | collective-permute-done | bytes 524320 | tf_op jit(solution)/shard_map/ppermute | solution.py:103
  670.9 8.3 %collective-permute-start.107 = (bf16[128,2048]{1,0:T(8,128)(2,1)S(1)}, bf16[128,2048]{1,0:T(8,128)(2,1)S(1)}, u32[]{:S(2)}, u32[]{:S(2)}) collective-permute-start(bf16[128,2048]{1,0:T(8,128)(2,1)S(1)} %get-tuple-element.324), channel_id=1, source_target_pairs={{0,4},{1,5},{2,6},{3,7},{4,0},{5,1},{6,2},{7,3},{8,12},{9,13},{10,... | collective-permute-start | bytes 1572872 | tf_op jit(solution)/shard_map/ppermute | solution.py:103
  (589 shorter events, 436.6 us)
Async XLA Ops:
  16.5 30.2 %collective-permute-start.9 = (bf16[192,2048]{1,0:T(8,128)(2,1)S(1)}, bf16[192,2048]{1,0:T(8,128)(2,1)S(1)}, u32[]{:S(2)}, u32[]{:S(2)}) collective-permute-start(bf16[192,2048]{1,0:T(8,128)(2,1)S(1)} %pad_maximum_fusion.9.refs_0_), channel_id=1, source_target_pairs={{0,1},{1,0},{2,3},{3,2},{4,5},{5,4},{6,7},{7,6},{8,9},{9,8},{10,11... | collective-permute-start | bytes 2359304 | tf_op jit(solution)/shard_map/ppermute | solution.py:103
  19.2 53.7 %all-to-all-start = ((bf16[16,80,384]{2,1,0:T(8,128)(2,1)}), bf16[16,80,384]{2,1,0:T(8,128)(2,1)}, u32[]{:S(2)}, u32[]{:S(2)}) async-start(bf16[16,80,384]{2,1,0:T(8,128)(2,1)} %copy.91), calls=%async_computation | async-start | bytes 1966080 | tf_op jit(solution)/shard_map/all_to_all | solution.py:860
  39.9 27.2 %collective-permute-start.8 = (bf16[192,2048]{1,0:T(8,128)(2,1)S(1)}, bf16[192,2048]{1,0:T(8,128)(2,1)}, u32[]{:S(2)}, u32[]{:S(2)}) collective-permute-start(bf16[192,2048]{1,0:T(8,128)(2,1)S(1)} %collective-permute-done.3.refs_1_), channel_id=1, source_target_pairs={{0,2},{1,3},{2,0},{3,1},{4,6},{5,7},{6,4},{7,5},{8,10},{9,11},{10,... | collective-permute-start | bytes 2359304 | tf_op jit(solution)/shard_map/ppermute | solution.py:103
  46.7 26.2 %collective-permute-start.13 = (bf16[192,2048]{1,0:T(8,128)(2,1)S(1)}, bf16[192,2048]{1,0:T(8,128)(2,1)}, u32[]{:S(2)}, u32[]{:S(2)}) collective-permute-start(bf16[192,2048]{1,0:T(8,128)(2,1)S(1)} %collective-permute-done.5.refs_4_), channel_id=1, source_target_pairs={{0,1},{1,0},{2,3},{3,2},{4,5},{5,4},{6,7},{7,6},{8,9},{9,8},{10,11... | collective-permute-start | bytes 2359304 | tf_op jit(solution)/shard_map/ppermute | solution.py:103
  71.5 27.7 %collective-permute-start.16 = (bf16[192,2048]{1,0:T(8,128)(2,1)S(1)}, bf16[192,2048]{1,0:T(8,128)(2,1)}, u32[]{:S(2)}, u32[]{:S(2)}) collective-permute-start(bf16[192,2048]{1,0:T(8,128)(2,1)S(1)} %broadcast_select_fusion.1.refs_2_), channel_id=1, source_target_pairs={{0,1},{1,0},{2,3},{3,2},{4,5},{5,4},{6,7},{7,6},{8,9},{9,8},{10,11... | collective-permute-start | bytes 2359304 | tf_op jit(solution)/shard_map/ppermute | solution.py:103
  72.4 29.1 %collective-permute-start.18 = (bf16[192,2048]{1,0:T(8,128)(2,1)}, bf16[192,2048]{1,0:T(8,128)(2,1)}, u32[]{:S(2)}, u32[]{:S(2)}) collective-permute-start(bf16[192,2048]{1,0:T(8,128)(2,1)} %collective-permute-done.8.refs_5_), channel_id=1, source_target_pairs={{0,1},{1,0},{2,3},{3,2},{4,5},{5,4},{6,7},{7,6},{8,9},{9,8},{10,11... | collective-permute-start | bytes 2359304 | tf_op jit(solution)/shard_map/ppermute | solution.py:103
  101.5 34.4 %collective-permute-start = (bf16[128,2048]{1,0:T(8,128)(2,1)}, bf16[128,2048]{1,0:T(8,128)(2,1)}, u32[]{:S(2)}, u32[]{:S(2)}) collective-permute-start(bf16[128,2048]{1,0:T(8,128)(2,1)} %refs_0_.1), channel_id=1, source_target_pairs={{0,4},{1,5},{2,6},{3,7},{4,0},{5,1},{6,2},{7,3},{8,12},{9,13},{10,... | collective-permute-start | bytes 1572872 | tf_op jit(solution)/shard_map/ppermute | solution.py:103
  117.0 52.9 %collective-permute-start.31 = (bf16[512,2048]{1,0:T(8,128)(2,1)}, bf16[512,2048]{1,0:T(8,128)(2,1)}, u32[]{:S(2)}, u32[]{:S(2)}) collective-permute-start(bf16[512,2048]{1,0:T(8,128)(2,1)} %tails.1), channel_id=1, source_target_pairs={{0,16},{16,0},{1,17},{17,1},{2,18},{18,2},{3,19},{19,3},{4,20},{20... | collective-permute-start | bytes 6291464 | tf_op jit(solution)/shard_map/ppermute | solution.py:58
  320.4 39.5 %collective-permute-start.61 = (bf16[256,2048]{1,0:T(8,128)(2,1)S(1)}, bf16[256,2048]{1,0:T(8,128)(2,1)S(1)}, u32[]{:S(2)}, u32[]{:S(2)}) collective-permute-start(bf16[256,2048]{1,0:T(8,128)(2,1)S(1)} %convolution_convert_fusion.13.refs_0_), channel_id=1, source_target_pairs={{0,16},{16,0},{1,17},{17,1},{2,18},{18,2},{3,19},{19,3},{4,20},{20... | collective-permute-start | bytes 3145736 | tf_op jit(solution)/shard_map/ppermute | solution.py:58
  320.9 56.2 %collective-permute-start.64 = (bf16[256,2048]{1,0:T(8,128)(2,1)S(1)}, bf16[256,2048]{1,0:T(8,128)(2,1)S(1)}, u32[]{:S(2)}, u32[]{:S(2)}) collective-permute-start(bf16[256,2048]{1,0:T(8,128)(2,1)S(1)} %convolution_convert_fusion.12.refs_1_), channel_id=1, source_target_pairs={{0,16},{16,0},{1,17},{17,1},{2,18},{18,2},{3,19},{19,3},{4,20},{20... | collective-permute-start | bytes 3145736 | tf_op jit(solution)/shard_map/ppermute | solution.py:58
  377.5 36.8 %collective-permute-start.65 = (bf16[1024,2048]{1,0:T(8,128)(2,1)}, bf16[1024,2048]{1,0:T(8,128)(2,1)}, u32[]{:S(2)}, u32[]{:S(2)}) collective-permute-start(bf16[1024,2048]{1,0:T(8,128)(2,1)} %bitcast.40), channel_id=1, source_target_pairs={{0,1},{1,0},{2,3},{3,2},{4,5},{5,4},{6,7},{7,6},{8,9},{9,8},{10,11... | collective-permute-start | bytes 12582920 | tf_op jit(solution)/shard_map/ppermute | solution.py:103
  377.7 29.0 %collective-permute-start.68 = (bf16[256,2048]{1,0:T(8,128)(2,1)S(1)}, bf16[256,2048]{1,0:T(8,128)(2,1)S(1)}, u32[]{:S(2)}, u32[]{:S(2)}) collective-permute-start(bf16[256,2048]{1,0:T(8,128)(2,1)S(1)} %convolution_convert_fusion.11.refs_2_), channel_id=1, source_target_pairs={{0,16},{16,0},{1,17},{17,1},{2,18},{18,2},{3,19},{19,3},{4,20},{20... | collective-permute-start | bytes 3145736 | tf_op jit(solution)/shard_map/ppermute | solution.py:58
  378.2 49.2 %collective-permute-start.75 = (bf16[256,2048]{1,0:T(8,128)(2,1)S(1)}, bf16[256,2048]{1,0:T(8,128)(2,1)S(1)}, u32[]{:S(2)}, u32[]{:S(2)}) collective-permute-start(bf16[256,2048]{1,0:T(8,128)(2,1)S(1)} %convolution_convert_fusion.10.refs_3_), channel_id=1, source_target_pairs={{0,16},{16,0},{1,17},{17,1},{2,18},{18,2},{3,19},{19,3},{4,20},{20... | collective-permute-start | bytes 3145736 | tf_op jit(solution)/shard_map/ppermute | solution.py:58
  427.4 38.3 %collective-permute-start.80 = (bf16[256,2048]{1,0:T(8,128)(2,1)S(1)}, bf16[256,2048]{1,0:T(8,128)(2,1)S(1)}, u32[]{:S(2)}, u32[]{:S(2)}) collective-permute-start(bf16[256,2048]{1,0:T(8,128)(2,1)S(1)} %convolution_convert_fusion.9.refs_0_), channel_id=1, source_target_pairs={{0,16},{16,0},{1,17},{17,1},{2,18},{18,2},{3,19},{19,3},{4,20},{20... | collective-permute-start | bytes 3145736 | tf_op jit(solution)/shard_map/ppermute | solution.py:58
  430.9 52.7 %collective-permute-start.83 = (bf16[256,2048]{1,0:T(8,128)(2,1)S(1)}, bf16[256,2048]{1,0:T(8,128)(2,1)S(1)}, u32[]{:S(2)}, u32[]{:S(2)}) collective-permute-start(bf16[256,2048]{1,0:T(8,128)(2,1)S(1)} %convolution_convert_fusion.8.refs_1_), channel_id=1, source_target_pairs={{0,16},{16,0},{1,17},{17,1},{2,18},{18,2},{3,19},{19,3},{4,20},{20... | collective-permute-start | bytes 3145736 | tf_op jit(solution)/shard_map/ppermute | solution.py:58
  465.7 33.5 %collective-permute-start.84 = (bf16[256,2048]{1,0:T(8,128)(2,1)}, bf16[256,2048]{1,0:T(8,128)(2,1)}, u32[]{:S(2)}, u32[]{:S(2)}) collective-permute-start(bf16[256,2048]{1,0:T(8,128)(2,1)} %convolution_convert_fusion.7.refs_2_), channel_id=1, source_target_pairs={{0,16},{16,0},{1,17},{17,1},{2,18},{18,2},{3,19},{19,3},{4,20},{20... | collective-permute-start | bytes 3145736 | tf_op jit(solution)/shard_map/ppermute | solution.py:58
  484.6 34.8 %collective-permute-start.87 = (bf16[256,2048]{1,0:T(8,128)(2,1)}, bf16[256,2048]{1,0:T(8,128)(2,1)}, u32[]{:S(2)}, u32[]{:S(2)}) collective-permute-start(bf16[256,2048]{1,0:T(8,128)(2,1)} %convolution_convert_fusion.6.refs_3_), channel_id=1, source_target_pairs={{0,16},{16,0},{1,17},{17,1},{2,18},{18,2},{3,19},{19,3},{4,20},{20... | collective-permute-start | bytes 3145736 | tf_op jit(solution)/shard_map/ppermute | solution.py:58
  503.4 119.2 %all-gather.2.cloned.1.call-start = ((), (), s32[]{:S(2)}) async-start(), calls=%async_computation.4 | async-start | bytes 8912896 | tf_op jit(solution)/shard_map/all_gather | solution.py:1074
  519.4 25.7 %collective-permute-start.88 = (bf16[256,2048]{1,0:T(8,128)(2,1)S(1)}, bf16[256,2048]{1,0:T(8,128)(2,1)}, u32[]{:S(2)}, u32[]{:S(2)}) collective-permute-start(bf16[256,2048]{1,0:T(8,128)(2,1)S(1)} %convolution_convert_fusion.5.refs_0_), channel_id=1, source_target_pairs={{0,16},{16,0},{1,17},{17,1},{2,18},{18,2},{3,19},{19,3},{4,20},{20... | collective-permute-start | bytes 3145736 | tf_op jit(solution)/shard_map/ppermute | solution.py:58
  594.1 47.4 %all-to-all-start.3 = ((bf16[16,384,128]{2,1,0:T(8,128)(2,1)}), bf16[16,384,128]{2,1,0:T(8,128)(2,1)}, u32[]{:S(2)}, u32[]{:S(2)}) async-start(bf16[16,384,128]{2,1,0:T(8,128)(2,1)} %bitcast_bitcast_fusion), calls=%async_computation.3 | async-start | bytes 3145728 | tf_op jit(solution)/shard_map/all_to_all | solution.py:860
  599.0 29.3 %collective-permute-start.101 = (bf16[256,2048]{1,0:T(8,128)(2,1)}, bf16[256,2048]{1,0:T(8,128)(2,1)}, u32[]{:S(2)}, u32[]{:S(2)}) collective-permute-start(bf16[256,2048]{1,0:T(8,128)(2,1)} %convolution_convert_fusion.3.refs_2_), channel_id=1, source_target_pairs={{0,16},{16,0},{1,17},{17,1},{2,18},{18,2},{3,19},{19,3},{4,20},{20... | collective-permute-start | bytes 3145736 | tf_op jit(solution)/shard_map/ppermute | solution.py:58
  599.3 62.1 %collective-permute-start.105 = (bf16[256,2048]{1,0:T(8,128)(2,1)}, bf16[256,2048]{1,0:T(8,128)(2,1)}, u32[]{:S(2)}, u32[]{:S(2)}) collective-permute-start(bf16[256,2048]{1,0:T(8,128)(2,1)} %convolution_convert_fusion.2.refs_3_), channel_id=1, source_target_pairs={{0,16},{16,0},{1,17},{17,1},{2,18},{18,2},{3,19},{19,3},{4,20},{20... | collective-permute-start | bytes 3145736 | tf_op jit(solution)/shard_map/ppermute | solution.py:58
  604.4 65.7 %collective-permute-start.62 = (bf16[128,2048]{1,0:T(8,128)(2,1)}, bf16[128,2048]{1,0:T(8,128)(2,1)}, u32[]{:S(2)}, u32[]{:S(2)}) collective-permute-start(bf16[128,2048]{1,0:T(8,128)(2,1)} %get-tuple-element.331), channel_id=1, source_target_pairs={{0,2},{1,3},{2,0},{3,1},{4,6},{5,7},{6,4},{7,5},{8,10},{9,11},{10,... | collective-permute-start | bytes 1572872 | tf_op jit(solution)/shard_map/ppermute | solution.py:103
  685.2 28.0 %collective-permute-start.116 = (bf16[128,2048]{1,0:T(8,128)(2,1)S(1)}, bf16[128,2048]{1,0:T(8,128)(2,1)S(1)}, u32[]{:S(2)}, u32[]{:S(2)}) collective-permute-start(bf16[128,2048]{1,0:T(8,128)(2,1)S(1)} %bitcast.223), channel_id=1, source_target_pairs={{0,16},{16,0},{1,17},{17,1},{2,18},{18,2},{3,19},{19,3},{4,20},{20... | collective-permute-start | bytes 1572872 | tf_op jit(solution)/shard_map/ppermute | solution.py:58
  (206 other events, 3417.6 us)
Sparse Core Ops, SparseCore 0:
  519.5 76.6 all-gather.1

commit v6 on v5

--- a/solution.py
+++ b/solution.py
@@ -1145,22 +1145,20 @@
         ]
     )
     out_part = mm(my_part(attended_t, 0), branch_all).astype(jnp.bfloat16)
-    out_part, w_columns = ride(in_rounds, out_part, w_columns)
-    out_part_far = dp_start(out_part)
     dense = [
         w_columns[:, i * part : (i + 1) * part].reshape(width, w_rows).T for i in range(3)
     ]
+    out_part, *dense = ride(in_rounds, out_part, *dense)
+    out_part_far = dp_start(out_part)
+    dense_far = [dp_start(values) for values in dense]
     if groups == 2:
         both_total = list(merge(grad_both[:4], both_far[:4], 2, len(grad_both)))
-        gain_parts, both_total[0], both_total[1], *dense = ride(
-            in_rounds, gain_parts, *both_total, *dense
-        )
+        gain_parts, both_total[0], both_total[1] = ride(in_rounds, gain_parts, *both_total)
         both_total = merge(grad_both[4:], both_far[4:], 2, 4, both_total)
     else:
         in_rounds.step()
         both_total = both_far[0].astype(jnp.float32)
         both_total = (both_total[:, :ff], both_total[:, ff:])
-    dense_far = [dp_start(values) for values in dense]
     out_part_far, dense_far[0], *both_total = in_rounds.step(
         out_part_far, dense_far[0], *both_total
     )

time: 736 us -> 746 us (1.014)
  waiting for transfers between devices: 193 us -> 210 us
  other arithmetic: 77.6 us -> 69.5 us
    ppermute x37, waiting for transfers between devices: 34.6 us -> 44.5 us  [swap(): return lax.ppermute(values, axis, [(i, i ^ step) for i in range(count)])]
    all_to_all x4, waiting for transfers between devices: 8.82 us -> 17.3 us  [exchange(): lax.all_to_all(values, 'expert', split_axis=0, concat_axis=0, tiled=True)]
    unnamed x220 -> x228, local copies, waits for them, and re-layouts: 18.9 us -> 20.2 us
  transfers between devices with their start and end apart: 124 -> 124, of which waited for: 38 -> 42; matrix products, arithmetic and copies ran while one was open for 29% -> 28% of each run, Pallas kernels for 14% -> 14%
where the time goes in v6:
time: 746 us; the launch traced here: 735 us
  waiting for transfers between devices  210 us (28%)
  starting transfers between devices  166 us (22%)
  matrix products  120 us (16%)
  Pallas kernels  111 us (15%)
  other arithmetic  69.5 us (9%)
  local copies, waits for them, and re-layouts  42.8 us (6%)
  between operations  16.5 us (2%)
    ppermute x82, waiting for transfers between devices, send(): return lax.ppermute(values, 'expert', pairs)  148 us
    ppermute x82, starting transfers between devices, send(): return lax.ppermute(values, 'expert', pairs)  108 us
    ppermute x37, waiting for transfers between devices, swap(): return lax.ppermute(values, axis, [(i, i ^ step) for i in range(count)])  44.5 us
    ppermute x37, starting transfers between devices, swap(): return lax.ppermute(values, axis, [(i, i ^ step) for i in range(count)])  38.5 us
    dot_general x12, matrix products, contract_rows(): lax.dot_general(left, right, (((0,), (0,)), ((), ())), preferred_element_...  38.5 us
    dot_general x3, matrix products, contract_cols(): lax.dot_general(left, right, (((1,), (1,)), ((), ())), preferred_element_...  35.9 us
    dot_general x5, matrix products, mm(): return jnp.dot(left, right, preferred_element_type=jnp.float32)  31.9 us
    convert_element_type x18, other arithmetic, add_low(): (left.astype(jnp.float32) + right.astype(jnp.float32)).astype(jnp.bfloat16)  23.4 us
  transfers between devices with their start and end apart: 124, of which 42 were waited for; matrix products, arithmetic and copies ran while one was open for 28% of the time, Pallas kernels for 14%

profile of v6, /device:TPU:0, one launch (start us, length us, event | category | flops | bytes accessed | tf_op | source)
XLA Modules:
  0.0 735.3 jit_solution(11613647450140172620)
XLA Ops:
  25.1 6.7 collective-permute-done.3.refs_1_
  47.2 19.9 %collective-permute-done.7 = bf16[192,2048]{1,0:T(8,128)(2,1)S(1)} collective-permute-done((bf16[192,2048]{1,0:T(8,128)(2,1)}, bf16[192,2048]{1,0:T(8,128)(2,1)S(1)}, u32[]{:S(2)}, u32[]{:S(2)}) %collective-permute-start.7) | collective-permute-done | bytes 786464 | tf_op jit(solution)/shard_map/ppermute | solution.py:103
  72.9 20.5 %collective-permute-done.10 = bf16[192,2048]{1,0:T(8,128)(2,1)} collective-permute-done((bf16[192,2048]{1,0:T(8,128)(2,1)}, bf16[192,2048]{1,0:T(8,128)(2,1)}, u32[]{:S(2)}, u32[]{:S(2)}) %collective-permute-start.10) | collective-permute-done | bytes 786464 | tf_op jit(solution)/shard_map/ppermute | solution.py:103
  105.3 7.3 collective-permute-done.15.refs_7_
  124.7 11.3 %heads_in.1 = (f32[128,2048]{1,0:T(8,128)}, f32[128,2048]{1,0:T(8,128)}, bf16[2048,128]{1,0:T(8,128)(2,1)}, bf16[128,2048]{1,0:T(8,128)(2,1)}, f32[2,2048]{1,0:T(2,128)}) custom-call(s32[16]{0:T(128)} %pad_add_fusion.order, bf16[2048,384]{1,0:T(8,128)(2,1)} %bitcast.218, bf16[192,2048]{1,0:T(8,128)(2,1)} %copy-done.2, bf16[192,2048]{1,0:T(8,128)(2,1)} %copy-done.10, ...), custom_call_target="tpu_custom_call" | custom-call | flops 3221225472 | bytes 8388608 | tf_op jit(solution)/shard_map/heads_in/pallas_call | solution.py:404
  155.2 14.8 %attend.1 = (bf16[128,2048]{1,0:T(8,128)(2,1)}, bf16[2048,128]{1,0:T(8,128)(2,1)}, bf16[128,2048]{1,0:T(8,128)(2,1)}, bf16[2048,128]{1,0:T(8,128)(2,1)}, bf16[20...) custom-call(f32[128,2048]{1,0:T(8,128)} %get-tuple-element.182.query_raw, ...), custom_call_target="tpu_custom_call" | custom-call | flops 2147483648 | bytes 6291456 | tf_op jit(solution)/shard_map/attend/pallas_call | solution.py:605
  181.9 8.8 %all-to-all-done.1.attended = bf16[16,128,128]{2,1,0:T(8,128)(2,1)S(1)} async-done(((bf16[16,128,128]{2,1,0:T(8,128)(2,1)}), bf16[16,128,128]{2,1,0:T(8,128)(2,1)S(1)}, u32[]{:S(2)}, u32[]{:S(2)}) %all-to-all-start.1) | async-done | bytes 524320 | tf_op jit(solution)/shard_map/all_to_all | solution.py:860
  219.7 12.6 %collective-permute-done.46 = bf16[128,2048]{1,0:T(8,128)(2,1)S(1)} collective-permute-done((bf16[128,2048]{1,0:T(8,128)(2,1)}, bf16[128,2048]{1,0:T(8,128)(2,1)S(1)}, u32[]{:S(2)}, u32[]{:S(2)}) %collective-permute-start.46) | collective-permute-done | bytes 524320 | tf_op jit(solution)/shard_map/ppermute | solution.py:103
  236.9 9.4 %collective-permute-done.49 = bf16[128,2048]{1,0:T(8,128)(2,1)S(1)} collective-permute-done((bf16[128,2048]{1,0:T(8,128)(2,1)S(1)}, bf16[128,2048]{1,0:T(8,128)(2,1)S(1)}, u32[]{:S(2)}, u32[]{:S(2)}) %collective-permute-start.49) | collective-permute-done | bytes 524320 | tf_op jit(solution)/shard_map/ppermute | solution.py:103
  248.9 8.6 %collective-permute-done.53.refs_7_ = bf16[128,2048]{1,0:T(8,128)(2,1)} collective-permute-done((bf16[128,2048]{1,0:T(8,128)(2,1)S(1)}, bf16[128,2048]{1,0:T(8,128)(2,1)}, u32[]{:S(2)}, u32[]{:S(2)}) %collective-permute-start.53) | collective-permute-done | bytes 524320 | tf_op jit(solution)/shard_map/ppermute | solution.py:103
  265.6 8.2 %pick.2 = bf16[1536,2048]{1,0:T(8,128)(2,1)} custom-call(bf16[16,96,128]{2,1,0:T(8,128)(2,1)} %fusion.55.picks, f32[1536,1]{1,0:T(8,128)} %broadcast_in_dim.82.scale, bf16[128,2048]{1,0:T(8,128)(2,1)} %get-tuple-element.197.refs_0_, bf16[128,2048]{1,0:T(8,128)(2,1)} %collective-permute-done.42.refs_1_, bf16[128,2048]{1,0:T(8,128)(2,1)} %copy-done.75, ...), custom_call_target="tpu_custom_call" | custom-call | flops 805306368 | bytes 14680064 | tf_op jit(solution)/shard_map/pick/pallas_call | solution.py:264
  276.6 18.3 %fusion.13 = f32[1536,2048]{1,0:T(8,128)S(1)} fusion(bf16[1536,2048]{1,0:T(8,128)(2,1)} %pick.2, bf16[2048,1024]{1,0:T(8,128)(2,1)} %bitcast.253, bf16[2048,1024]{1,0:T(8,128)(2,1)} %bitcast.256), kind=kOutput, calls=%fused_computation.33 | convolution fusion | flops 12901679104 | bytes 27262976 | tf_op jit(solution)/shard_map/dot_general | solution.py:41
  301.2 8.3 %pick.3 = bf16[1536,2048]{1,0:T(8,128)(2,1)} custom-call(bf16[16,96,128]{2,1,0:T(8,128)(2,1)} %fusion.55.picks, f32[1536,1]{1,0:T(8,128)} %reshape.372.scale, bf16[128,2048]{1,0:T(8,128)(2,1)} %refs_0_.1, bf16[128,2048]{1,0:T(8,128)(2,1)} %collective-permute-done.refs_1_, bf16[128,2048]{1,0:T(8,128)(2,1)} %copy-done.74, ...), custom_call_target="tpu_custom_call" | custom-call | flops 805306368 | bytes 14680064 | tf_op jit(solution)/shard_map/pick/pallas_call | solution.py:264
  334.8 16.5 %multiply_convert_fusion.1 = (bf16[1536,1024]{1,0:T(8,128)(2,1)S(1)}, bf16[1536,1024]{1,0:T(8,128)(2,1)}) fusion(f32[1536,2048]{1,0:T(8,128)} %copy-done.62, bf16[1536,2048]{1,0:T(8,128)(2,1)} %pick.3, bf16[1,1024,2048]{2,1,0:T(8,128)(2,1)} %param.31), kind=kOutput, calls=%fused_computation.4 | convolution fusion | flops 6462898176 | bytes 29360128 | tf_op jit(solution)/shard_map/dot_general | solution.py:51
  364.8 9.3 %convolution_convert_fusion.1 = bf16[768,2048]{1,0:T(8,128)(2,1)S(1)} fusion(bf16[1536,2048]{1,0:T(8,128)(2,1)S(1)} %copy-done.55, bf16[2048,1024]{1,0:T(8,128)(2,1)} %bitcast.254, bf16[2048,1024]{1,0:T(8,128)(2,1)} %bitcast.257), kind=kOutput, calls=%fused_computation.17 | convolution fusion | flops 6460801024 | bytes 14680064 | tf_op jit(solution)/shard_map/dot_general | solution.py:51
  383.2 10.1 %convolution_convert_fusion = bf16[768,2048]{1,0:T(8,128)(2,1)} fusion(bf16[1536,2048]{1,0:T(8,128)(2,1)S(1)} %copy-done.55, bf16[2048,1024]{1,0:T(8,128)(2,1)S(1)} %bitcast.255, bf16[2048,1024]{1,0:T(8,128)(2,1)} %bitcast.258), kind=kOutput, calls=%fused_computation.16 | convolution fusion | flops 6460801024 | bytes 14680064 | tf_op jit(solution)/shard_map/dot_general | solution.py:51
  431.8 8.5 %collective-permute-done.74 = bf16[128,2048]{1,0:T(8,128)(2,1)S(1)} collective-permute-done((bf16[128,2048]{1,0:T(8,128)(2,1)S(1)}, bf16[128,2048]{1,0:T(8,128)(2,1)S(1)}, u32[]{:S(2)}, u32[]{:S(2)}) %collective-permute-start.74) | collective-permute-done | bytes 524320 | tf_op jit(solution)/shard_map/ppermute | solution.py:103
  492.2 7.4 %out_project_back.1 = bf16[16,128,128]{2,1,0:T(8,128)(2,1)} custom-call(s32[17]{0:T(128)} %concatenate.60.where, bf16[128,2048]{1,0:T(8,128)(2,1)} %fusion.82.branch, bf16[192,2048]{1,0:T(8,128)(2,1)} %copy-done.2, bf16[192,2048]{1,0:T(8,128)(2,1)} %copy-done.10, bf16[192,2048]{1,0:T(8,128)(2,1)} %copy-done.4, bf16[192,2048]{1,0:T(8,128)(2,1)} %copy-done.6, ...), custom_call_target="tpu_custom_call" | custom-call | flops 1073741824 | bytes 8388608 | tf_op jit(solution)/shard_map/out_project_back/pallas_call | solution.py:527
  520.6 21.9 %attend_back.1 = (f32[128,2048]{1,0:T(8,128)}, f32[128,2048]{1,0:T(8,128)}, bf16[128,2048]{1,0:T(8,128)(2,1)}, f32[1,2048]{1,0:T(1,128)}, f32[1,2048]{1,0:T(1,128)}, /*index=5*/f32[128,2]{1,0:T(8,128)}) custom-call(s32[2048,128]{1,0:T(8,128)} %broadcast_in_dim.45.key_seg, s32[1,2048]{1,0:T(1,128)} %bitcast.248, f32[1,2048]{1,0:T(1,128)} %get-tuple-element.247.log_total, ...), custom_call_target="tpu_custom_call" | custom-call | flops 5368709120 | bytes 10485760 | tf_op jit(solution)/shard_map/attend_back/pallas_call | solution.py:745
  581.4 10.6 %collective-permute-done.99.refs_5_ = bf16[256,2048]{1,0:T(8,128)(2,1)S(1)} collective-permute-done((bf16[256,2048]{1,0:T(8,128)(2,1)S(1)}, bf16[256,2048]{1,0:T(8,128)(2,1)S(1)}, u32[]{:S(2)}, u32[]{:S(2)}) %collective-permute-start.99) | collective-permute-done | bytes 1048608 | tf_op jit(solution)/shard_map/ppermute | solution.py:58
  623.1 8.5 %all-to-all-done.3 = bf16[16,384,128]{2,1,0:T(8,128)(2,1)} async-done(((bf16[16,384,128]{2,1,0:T(8,128)(2,1)}), bf16[16,384,128]{2,1,0:T(8,128)(2,1)}, u32[]{:S(2)}, u32[]{:S(2)}) %all-to-all-start.3) | async-done | bytes 1572896 | tf_op jit(solution)/shard_map/all_to_all | solution.py:860
  650.7 6.7 collective-permute-start.103
  673.0 7.3 collective-permute-done.86
  681.0 14.8 %collective-permute-done.118 = bf16[128,2048]{1,0:T(8,128)(2,1)S(1)} collective-permute-done((bf16[128,2048]{1,0:T(8,128)(2,1)S(1)}, bf16[128,2048]{1,0:T(8,128)(2,1)S(1)}, u32[]{:S(2)}, u32[]{:S(2)}) %collective-permute-start.118) | collective-permute-done | bytes 524320 | tf_op jit(solution)/shard_map/ppermute | solution.py:58
  (597 shorter events, 442.4 us)
Async XLA Ops:
  16.6 30.1 %collective-permute-start.9 = (bf16[192,2048]{1,0:T(8,128)(2,1)S(1)}, bf16[192,2048]{1,0:T(8,128)(2,1)S(1)}, u32[]{:S(2)}, u32[]{:S(2)}) collective-permute-start(bf16[192,2048]{1,0:T(8,128)(2,1)S(1)} %pad_maximum_fusion.9.refs_0_), channel_id=1, source_target_pairs={{0,1},{1,0},{2,3},{3,2},{4,5},{5,4},{6,7},{7,6},{8,9},{9,8},{10,11... | collective-permute-start | bytes 2359304 | tf_op jit(solution)/shard_map/ppermute | solution.py:103
  19.2 53.7 %all-to-all-start = ((bf16[16,80,384]{2,1,0:T(8,128)(2,1)}), bf16[16,80,384]{2,1,0:T(8,128)(2,1)}, u32[]{:S(2)}, u32[]{:S(2)}) async-start(bf16[16,80,384]{2,1,0:T(8,128)(2,1)} %copy.91), calls=%async_computation | async-start | bytes 1966080 | tf_op jit(solution)/shard_map/all_to_all | solution.py:860
  39.9 27.2 %collective-permute-start.8 = (bf16[192,2048]{1,0:T(8,128)(2,1)S(1)}, bf16[192,2048]{1,0:T(8,128)(2,1)}, u32[]{:S(2)}, u32[]{:S(2)}) collective-permute-start(bf16[192,2048]{1,0:T(8,128)(2,1)S(1)} %collective-permute-done.3.refs_1_), channel_id=1, source_target_pairs={{0,2},{1,3},{2,0},{3,1},{4,6},{5,7},{6,4},{7,5},{8,10},{9,11},{10,... | collective-permute-start | bytes 2359304 | tf_op jit(solution)/shard_map/ppermute | solution.py:103
  71.5 27.7 %collective-permute-start.16 = (bf16[192,2048]{1,0:T(8,128)(2,1)S(1)}, bf16[192,2048]{1,0:T(8,128)(2,1)}, u32[]{:S(2)}, u32[]{:S(2)}) collective-permute-start(bf16[192,2048]{1,0:T(8,128)(2,1)S(1)} %broadcast_select_fusion.1.refs_2_), channel_id=1, source_target_pairs={{0,1},{1,0},{2,3},{3,2},{4,5},{5,4},{6,7},{7,6},{8,9},{9,8},{10,11... | collective-permute-start | bytes 2359304 | tf_op jit(solution)/shard_map/ppermute | solution.py:103
  72.4 29.1 %collective-permute-start.18 = (bf16[192,2048]{1,0:T(8,128)(2,1)}, bf16[192,2048]{1,0:T(8,128)(2,1)}, u32[]{:S(2)}, u32[]{:S(2)}) collective-permute-start(bf16[192,2048]{1,0:T(8,128)(2,1)} %collective-permute-done.8.refs_5_), channel_id=1, source_target_pairs={{0,1},{1,0},{2,3},{3,2},{4,5},{5,4},{6,7},{7,6},{8,9},{9,8},{10,11... | collective-permute-start | bytes 2359304 | tf_op jit(solution)/shard_map/ppermute | solution.py:103
  101.5 34.4 %collective-permute-start = (bf16[128,2048]{1,0:T(8,128)(2,1)}, bf16[128,2048]{1,0:T(8,128)(2,1)}, u32[]{:S(2)}, u32[]{:S(2)}) collective-permute-start(bf16[128,2048]{1,0:T(8,128)(2,1)} %refs_0_.1), channel_id=1, source_target_pairs={{0,4},{1,5},{2,6},{3,7},{4,0},{5,1},{6,2},{7,3},{8,12},{9,13},{10,... | collective-permute-start | bytes 1572872 | tf_op jit(solution)/shard_map/ppermute | solution.py:103
  117.0 53.0 %collective-permute-start.31 = (bf16[512,2048]{1,0:T(8,128)(2,1)}, bf16[512,2048]{1,0:T(8,128)(2,1)}, u32[]{:S(2)}, u32[]{:S(2)}) collective-permute-start(bf16[512,2048]{1,0:T(8,128)(2,1)} %tails.1), channel_id=1, source_target_pairs={{0,16},{16,0},{1,17},{17,1},{2,18},{18,2},{3,19},{19,3},{4,20},{20... | collective-permute-start | bytes 6291464 | tf_op jit(solution)/shard_map/ppermute | solution.py:58
  320.8 39.5 %collective-permute-start.61 = (bf16[256,2048]{1,0:T(8,128)(2,1)S(1)}, bf16[256,2048]{1,0:T(8,128)(2,1)S(1)}, u32[]{:S(2)}, u32[]{:S(2)}) collective-permute-start(bf16[256,2048]{1,0:T(8,128)(2,1)S(1)} %convolution_convert_fusion.13.refs_0_), channel_id=1, source_target_pairs={{0,16},{16,0},{1,17},{17,1},{2,18},{18,2},{3,19},{19,3},{4,20},{20... | collective-permute-start | bytes 3145736 | tf_op jit(solution)/shard_map/ppermute | solution.py:58
  321.3 56.2 %collective-permute-start.64 = (bf16[256,2048]{1,0:T(8,128)(2,1)S(1)}, bf16[256,2048]{1,0:T(8,128)(2,1)S(1)}, u32[]{:S(2)}, u32[]{:S(2)}) collective-permute-start(bf16[256,2048]{1,0:T(8,128)(2,1)S(1)} %convolution_convert_fusion.12.refs_1_), channel_id=1, source_target_pairs={{0,16},{16,0},{1,17},{17,1},{2,18},{18,2},{3,19},{19,3},{4,20},{20... | collective-permute-start | bytes 3145736 | tf_op jit(solution)/shard_map/ppermute | solution.py:58
  377.9 36.8 %collective-permute-start.65 = (bf16[1024,2048]{1,0:T(8,128)(2,1)}, bf16[1024,2048]{1,0:T(8,128)(2,1)}, u32[]{:S(2)}, u32[]{:S(2)}) collective-permute-start(bf16[1024,2048]{1,0:T(8,128)(2,1)} %bitcast.40), channel_id=1, source_target_pairs={{0,1},{1,0},{2,3},{3,2},{4,5},{5,4},{6,7},{7,6},{8,9},{9,8},{10,11... | collective-permute-start | bytes 12582920 | tf_op jit(solution)/shard_map/ppermute | solution.py:103
  378.1 29.0 %collective-permute-start.68 = (bf16[256,2048]{1,0:T(8,128)(2,1)S(1)}, bf16[256,2048]{1,0:T(8,128)(2,1)S(1)}, u32[]{:S(2)}, u32[]{:S(2)}) collective-permute-start(bf16[256,2048]{1,0:T(8,128)(2,1)S(1)} %convolution_convert_fusion.11.refs_2_), channel_id=1, source_target_pairs={{0,16},{16,0},{1,17},{17,1},{2,18},{18,2},{3,19},{19,3},{4,20},{20... | collective-permute-start | bytes 3145736 | tf_op jit(solution)/shard_map/ppermute | solution.py:58
  378.6 49.2 %collective-permute-start.75 = (bf16[256,2048]{1,0:T(8,128)(2,1)S(1)}, bf16[256,2048]{1,0:T(8,128)(2,1)S(1)}, u32[]{:S(2)}, u32[]{:S(2)}) collective-permute-start(bf16[256,2048]{1,0:T(8,128)(2,1)S(1)} %convolution_convert_fusion.10.refs_3_), channel_id=1, source_target_pairs={{0,16},{16,0},{1,17},{17,1},{2,18},{18,2},{3,19},{19,3},{4,20},{20... | collective-permute-start | bytes 3145736 | tf_op jit(solution)/shard_map/ppermute | solution.py:58
  427.9 38.2 %collective-permute-start.80 = (bf16[256,2048]{1,0:T(8,128)(2,1)S(1)}, bf16[256,2048]{1,0:T(8,128)(2,1)S(1)}, u32[]{:S(2)}, u32[]{:S(2)}) collective-permute-start(bf16[256,2048]{1,0:T(8,128)(2,1)S(1)} %convolution_convert_fusion.9.refs_0_), channel_id=1, source_target_pairs={{0,16},{16,0},{1,17},{17,1},{2,18},{18,2},{3,19},{19,3},{4,20},{20... | collective-permute-start | bytes 3145736 | tf_op jit(solution)/shard_map/ppermute | solution.py:58
  431.3 52.7 %collective-permute-start.83 = (bf16[256,2048]{1,0:T(8,128)(2,1)S(1)}, bf16[256,2048]{1,0:T(8,128)(2,1)S(1)}, u32[]{:S(2)}, u32[]{:S(2)}) collective-permute-start(bf16[256,2048]{1,0:T(8,128)(2,1)S(1)} %convolution_convert_fusion.8.refs_1_), channel_id=1, source_target_pairs={{0,16},{16,0},{1,17},{17,1},{2,18},{18,2},{3,19},{19,3},{4,20},{20... | collective-permute-start | bytes 3145736 | tf_op jit(solution)/shard_map/ppermute | solution.py:58
  466.1 33.5 %collective-permute-start.84 = (bf16[256,2048]{1,0:T(8,128)(2,1)}, bf16[256,2048]{1,0:T(8,128)(2,1)}, u32[]{:S(2)}, u32[]{:S(2)}) collective-permute-start(bf16[256,2048]{1,0:T(8,128)(2,1)} %convolution_convert_fusion.7.refs_2_), channel_id=1, source_target_pairs={{0,16},{16,0},{1,17},{17,1},{2,18},{18,2},{3,19},{19,3},{4,20},{20... | collective-permute-start | bytes 3145736 | tf_op jit(solution)/shard_map/ppermute | solution.py:58
  485.0 34.9 %collective-permute-start.87 = (bf16[256,2048]{1,0:T(8,128)(2,1)}, bf16[256,2048]{1,0:T(8,128)(2,1)}, u32[]{:S(2)}, u32[]{:S(2)}) collective-permute-start(bf16[256,2048]{1,0:T(8,128)(2,1)} %convolution_convert_fusion.6.refs_3_), channel_id=1, source_target_pairs={{0,16},{16,0},{1,17},{17,1},{2,18},{18,2},{3,19},{19,3},{4,20},{20... | collective-permute-start | bytes 3145736 | tf_op jit(solution)/shard_map/ppermute | solution.py:58
  503.9 136.5 %all-gather.2.cloned.1.call-start = ((), (), s32[]{:S(2)}) async-start(), calls=%async_computation.4 | async-start | bytes 8912896 | tf_op jit(solution)/shard_map/all_gather | solution.py:1074
  594.6 37.1 %all-to-all-start.3 = ((bf16[16,384,128]{2,1,0:T(8,128)(2,1)}), bf16[16,384,128]{2,1,0:T(8,128)(2,1)}, u32[]{:S(2)}, u32[]{:S(2)}) async-start(bf16[16,384,128]{2,1,0:T(8,128)(2,1)} %bitcast_bitcast_fusion), calls=%async_computation.3 | async-start | bytes 3145728 | tf_op jit(solution)/shard_map/all_to_all | solution.py:860
  599.5 45.9 %collective-permute-start.101 = (bf16[256,2048]{1,0:T(8,128)(2,1)}, bf16[256,2048]{1,0:T(8,128)(2,1)}, u32[]{:S(2)}, u32[]{:S(2)}) collective-permute-start(bf16[256,2048]{1,0:T(8,128)(2,1)} %convolution_convert_fusion.3.refs_2_), channel_id=1, source_target_pairs={{0,16},{16,0},{1,17},{17,1},{2,18},{18,2},{3,19},{19,3},{4,20},{20... | collective-permute-start | bytes 3145736 | tf_op jit(solution)/shard_map/ppermute | solution.py:58
  599.8 60.5 %collective-permute-start.105 = (bf16[256,2048]{1,0:T(8,128)(2,1)}, bf16[256,2048]{1,0:T(8,128)(2,1)}, u32[]{:S(2)}, u32[]{:S(2)}) collective-permute-start(bf16[256,2048]{1,0:T(8,128)(2,1)} %convolution_convert_fusion.2.refs_3_), channel_id=1, source_target_pairs={{0,16},{16,0},{1,17},{17,1},{2,18},{18,2},{3,19},{19,3},{4,20},{20... | collective-permute-start | bytes 3145736 | tf_op jit(solution)/shard_map/ppermute | solution.py:58
  604.9 67.5 %collective-permute-start.62 = (bf16[128,2048]{1,0:T(8,128)(2,1)}, bf16[128,2048]{1,0:T(8,128)(2,1)}, u32[]{:S(2)}, u32[]{:S(2)}) collective-permute-start(bf16[128,2048]{1,0:T(8,128)(2,1)} %get-tuple-element.329), channel_id=1, source_target_pairs={{0,2},{1,3},{2,0},{3,1},{4,6},{5,7},{6,4},{7,5},{8,10},{9,11},{10,... | collective-permute-start | bytes 1572872 | tf_op jit(solution)/shard_map/ppermute | solution.py:103
  669.6 35.3 %collective-permute-start.108 = (bf16[128,2048]{1,0:T(8,128)(2,1)S(1)}, bf16[128,2048]{1,0:T(8,128)(2,1)S(1)}, u32[]{:S(2)}, u32[]{:S(2)}) collective-permute-start(bf16[128,2048]{1,0:T(8,128)(2,1)S(1)} %convolution_convert_fusion.14), channel_id=1, source_target_pairs={{0,16},{16,0},{1,17},{17,1},{2,18},{18,2},{3,19},{19,3},{4,20},{20... | collective-permute-start | bytes 1572872 | tf_op jit(solution)/shard_map/ppermute | solution.py:58
  672.4 34.1 %collective-permute-start.109 = (bf16[128,2048]{1,0:T(8,128)(2,1)S(1)}, bf16[128,2048]{1,0:T(8,128)(2,1)S(1)}, u32[]{:S(2)}, u32[]{:S(2)}) collective-permute-start(bf16[128,2048]{1,0:T(8,128)(2,1)S(1)} %bitcast.225), channel_id=1, source_target_pairs={{0,16},{16,0},{1,17},{17,1},{2,18},{18,2},{3,19},{19,3},{4,20},{20... | collective-permute-start | bytes 1572872 | tf_op jit(solution)/shard_map/ppermute | solution.py:58
  672.7 33.7 %collective-permute-start.96 = (bf16[128,2048]{1,0:T(8,128)(2,1)S(1)}, bf16[128,2048]{1,0:T(8,128)(2,1)S(1)}, u32[]{:S(2)}, u32[]{:S(2)}) collective-permute-start(bf16[128,2048]{1,0:T(8,128)(2,1)S(1)} %get-tuple-element.323), channel_id=1, source_target_pairs={{0,2},{1,3},{2,0},{3,1},{4,6},{5,7},{6,4},{7,5},{8,10},{9,11},{10,... | collective-permute-start | bytes 1572872 | tf_op jit(solution)/shard_map/ppermute | solution.py:103
  (210 other events, 3476.8 us)
Sparse Core Ops, SparseCore 0:
  520.0 78.0 all-gather.1

commit v7 on v5

--- a/solution.py
+++ b/solution.py
@@ -15,7 +15,8 @@
 rope_base = 50000.0
 negative = -1e30
 score_scale = HEAD_DIM ** (-0.5)
-query_block = 256
+def query_block_of(count):
+    return 512 if count <= 2048 else 256
 
 
 def norm_rows(values, norm_gain):
@@ -597,6 +598,7 @@
 
 def attend(query_raw, key_raw, value_t, inverse, gains, cosine, rope_sine, key_seg, query_seg):
     count = query_raw.shape[1]
+    query_block = query_block_of(count)
     whole = lambda i: (0, 0)
     across = lambda rows: pl.BlockSpec((rows, query_block), lambda i: (0, i))
     down = pl.BlockSpec((query_block, HEAD_DIM), lambda i: (i, 0))
@@ -736,6 +738,7 @@
     rope_sine,
 ):
     count = query.shape[0]
+    query_block = query_block_of(count)
     whole = lambda i: (0, 0)
     across = lambda rows: pl.BlockSpec((rows, query_block), lambda i: (0, i))
     down = pl.BlockSpec((query_block, HEAD_DIM), lambda i: (i, 0))

time: 736 us -> 732 us (level)
  transfers between devices with their start and end apart: 124 -> 124, of which waited for: 38 -> 39; matrix products, arithmetic and copies ran while one was open for 29% -> 29% of each run, Pallas kernels for 14% -> 14%
where the time goes in v7:
time: 732 us; the launch traced here: 723 us
  waiting for transfers between devices  195 us (27%)
  starting transfers between devices  167 us (23%)
  matrix products  120 us (16%)
  Pallas kernels  107 us (15%)
  other arithmetic  77.6 us (11%)
  local copies, waits for them, and re-layouts  40.1 us (5%)
  between operations  16.3 us (2%)
    ppermute x82, waiting for transfers between devices, send(): return lax.ppermute(values, 'expert', pairs)  148 us
    ppermute x82, starting transfers between devices, send(): return lax.ppermute(values, 'expert', pairs)  108 us
    ppermute x37, starting transfers between devices, swap(): return lax.ppermute(values, axis, [(i, i ^ step) for i in range(count)])  41 us
    dot_general x12, matrix products, contract_rows(): lax.dot_general(left, right, (((0,), (0,)), ((), ())), preferred_element_...  38.4 us
    ppermute x37, waiting for transfers between devices, swap(): return lax.ppermute(values, axis, [(i, i ^ step) for i in range(count)])  37.7 us
    dot_general x3, matrix products, contract_cols(): lax.dot_general(left, right, (((1,), (1,)), ((), ())), preferred_element_...  35.9 us
    dot_general x5, matrix products, mm(): return jnp.dot(left, right, preferred_element_type=jnp.float32)  32.6 us
    convert_element_type x18, other arithmetic, add_low(): (left.astype(jnp.float32) + right.astype(jnp.float32)).astype(jnp.bfloat16)  30.2 us
  transfers between devices with their start and end apart: 124, of which 39 were waited for; matrix products, arithmetic and copies ran while one was open for 29% of the time, Pallas kernels for 14%

profile of v7, /device:TPU:0, one launch (start us, length us, event | category | flops | bytes accessed | tf_op | source)
XLA Modules:
  0.0 722.8 jit_solution(14154452113632553589)
XLA Ops:
  25.1 6.7 collective-permute-done.3.refs_1_
  31.8 6.5 collective-permute-done.5.refs_4_
  47.2 19.9 %collective-permute-done.7 = bf16[192,2048]{1,0:T(8,128)(2,1)S(1)} collective-permute-done((bf16[192,2048]{1,0:T(8,128)(2,1)}, bf16[192,2048]{1,0:T(8,128)(2,1)S(1)}, u32[]{:S(2)}, u32[]{:S(2)}) %collective-permute-start.7) | collective-permute-done | bytes 786464 | tf_op jit(solution)/shard_map/ppermute | solution.py:104
  72.9 20.5 %collective-permute-done.10 = bf16[192,2048]{1,0:T(8,128)(2,1)} collective-permute-done((bf16[192,2048]{1,0:T(8,128)(2,1)}, bf16[192,2048]{1,0:T(8,128)(2,1)}, u32[]{:S(2)}, u32[]{:S(2)}) %collective-permute-start.10) | collective-permute-done | bytes 786464 | tf_op jit(solution)/shard_map/ppermute | solution.py:104
  105.3 7.3 %collective-permute-done.15.refs_7_ = bf16[192,2048]{1,0:T(8,128)(2,1)} collective-permute-done((bf16[192,2048]{1,0:T(8,128)(2,1)S(1)}, bf16[192,2048]{1,0:T(8,128)(2,1)}, u32[]{:S(2)}, u32[]{:S(2)}) %collective-permute-start.15) | collective-permute-done | bytes 786464 | tf_op jit(solution)/shard_map/ppermute | solution.py:104
  124.6 11.3 %heads_in.1 = (f32[128,2048]{1,0:T(8,128)}, f32[128,2048]{1,0:T(8,128)}, bf16[2048,128]{1,0:T(8,128)(2,1)}, bf16[128,2048]{1,0:T(8,128)(2,1)}, f32[2,2048]{1,0:T(2,128)}) custom-call(s32[16]{0:T(128)} %pad_add_fusion.order, bf16[2048,384]{1,0:T(8,128)(2,1)} %bitcast.218, bf16[192,2048]{1,0:T(8,128)(2,1)} %copy-done.2, bf16[192,2048]{1,0:T(8,128)(2,1)} %copy-done.10, ...), custom_call_target="tpu_custom_call" | custom-call | flops 3221225472 | bytes 8388608 | tf_op jit(solution)/shard_map/heads_in/pallas_call | solution.py:405
  155.3 12.3 %attend.1 = (bf16[128,2048]{1,0:T(8,128)(2,1)}, bf16[2048,128]{1,0:T(8,128)(2,1)}, bf16[128,2048]{1,0:T(8,128)(2,1)}, bf16[2048,128]{1,0:T(8,128)(2,1)}, bf16[20...) custom-call(f32[128,2048]{1,0:T(8,128)} %get-tuple-element.183.query_raw, ...), custom_call_target="tpu_custom_call" | custom-call | flops 2147483648 | bytes 6291456 | tf_op jit(solution)/shard_map/attend/pallas_call | solution.py:607
  179.3 9.0 %all-to-all-done.1.attended = bf16[16,128,128]{2,1,0:T(8,128)(2,1)S(1)} async-done(((bf16[16,128,128]{2,1,0:T(8,128)(2,1)}), bf16[16,128,128]{2,1,0:T(8,128)(2,1)S(1)}, u32[]{:S(2)}, u32[]{:S(2)}) %all-to-all-start.1) | async-done | bytes 524320 | tf_op jit(solution)/shard_map/all_to_all | solution.py:863
  189.8 6.5 out_project.1
  217.2 12.7 %collective-permute-done.46 = bf16[128,2048]{1,0:T(8,128)(2,1)S(1)} collective-permute-done((bf16[128,2048]{1,0:T(8,128)(2,1)}, bf16[128,2048]{1,0:T(8,128)(2,1)S(1)}, u32[]{:S(2)}, u32[]{:S(2)}) %collective-permute-start.46) | collective-permute-done | bytes 524320 | tf_op jit(solution)/shard_map/ppermute | solution.py:104
  234.5 9.5 %collective-permute-done.49 = bf16[128,2048]{1,0:T(8,128)(2,1)S(1)} collective-permute-done((bf16[128,2048]{1,0:T(8,128)(2,1)S(1)}, bf16[128,2048]{1,0:T(8,128)(2,1)S(1)}, u32[]{:S(2)}, u32[]{:S(2)}) %collective-permute-start.49) | collective-permute-done | bytes 524320 | tf_op jit(solution)/shard_map/ppermute | solution.py:104
  246.4 8.6 %collective-permute-done.53.refs_7_ = bf16[128,2048]{1,0:T(8,128)(2,1)} collective-permute-done((bf16[128,2048]{1,0:T(8,128)(2,1)S(1)}, bf16[128,2048]{1,0:T(8,128)(2,1)}, u32[]{:S(2)}, u32[]{:S(2)}) %collective-permute-start.53) | collective-permute-done | bytes 524320 | tf_op jit(solution)/shard_map/ppermute | solution.py:104
  263.1 8.2 %pick.2 = bf16[1536,2048]{1,0:T(8,128)(2,1)} custom-call(bf16[16,96,128]{2,1,0:T(8,128)(2,1)} %fusion.55.picks, f32[1536,1]{1,0:T(8,128)} %broadcast_in_dim.82.scale, bf16[128,2048]{1,0:T(8,128)(2,1)} %get-tuple-element.198.refs_0_, bf16[128,2048]{1,0:T(8,128)(2,1)} %collective-permute-done.42.refs_1_, bf16[128,2048]{1,0:T(8,128)(2,1)} %copy-done.72, ...), custom_call_target="tpu_custom_call" | custom-call | flops 805306368 | bytes 14680064 | tf_op jit(solution)/shard_map/pick/pallas_call | solution.py:265
  274.1 18.3 %fusion.13 = f32[1536,2048]{1,0:T(8,128)S(1)} fusion(bf16[1536,2048]{1,0:T(8,128)(2,1)} %pick.2, bf16[2048,1024]{1,0:T(8,128)(2,1)} %bitcast.253, bf16[2048,1024]{1,0:T(8,128)(2,1)} %bitcast.256), kind=kOutput, calls=%fused_computation.33 | convolution fusion | flops 12901679104 | bytes 27262976 | tf_op jit(solution)/shard_map/dot_general | solution.py:42
  298.6 8.3 %pick.3 = bf16[1536,2048]{1,0:T(8,128)(2,1)} custom-call(bf16[16,96,128]{2,1,0:T(8,128)(2,1)} %fusion.55.picks, f32[1536,1]{1,0:T(8,128)} %reshape.372.scale, bf16[128,2048]{1,0:T(8,128)(2,1)} %refs_0_.1, bf16[128,2048]{1,0:T(8,128)(2,1)} %collective-permute-done.refs_1_, bf16[128,2048]{1,0:T(8,128)(2,1)} %copy-done.71, ...), custom_call_target="tpu_custom_call" | custom-call | flops 805306368 | bytes 14680064 | tf_op jit(solution)/shard_map/pick/pallas_call | solution.py:265
  332.2 16.5 %multiply_convert_fusion.1 = (bf16[1536,1024]{1,0:T(8,128)(2,1)S(1)}, bf16[1536,1024]{1,0:T(8,128)(2,1)}) fusion(f32[1536,2048]{1,0:T(8,128)} %copy-done.60, bf16[1536,2048]{1,0:T(8,128)(2,1)} %pick.3, bf16[1,1024,2048]{2,1,0:T(8,128)(2,1)} %param.31), kind=kOutput, calls=%fused_computation.4 | convolution fusion | flops 6462898176 | bytes 29360128 | tf_op jit(solution)/shard_map/dot_general | solution.py:52
  362.1 9.3 %convolution_convert_fusion.1 = bf16[768,2048]{1,0:T(8,128)(2,1)S(1)} fusion(bf16[1536,2048]{1,0:T(8,128)(2,1)S(1)} %copy-done.53, bf16[2048,1024]{1,0:T(8,128)(2,1)} %bitcast.254, bf16[2048,1024]{1,0:T(8,128)(2,1)} %bitcast.257), kind=kOutput, calls=%fused_computation.17 | convolution fusion | flops 6460801024 | bytes 14680064 | tf_op jit(solution)/shard_map/dot_general | solution.py:52
  380.5 10.1 %convolution_convert_fusion = bf16[768,2048]{1,0:T(8,128)(2,1)} fusion(bf16[1536,2048]{1,0:T(8,128)(2,1)S(1)} %copy-done.53, bf16[2048,1024]{1,0:T(8,128)(2,1)S(1)} %bitcast.255, bf16[2048,1024]{1,0:T(8,128)(2,1)} %bitcast.258), kind=kOutput, calls=%fused_computation.16 | convolution fusion | flops 6460801024 | bytes 14680064 | tf_op jit(solution)/shard_map/dot_general | solution.py:52
  429.7 7.9 %collective-permute-done.74 = bf16[128,2048]{1,0:T(8,128)(2,1)S(1)} collective-permute-done((bf16[128,2048]{1,0:T(8,128)(2,1)S(1)}, bf16[128,2048]{1,0:T(8,128)(2,1)S(1)}, u32[]{:S(2)}, u32[]{:S(2)}) %collective-permute-start.74) | collective-permute-done | bytes 524320 | tf_op jit(solution)/shard_map/ppermute | solution.py:104
  489.5 7.4 %out_project_back.1 = bf16[16,128,128]{2,1,0:T(8,128)(2,1)} custom-call(s32[17]{0:T(128)} %concatenate.60.where, bf16[128,2048]{1,0:T(8,128)(2,1)} %fusion.82.branch, bf16[192,2048]{1,0:T(8,128)(2,1)} %copy-done.2, bf16[192,2048]{1,0:T(8,128)(2,1)} %copy-done.10, bf16[192,2048]{1,0:T(8,128)(2,1)} %copy-done.4, bf16[192,2048]{1,0:T(8,128)(2,1)} %copy-done.6, ...), custom_call_target="tpu_custom_call" | custom-call | flops 1073741824 | bytes 8388608 | tf_op jit(solution)/shard_map/out_project_back/pallas_call | solution.py:528
  518.3 19.6 %attend_back.1 = (f32[128,2048]{1,0:T(8,128)}, f32[128,2048]{1,0:T(8,128)}, bf16[128,2048]{1,0:T(8,128)(2,1)}, f32[1,2048]{1,0:T(1,128)}, f32[1,2048]{1,0:T(1,128)}, /*index=5*/f32[128,2]{1,0:T(8,128)}) custom-call(s32[2048,128]{1,0:T(8,128)} %broadcast_in_dim.45.key_seg, s32[1,2048]{1,0:T(1,128)} %bitcast.248, f32[1,2048]{1,0:T(1,128)} %get-tuple-element.248.log_total, ...), custom_call_target="tpu_custom_call" | custom-call | flops 5368709120 | bytes 10485760 | tf_op jit(solution)/shard_map/attend_back/pallas_call | solution.py:748
  579.3 10.3 %collective-permute-done.99.refs_5_ = bf16[256,2048]{1,0:T(8,128)(2,1)S(1)} collective-permute-done((bf16[256,2048]{1,0:T(8,128)(2,1)S(1)}, bf16[256,2048]{1,0:T(8,128)(2,1)S(1)}, u32[]{:S(2)}, u32[]{:S(2)}) %collective-permute-start.99) | collective-permute-done | bytes 1048608 | tf_op jit(solution)/shard_map/ppermute | solution.py:59
  626.1 13.2 %collective-permute-done.97 = bf16[128,2048]{1,0:T(8,128)(2,1)} collective-permute-done((bf16[128,2048]{1,0:T(8,128)(2,1)}, bf16[128,2048]{1,0:T(8,128)(2,1)}, u32[]{:S(2)}, u32[]{:S(2)}) %collective-permute-start.97) | collective-permute-done | bytes 524320 | tf_op jit(solution)/shard_map/ppermute | solution.py:104
  669.0 7.9 %collective-permute-start.107 = (bf16[128,2048]{1,0:T(8,128)(2,1)S(1)}, bf16[128,2048]{1,0:T(8,128)(2,1)S(1)}, u32[]{:S(2)}, u32[]{:S(2)}) collective-permute-start(bf16[128,2048]{1,0:T(8,128)(2,1)S(1)} %get-tuple-element.324), channel_id=1, source_target_pairs={{0,4},{1,5},{2,6},{3,7},{4,0},{5,1},{6,2},{7,3},{8,12},{9,13},{10,... | collective-permute-start | bytes 1572872 | tf_op jit(solution)/shard_map/ppermute | solution.py:104
  (589 shorter events, 438.8 us)
Async XLA Ops:
  16.5 30.2 %collective-permute-start.9 = (bf16[192,2048]{1,0:T(8,128)(2,1)S(1)}, bf16[192,2048]{1,0:T(8,128)(2,1)S(1)}, u32[]{:S(2)}, u32[]{:S(2)}) collective-permute-start(bf16[192,2048]{1,0:T(8,128)(2,1)S(1)} %pad_maximum_fusion.9.refs_0_), channel_id=1, source_target_pairs={{0,1},{1,0},{2,3},{3,2},{4,5},{5,4},{6,7},{7,6},{8,9},{9,8},{10,11... | collective-permute-start | bytes 2359304 | tf_op jit(solution)/shard_map/ppermute | solution.py:104
  19.2 53.7 %all-to-all-start = ((bf16[16,80,384]{2,1,0:T(8,128)(2,1)}), bf16[16,80,384]{2,1,0:T(8,128)(2,1)}, u32[]{:S(2)}, u32[]{:S(2)}) async-start(bf16[16,80,384]{2,1,0:T(8,128)(2,1)} %copy.91), calls=%async_computation | async-start | bytes 1966080 | tf_op jit(solution)/shard_map/all_to_all | solution.py:863
  39.9 27.2 %collective-permute-start.8 = (bf16[192,2048]{1,0:T(8,128)(2,1)S(1)}, bf16[192,2048]{1,0:T(8,128)(2,1)}, u32[]{:S(2)}, u32[]{:S(2)}) collective-permute-start(bf16[192,2048]{1,0:T(8,128)(2,1)S(1)} %collective-permute-done.3.refs_1_), channel_id=1, source_target_pairs={{0,2},{1,3},{2,0},{3,1},{4,6},{5,7},{6,4},{7,5},{8,10},{9,11},{10,... | collective-permute-start | bytes 2359304 | tf_op jit(solution)/shard_map/ppermute | solution.py:104
  46.7 26.2 %collective-permute-start.13 = (bf16[192,2048]{1,0:T(8,128)(2,1)S(1)}, bf16[192,2048]{1,0:T(8,128)(2,1)}, u32[]{:S(2)}, u32[]{:S(2)}) collective-permute-start(bf16[192,2048]{1,0:T(8,128)(2,1)S(1)} %collective-permute-done.5.refs_4_), channel_id=1, source_target_pairs={{0,1},{1,0},{2,3},{3,2},{4,5},{5,4},{6,7},{7,6},{8,9},{9,8},{10,11... | collective-permute-start | bytes 2359304 | tf_op jit(solution)/shard_map/ppermute | solution.py:104
  71.5 27.7 %collective-permute-start.16 = (bf16[192,2048]{1,0:T(8,128)(2,1)S(1)}, bf16[192,2048]{1,0:T(8,128)(2,1)}, u32[]{:S(2)}, u32[]{:S(2)}) collective-permute-start(bf16[192,2048]{1,0:T(8,128)(2,1)S(1)} %broadcast_select_fusion.1.refs_2_), channel_id=1, source_target_pairs={{0,1},{1,0},{2,3},{3,2},{4,5},{5,4},{6,7},{7,6},{8,9},{9,8},{10,11... | collective-permute-start | bytes 2359304 | tf_op jit(solution)/shard_map/ppermute | solution.py:104
  72.4 29.1 %collective-permute-start.18 = (bf16[192,2048]{1,0:T(8,128)(2,1)}, bf16[192,2048]{1,0:T(8,128)(2,1)}, u32[]{:S(2)}, u32[]{:S(2)}) collective-permute-start(bf16[192,2048]{1,0:T(8,128)(2,1)} %collective-permute-done.8.refs_5_), channel_id=1, source_target_pairs={{0,1},{1,0},{2,3},{3,2},{4,5},{5,4},{6,7},{7,6},{8,9},{9,8},{10,11... | collective-permute-start | bytes 2359304 | tf_op jit(solution)/shard_map/ppermute | solution.py:104
  101.5 34.4 %collective-permute-start = (bf16[128,2048]{1,0:T(8,128)(2,1)}, bf16[128,2048]{1,0:T(8,128)(2,1)}, u32[]{:S(2)}, u32[]{:S(2)}) collective-permute-start(bf16[128,2048]{1,0:T(8,128)(2,1)} %refs_0_.1), channel_id=1, source_target_pairs={{0,4},{1,5},{2,6},{3,7},{4,0},{5,1},{6,2},{7,3},{8,12},{9,13},{10,... | collective-permute-start | bytes 1572872 | tf_op jit(solution)/shard_map/ppermute | solution.py:104
  117.0 51.8 %collective-permute-start.31 = (bf16[512,2048]{1,0:T(8,128)(2,1)}, bf16[512,2048]{1,0:T(8,128)(2,1)}, u32[]{:S(2)}, u32[]{:S(2)}) collective-permute-start(bf16[512,2048]{1,0:T(8,128)(2,1)} %tails.1), channel_id=1, source_target_pairs={{0,16},{16,0},{1,17},{17,1},{2,18},{18,2},{3,19},{19,3},{4,20},{20... | collective-permute-start | bytes 6291464 | tf_op jit(solution)/shard_map/ppermute | solution.py:59
  318.2 39.5 %collective-permute-start.61 = (bf16[256,2048]{1,0:T(8,128)(2,1)S(1)}, bf16[256,2048]{1,0:T(8,128)(2,1)S(1)}, u32[]{:S(2)}, u32[]{:S(2)}) collective-permute-start(bf16[256,2048]{1,0:T(8,128)(2,1)S(1)} %convolution_convert_fusion.13.refs_0_), channel_id=1, source_target_pairs={{0,16},{16,0},{1,17},{17,1},{2,18},{18,2},{3,19},{19,3},{4,20},{20... | collective-permute-start | bytes 3145736 | tf_op jit(solution)/shard_map/ppermute | solution.py:59
  319.3 55.6 %collective-permute-start.64 = (bf16[256,2048]{1,0:T(8,128)(2,1)S(1)}, bf16[256,2048]{1,0:T(8,128)(2,1)S(1)}, u32[]{:S(2)}, u32[]{:S(2)}) collective-permute-start(bf16[256,2048]{1,0:T(8,128)(2,1)S(1)} %convolution_convert_fusion.12.refs_1_), channel_id=1, source_target_pairs={{0,16},{16,0},{1,17},{17,1},{2,18},{18,2},{3,19},{19,3},{4,20},{20... | collective-permute-start | bytes 3145736 | tf_op jit(solution)/shard_map/ppermute | solution.py:59
  375.3 36.8 %collective-permute-start.65 = (bf16[1024,2048]{1,0:T(8,128)(2,1)}, bf16[1024,2048]{1,0:T(8,128)(2,1)}, u32[]{:S(2)}, u32[]{:S(2)}) collective-permute-start(bf16[1024,2048]{1,0:T(8,128)(2,1)} %bitcast.40), channel_id=1, source_target_pairs={{0,1},{1,0},{2,3},{3,2},{4,5},{5,4},{6,7},{7,6},{8,9},{9,8},{10,11... | collective-permute-start | bytes 12582920 | tf_op jit(solution)/shard_map/ppermute | solution.py:104
  375.4 29.0 %collective-permute-start.68 = (bf16[256,2048]{1,0:T(8,128)(2,1)S(1)}, bf16[256,2048]{1,0:T(8,128)(2,1)S(1)}, u32[]{:S(2)}, u32[]{:S(2)}) collective-permute-start(bf16[256,2048]{1,0:T(8,128)(2,1)S(1)} %convolution_convert_fusion.11.refs_2_), channel_id=1, source_target_pairs={{0,16},{16,0},{1,17},{17,1},{2,18},{18,2},{3,19},{19,3},{4,20},{20... | collective-permute-start | bytes 3145736 | tf_op jit(solution)/shard_map/ppermute | solution.py:59
  376.6 48.6 %collective-permute-start.75 = (bf16[256,2048]{1,0:T(8,128)(2,1)S(1)}, bf16[256,2048]{1,0:T(8,128)(2,1)S(1)}, u32[]{:S(2)}, u32[]{:S(2)}) collective-permute-start(bf16[256,2048]{1,0:T(8,128)(2,1)S(1)} %convolution_convert_fusion.10.refs_3_), channel_id=1, source_target_pairs={{0,16},{16,0},{1,17},{17,1},{2,18},{18,2},{3,19},{19,3},{4,20},{20... | collective-permute-start | bytes 3145736 | tf_op jit(solution)/shard_map/ppermute | solution.py:59
  425.1 38.3 %collective-permute-start.80 = (bf16[256,2048]{1,0:T(8,128)(2,1)S(1)}, bf16[256,2048]{1,0:T(8,128)(2,1)S(1)}, u32[]{:S(2)}, u32[]{:S(2)}) collective-permute-start(bf16[256,2048]{1,0:T(8,128)(2,1)S(1)} %convolution_convert_fusion.9.refs_0_), channel_id=1, source_target_pairs={{0,16},{16,0},{1,17},{17,1},{2,18},{18,2},{3,19},{19,3},{4,20},{20... | collective-permute-start | bytes 3145736 | tf_op jit(solution)/shard_map/ppermute | solution.py:59
  428.6 52.7 %collective-permute-start.83 = (bf16[256,2048]{1,0:T(8,128)(2,1)S(1)}, bf16[256,2048]{1,0:T(8,128)(2,1)S(1)}, u32[]{:S(2)}, u32[]{:S(2)}) collective-permute-start(bf16[256,2048]{1,0:T(8,128)(2,1)S(1)} %convolution_convert_fusion.8.refs_1_), channel_id=1, source_target_pairs={{0,16},{16,0},{1,17},{17,1},{2,18},{18,2},{3,19},{19,3},{4,20},{20... | collective-permute-start | bytes 3145736 | tf_op jit(solution)/shard_map/ppermute | solution.py:59
  463.4 33.5 %collective-permute-start.84 = (bf16[256,2048]{1,0:T(8,128)(2,1)}, bf16[256,2048]{1,0:T(8,128)(2,1)}, u32[]{:S(2)}, u32[]{:S(2)}) collective-permute-start(bf16[256,2048]{1,0:T(8,128)(2,1)} %convolution_convert_fusion.7.refs_2_), channel_id=1, source_target_pairs={{0,16},{16,0},{1,17},{17,1},{2,18},{18,2},{3,19},{19,3},{4,20},{20... | collective-permute-start | bytes 3145736 | tf_op jit(solution)/shard_map/ppermute | solution.py:59
  482.4 34.8 %collective-permute-start.87 = (bf16[256,2048]{1,0:T(8,128)(2,1)}, bf16[256,2048]{1,0:T(8,128)(2,1)}, u32[]{:S(2)}, u32[]{:S(2)}) collective-permute-start(bf16[256,2048]{1,0:T(8,128)(2,1)} %convolution_convert_fusion.6.refs_3_), channel_id=1, source_target_pairs={{0,16},{16,0},{1,17},{17,1},{2,18},{18,2},{3,19},{19,3},{4,20},{20... | collective-permute-start | bytes 3145736 | tf_op jit(solution)/shard_map/ppermute | solution.py:59
  501.2 119.2 %all-gather.2.cloned.1.call-start = ((), (), s32[]{:S(2)}) async-start(), calls=%async_computation.4 | async-start | bytes 8912896 | tf_op jit(solution)/shard_map/all_gather | solution.py:1077
  517.2 25.7 %collective-permute-start.88 = (bf16[256,2048]{1,0:T(8,128)(2,1)S(1)}, bf16[256,2048]{1,0:T(8,128)(2,1)}, u32[]{:S(2)}, u32[]{:S(2)}) collective-permute-start(bf16[256,2048]{1,0:T(8,128)(2,1)S(1)} %convolution_convert_fusion.5.refs_0_), channel_id=1, source_target_pairs={{0,16},{16,0},{1,17},{17,1},{2,18},{18,2},{3,19},{19,3},{4,20},{20... | collective-permute-start | bytes 3145736 | tf_op jit(solution)/shard_map/ppermute | solution.py:59
  592.1 47.1 %all-to-all-start.3 = ((bf16[16,384,128]{2,1,0:T(8,128)(2,1)}), bf16[16,384,128]{2,1,0:T(8,128)(2,1)}, u32[]{:S(2)}, u32[]{:S(2)}) async-start(bf16[16,384,128]{2,1,0:T(8,128)(2,1)} %bitcast_bitcast_fusion), calls=%async_computation.3 | async-start | bytes 3145728 | tf_op jit(solution)/shard_map/all_to_all | solution.py:863
  596.9 29.2 %collective-permute-start.101 = (bf16[256,2048]{1,0:T(8,128)(2,1)}, bf16[256,2048]{1,0:T(8,128)(2,1)}, u32[]{:S(2)}, u32[]{:S(2)}) collective-permute-start(bf16[256,2048]{1,0:T(8,128)(2,1)} %convolution_convert_fusion.3.refs_2_), channel_id=1, source_target_pairs={{0,16},{16,0},{1,17},{17,1},{2,18},{18,2},{3,19},{19,3},{4,20},{20... | collective-permute-start | bytes 3145736 | tf_op jit(solution)/shard_map/ppermute | solution.py:59
  597.6 61.7 %collective-permute-start.105 = (bf16[256,2048]{1,0:T(8,128)(2,1)}, bf16[256,2048]{1,0:T(8,128)(2,1)}, u32[]{:S(2)}, u32[]{:S(2)}) collective-permute-start(bf16[256,2048]{1,0:T(8,128)(2,1)} %convolution_convert_fusion.2.refs_3_), channel_id=1, source_target_pairs={{0,16},{16,0},{1,17},{17,1},{2,18},{18,2},{3,19},{19,3},{4,20},{20... | collective-permute-start | bytes 3145736 | tf_op jit(solution)/shard_map/ppermute | solution.py:59
  602.3 66.0 %collective-permute-start.62 = (bf16[128,2048]{1,0:T(8,128)(2,1)}, bf16[128,2048]{1,0:T(8,128)(2,1)}, u32[]{:S(2)}, u32[]{:S(2)}) collective-permute-start(bf16[128,2048]{1,0:T(8,128)(2,1)} %get-tuple-element.331), channel_id=1, source_target_pairs={{0,2},{1,3},{2,0},{3,1},{4,6},{5,7},{6,4},{7,5},{8,10},{9,11},{10,... | collective-permute-start | bytes 1572872 | tf_op jit(solution)/shard_map/ppermute | solution.py:104
  683.2 27.6 %collective-permute-start.116 = (bf16[128,2048]{1,0:T(8,128)(2,1)S(1)}, bf16[128,2048]{1,0:T(8,128)(2,1)S(1)}, u32[]{:S(2)}, u32[]{:S(2)}) collective-permute-start(bf16[128,2048]{1,0:T(8,128)(2,1)S(1)} %bitcast.223), channel_id=1, source_target_pairs={{0,16},{16,0},{1,17},{17,1},{2,18},{18,2},{3,19},{19,3},{4,20},{20... | collective-permute-start | bytes 1572872 | tf_op jit(solution)/shard_map/ppermute | solution.py:59
  (206 other events, 3402.3 us)
Sparse Core Ops, SparseCore 0:
  517.3 77.4 all-gather.1
